TPU v7x, 256 devices: a whole 4x4x8 slice. The times are simulated.
256 devices in a mesh: clip: 16 (over y_lo, z), chan: 16 (over x, y_hi, core).
Axes of the slice: x: 4, y: 4 (y_hi: 2, y_lo: 2; y = y_hi * 2 + y_lo), z: 8, core: 2. Of those that a mesh axis runs over, the one named last changes fastest.
Arguments:
- block_in: bfloat16 [16, 512, 4, 4, 128], P('clip', 'chan'), may hold values from -6 to 6
- conv_one: bfloat16 [512, 27, 512], P('chan'), may hold values from -0.0546875 to 0.0546875
- conv_two: bfloat16 [512, 27, 512], P('chan'), may hold values from -0.0546875 to 0.0546875
- out_cotangent: bfloat16 [16, 512, 4, 4, 128], P('clip', 'chan'), may hold values from -6 to 6
Outputs:
- block_out: float32 [16, 512, 4, 4, 128], P('clip', 'chan')
- block_in_grad: float32 [16, 512, 4, 4, 128], P('clip', 'chan')
- conv_one_grad: float32 [512, 27, 512], P('chan')
- conv_two_grad: float32 [512, 27, 512], P('chan')
All inputs are finite; a program needn't handle non-finite values.
Results may differ from a plain program's by a relative error of at most 0.0046.
Values may be sent and summed in bfloat16 or wider, within the bound.
No kernel may reach another device: no remote copies, remote signals or barrier semaphores. Data moves between devices by JAX's collectives and lax.ppermute only.
A program may use at most 64 MiB of HBM per device.

v0:
```python
import functools

import jax
import jax.numpy as jnp
from jax import lax
from jax.experimental import pallas as pl
from jax.experimental.pallas import tpu as pltpu
from jax.sharding import Mesh, PartitionSpec as P


XY = ("x", "yh")
SWAP = [(0, 1), (1, 0)]
F32 = jnp.float32
BF16 = jnp.bfloat16
TAPS = [(i, j, k) for i in range(3) for j in range(3) for k in range(3)]
COUNT = 16 * 16 * 128
FIELD = (16, 32, 128)
SMEM_SPEC = pl.BlockSpec(memory_space=pltpu.SMEM)
VMEM_SPEC = pl.BlockSpec(memory_space=pltpu.VMEM)


def call(body, outs, scratch, limit, flops, *args):
    return pl.pallas_call(
        body,
        out_shape=tuple(jax.ShapeDtypeStruct(*o) for o in outs),
        in_specs=[SMEM_SPEC if a.dtype == jnp.int32 else VMEM_SPEC for a in args],
        out_specs=(VMEM_SPEC,) * len(outs),
        scratch_shapes=[pltpu.VMEM(*s) for s in scratch],
        compiler_params=pltpu.CompilerParams(vmem_limit_bytes=limit << 20),
        cost_estimate=pl.CostEstimate(flops=flops, bytes_accessed=4 << 20, transcendentals=0),
    )(*args)


def per_group(total):
    row = lax.broadcasted_iota(jnp.int32, (32, 128), 0)
    return jnp.where(row < 16, jnp.sum(total[:16]), jnp.sum(total[16:]))


def moments(load):
    total = load(0)
    for cell in range(1, 16):
        total = total + load(cell)
    center = per_group(total) * (1.0 / COUNT)
    total = jnp.zeros((32, 128), F32)
    for cell in range(16):
        gap = load(cell) - center
        total = total + gap * gap
    return center, lax.rsqrt(per_group(total) * (1.0 / COUNT) + 1e-06)


def act_body(field_ref, out_ref):
    center, scale = moments(lambda cell: field_ref[cell].astype(F32))
    for cell in range(16):
        normed = (field_ref[cell].astype(F32) - center) * scale
        value = (normed * jax.nn.sigmoid(normed)).astype(BF16)
        for copy in range(8):
            out_ref[copy, cell] = value


def pull_body(count, final, *refs):
    field_ref, pieces = refs[0], refs[1 : 1 + count]
    extra_ref = refs[1 + count] if final else None
    out_ref, normed_ref, down_ref = refs[-3:]
    center, scale = moments(lambda cell: field_ref[cell].astype(F32))
    first = jnp.zeros((32, 128), F32)
    second = jnp.zeros((32, 128), F32)
    for cell in range(16):
        normed = (field_ref[cell].astype(F32) - center) * scale
        grad = None
        for n in range(8):
            piece = (pieces[0][n, cell] if count == 1 else pieces[n][cell]).astype(F32)
            grad = piece if grad is None else grad + piece
        gate = jax.nn.sigmoid(normed)
        down = grad * (gate * (1.0 + normed * (1.0 - gate)))
        normed_ref[cell] = normed
        down_ref[cell] = down
        first = first + down
        second = second + down * normed
    first = per_group(first) * (1.0 / COUNT)
    second = per_group(second) * (1.0 / COUNT)
    for cell in range(16):
        value = scale * (down_ref[cell] - first - normed_ref[cell] * second)
        if final:
            out_ref[cell] = extra_ref[cell].astype(F32) + value
        else:
            out_ref[cell] = value.astype(BF16)


def assemble(core_ref, own_ref, other_ref, acts):
    core = core_ref[0]

    def step(n, carry):
        low = pl.multiple_of(n * 64 + core * 32, 32)
        high = pl.multiple_of(n * 64 + 32 - core * 32, 32)
        for cell in range(16):
            columns = slice(cell % 2 * 128, cell % 2 * 128 + 128)
            acts[cell // 2, pl.ds(low, 32), columns] = own_ref[n, cell]
            acts[cell // 2, pl.ds(high, 32), columns] = other_ref[n, cell]
        return carry

    lax.fori_loop(0, 8, step, 0)


def conv_body(final, *refs):
    core_ref, own_ref, other_ref, kernel_ref = refs[:4]
    acts, products = refs[-2:]
    lane = lax.broadcasted_iota(jnp.int32, (32, 128), 1)
    assemble(core_ref, own_ref, other_ref, acts)

    def step(pair, carry):
        products[pair] = jnp.dot(kernel_ref[...], acts[pair], preferred_element_type=F32)
        return carry

    lax.fori_loop(0, 8, step, 0)

    def output(cell):
        sums = []
        for k in range(3):
            total = None
            for i in range(3):
                for j in range(3):
                    t, h = cell // 4 - 2 + i, cell % 4 - 1 + j
                    if not (0 <= t < 4 and 0 <= h < 4):
                        continue
                    source, row = t * 4 + h, (9 * i + 3 * j + k) * 32
                    left = source % 2 * 128
                    term = products[source // 2, row : row + 32, left : left + 128]
                    total = term if total is None else total + term
            sums.append(total)
        behind = jnp.where(lane == 0, 0.0, pltpu.roll(sums[0], 1, 1))
        ahead = jnp.where(lane == 127, 0.0, pltpu.roll(sums[2], 127, 1))
        return behind + sums[1] + ahead

    if final:
        extra_ref, out_ref = refs[4], refs[5]
        for cell in range(16):
            out_ref[cell] = extra_ref[cell].astype(F32) + output(cell)
    else:
        hidden_ref, out_ref = refs[4], refs[5]
        for cell in range(16):
            hidden_ref[cell] = output(cell)
        act_body(hidden_ref, out_ref)


def spread(field_ref, shifted, columns):
    lane = lax.broadcasted_iota(jnp.int32, (32, 128), 1)
    for cell in range(16):
        value = field_ref[cell].astype(F32)
        ahead = jnp.where(lane == 127, 0.0, pltpu.roll(value, 127, 1))
        behind = jnp.where(lane == 0, 0.0, pltpu.roll(value, 1, 1))
        shifted[0, cell] = ahead.astype(BF16)
        shifted[1, cell] = field_ref[cell]
        shifted[2, cell] = behind.astype(BF16)
    zero = jnp.zeros((32, 128), BF16)
    for index, (i, j, k) in enumerate(TAPS):
        for cell in range(16):
            t, h = cell // 4 + 2 - i, cell % 4 + 1 - j
            inside = 0 <= t < 4 and 0 <= h < 4
            value = shifted[k, t * 4 + h] if inside else zero
            left = cell % 2 * 128
            columns[cell // 2, index * 32 : index * 32 + 32, left : left + 128] = value


def partial_body(core_ref, field_ref, kernel_ref, mine_ref, theirs_ref, shifted, columns):
    spread(field_ref, shifted, columns)
    first = core_ref[0] == 0

    def step(pair, carry):
        out = jnp.dot(kernel_ref[...], columns[pair], preferred_element_type=F32)
        for half in range(2):
            part = out[:, half * 128 : half * 128 + 128]
            for n in range(8):
                low, high = part[n * 64 : n * 64 + 32], part[n * 64 + 32 : n * 64 + 64]
                mine_ref[n, pair * 2 + half] = jnp.where(first, low, high)
                theirs_ref[n, pair * 2 + half] = jnp.where(first, high, low).astype(BF16)
        return carry

    lax.fori_loop(0, 8, step, 0)


def grad_body(place_ref, field_ref, own_ref, other_ref, mine_ref, theirs_ref, shifted, columns, acts, total):
    spread(field_ref, shifted, columns)
    assemble(place_ref, own_ref, other_ref, acts)
    first = place_ref[1] == 0

    def step(pair, carry):
        term = lax.dot_general(
            columns[pair], acts[pair], (((1,), (1,)), ((), ())), preferred_element_type=F32
        )
        total[...] += term
        return carry

    total[...] = jnp.zeros_like(total)
    lax.fori_loop(0, 8, step, 0)
    for piece in range(8):
        left = piece % 4 * 128
        for k in range(27):
            row = k * 32 + piece // 4 * 8
            low = total[row : row + 8, left : left + 128]
            high = total[row + 16 : row + 24, left : left + 128]
            mine_ref[piece, k] = jnp.where(first, low, high)
            theirs_ref[piece, k] = jnp.where(first, high, low).astype(BF16)


def combine_body(place_ref, mine_ref, got_ref, *out_refs):
    here = place_ref[2]
    for k in range(8):
        x, y = lax.rem(here // 2 + k // 2, 4), lax.rem(here + k, 2)
        n = x * 2 + y
        for cell in range(16):
            out_refs[k][cell] = (mine_ref[n, cell] + got_ref[n, cell].astype(F32)).astype(BF16)


def total_body(pieces_ref, out_ref):
    for k in range(27):
        total = pieces_ref[0, k].astype(F32)
        for n in range(1, 8):
            total = total + pieces_ref[n, k].astype(F32)
        value = total.astype(BF16)
        for n in range(8):
            out_ref[n, k] = value


def finish_body(place_ref, full_ref, other_ref, out_ref):
    yl = place_ref[1]
    for piece in range(8):
        left = piece % 4 * 128
        low = pl.multiple_of((yl * 2 + piece // 4) * 8, 8)
        high = pl.multiple_of((2 - yl * 2 + piece // 4) * 8, 8)
        for k in range(27):
            out_ref[k, pl.ds(low, 8), left : left + 128] = full_ref[piece, k].astype(F32)
            out_ref[k, pl.ds(high, 8), left : left + 128] = other_ref[piece, k].astype(F32)


FLOPS = 2 * 512 * 864 * 2048
WIDE = (8, 16, 32, 128)
PIECES = (8, 27, 8, 128)
COLUMNS = [((3,) + FIELD, BF16), ((8, 864, 256), BF16)]
ACTS = ((8, 512, 256), BF16)


def exchange(value, axes):
    return lax.all_to_all(value, axes, 0, 0, tiled=True)


def swap(value, axis):
    return lax.ppermute(value, axis, SWAP)


def input_partial(place, field, turned):
    mine, theirs = call(partial_body, [(WIDE, F32), (WIDE, BF16)], COLUMNS, 16, FLOPS, place, field, turned)
    return mine, swap(theirs, "core")


def kernel_grad(place, field, own, other):
    scratch = COLUMNS + [ACTS, ((864, 512), F32)]
    mine, theirs = call(grad_body, [(PIECES, F32), (PIECES, BF16)], scratch, 20, FLOPS, place, field, own, other)
    got = swap(theirs, "yl")
    return (mine + got.astype(F32)).astype(BF16)


def reduce_clips(place, pair):
    (copies,) = call(total_body, [(PIECES, BF16)], [], 4, 1 << 20, exchange(pair, "z"))
    full = exchange(copies, "z")
    other = swap(full, "yl")
    (out,) = call(finish_body, [((27, 32, 512), F32)], [], 6, 1 << 20, place, full, other)
    return out.transpose(1, 0, 2)


def shards(block_in, conv_one, conv_two, out_cotangent):
    cells = lambda v: v[0].transpose(1, 2, 0, 3).reshape(FIELD)
    whole = lambda v: v.reshape(4, 4, 32, 128).transpose(2, 0, 1, 3)[None]
    rows = lambda w: w.transpose(1, 0, 2).reshape(864, 512)
    core, yl = lax.axis_index("core"), lax.axis_index("yl")
    place = jnp.stack([core, yl, lax.axis_index(XY)]).astype(jnp.int32)
    x_in, cot = cells(block_in), cells(out_cotangent)
    rows_one, rows_two = rows(conv_one), rows(conv_two)

    (copies,) = call(act_body, [(WIDE, BF16)], [], 4, 1 << 20, x_in)
    own = exchange(copies, XY)
    mine, got = input_partial(place, cot, rows_two.T)
    other = swap(own, "core")
    pair_two = (mine + got.astype(F32)).astype(BF16)
    pieces_two = exchange(pair_two, XY)
    conv_scratch = [ACTS, ((8, 864, 256), F32)]
    hidden, copies_two = call(
        functools.partial(conv_body, False), [(FIELD, F32), (WIDE, BF16)], conv_scratch, 18, FLOPS,
        place, own, other, rows_one,
    )
    own_two = exchange(copies_two, XY)
    (hidden_grad,) = call(
        functools.partial(pull_body, 1, False), [(FIELD, BF16)], [(FIELD, F32)] * 2, 6, 1 << 20,
        hidden, pieces_two,
    )
    grad_one = kernel_grad(place, hidden_grad, own, other)
    mine, got = input_partial(place, hidden_grad, rows_one.T)
    sends = call(combine_body, [(FIELD, BF16)] * 8, [], 10, 1 << 20, place, mine, got)
    pieces_one = [sends[0]]
    for k in range(1, 8):
        perm = [(n, (n // 2 + k // 2) % 4 * 2 + (n + k) % 2) for n in range(8)]
        pieces_one.append(lax.ppermute(sends[k], XY, perm))
    other_two = swap(own_two, "core")
    grad_two = kernel_grad(place, cot, own_two, other_two)
    out_one = reduce_clips(place, grad_one)
    out_two = reduce_clips(place, grad_two)
    (block_out,) = call(
        functools.partial(conv_body, True), [(FIELD, F32)], conv_scratch, 18, FLOPS,
        place, own_two, other_two, rows_two, x_in,
    )
    (in_grad,) = call(
        functools.partial(pull_body, 8, True), [(FIELD, F32)], [(FIELD, F32)] * 2, 6, 1 << 20,
        x_in, *pieces_one, cot,
    )
    return whole(block_out), whole(in_grad), out_one, out_two


def solution(mesh):
    fine = Mesh(mesh.devices.reshape(2, 8, 4, 2, 2), ("yl", "z", "x", "yh", "core"))
    clip, chan = ("yl", "z"), ("x", "yh", "core")
    field = P(clip, chan, None, None, None)
    kernel = P(chan, None, None)
    return jax.shard_map(
        shards,
        mesh=fine,
        in_specs=(field, kernel, kernel, field),
        out_specs=(field, field, kernel, kernel),
        check_vma=False,
    )
```

profile of v0, /device:TPU:2, one launch (start us, length us, event | category | flops | bytes accessed | tf_op | source)
XLA Modules:
  0.0 214.6 jit_solution(14423609286299857916)
XLA Ops:
  0.7 1.0 copy.16
  2.1 22.5 %all_to_all.35.refs_1_.own_ref = bf16[8,16,32,128]{3,2,1,0:T(8,128)(2,1)} all-to-all(bf16[8,16,32,128]{3,2,1,0:T(8,128)(2,1)S(1)} %shard_map.75), channel_id=1, replica_groups=mesh['yl'=2,'z'=8,'x'=4,'yh'=2,'core'=2] {'x','yh'}, dimensions={0} | all-to-all | bytes 2097152 | tf_op jit(solution)/shard_map/all_to_all | solution.py:243
  25.3 5.6 %shard_map.78 = (f32[8,16,32,128]{3,2,1,0:T(8,128)S(1)}, bf16[8,16,32,128]{3,2,1,0:T(8,128)(2,1)}) custom-call(s32[3]{0:T(128)S(1)} %pad_add_fusion.refs_0_.core_ref.place_ref, bf16[16,32,128]{2,1,0:T(8,128)(2,1)S(1)} %bitcast.43, bf16[512,864]{1,0:T(8,128)(2,1)S(1)} %bitcast.37), custom_call_target="tpu_custom_call" | custom-call | flops 1811939328 | bytes 4194304 | tf_op jit(solution)/shard_map/pallas_call | solution.py:23
  31.4 6.7 %shard_map.76 = (f32[16,32,128]{2,1,0:T(8,128)S(1)}, bf16[8,16,32,128]{3,2,1,0:T(8,128)(2,1)}) custom-call(s32[3]{0:T(128)S(1)} %pad_add_fusion.refs_0_.core_ref.place_ref, bf16[8,16,32,128]{3,2,1,0:T(8,128)(2,1)} %all_to_all.35.refs_1_.own_ref, bf16[8,16,32,128]{3,2,1,0:T(8,128)(2,1)} %collective-permute-done.refs_2_.other_ref, bf16[864,512]{1,0:T(8,128)(2,1)S(1)} %bitcast.39), custom_call_target="tpu_custom_call" | custom-call | flops 1811939328 | bytes 4194304 | tf_op jit(solution)/shard_map/pallas_call | solution.py:23
  38.1 5.8 %all-to-all-start.1 = ((bf16[8,16,32,128]{3,2,1,0:T(8,128)(2,1)}), bf16[8,16,32,128]{3,2,1,0:T(8,128)(2,1)}, u32[]{:S(2)}, u32[]{:S(2)}) async-start(bf16[8,16,32,128]{3,2,1,0:T(8,128)(2,1)} %get-tuple-element.22), calls=%async_computation.1 | async-start | bytes 2097152 | tf_op jit(solution)/shard_map/all_to_all | solution.py:243
  43.9 2.5 %add_convert_fusion = bf16[8,16,32,128]{3,2,1,0:T(8,128)(2,1)} fusion(f32[8,16,32,128]{3,2,1,0:T(8,128)S(1)} %get-tuple-element.24, bf16[8,16,32,128]{3,2,1,0:T(8,128)(2,1)} %collective-permute-done.2), kind=kLoop, calls=%fused_computation | loop fusion | flops 1572864 | bytes 4194304 | tf_op jit(solution)/shard_map/convert_element_type | solution.py:283
  46.4 12.7 %all-to-all-done.1.refs_1_.own_ref = bf16[8,16,32,128]{3,2,1,0:T(8,128)(2,1)} async-done(((bf16[8,16,32,128]{3,2,1,0:T(8,128)(2,1)}), bf16[8,16,32,128]{3,2,1,0:T(8,128)(2,1)}, u32[]{:S(2)}, u32[]{:S(2)}) %all-to-all-start.1) | async-done | bytes 1048608 | tf_op jit(solution)/shard_map/all_to_all | solution.py:243
  59.2 5.4 %all-to-all-start.2 = ((bf16[8,16,32,128]{3,2,1,0:T(8,128)(2,1)}), bf16[8,16,32,128]{3,2,1,0:T(8,128)(2,1)S(1)}, u32[]{:S(2)}, u32[]{:S(2)}) async-start(bf16[8,16,32,128]{3,2,1,0:T(8,128)(2,1)} %add_convert_fusion), calls=%async_computation.2 | async-start | bytes 2097152 | tf_op jit(solution)/shard_map/all_to_all | solution.py:243
  64.5 14.5 %all-to-all-done.2.refs_1_ = bf16[8,16,32,128]{3,2,1,0:T(8,128)(2,1)S(1)} async-done(((bf16[8,16,32,128]{3,2,1,0:T(8,128)(2,1)}), bf16[8,16,32,128]{3,2,1,0:T(8,128)(2,1)S(1)}, u32[]{:S(2)}, u32[]{:S(2)}) %all-to-all-start.2) | async-done | bytes 1048608 | tf_op jit(solution)/shard_map/all_to_all | solution.py:243
  79.7 6.2 %shard_map.83 = (f32[8,27,8,128]{3,2,1,0:T(8,128)S(1)}, bf16[8,27,8,128]{3,2,1,0:T(8,128)(2,1)S(1)}) custom-call(s32[3]{0:T(128)S(1)} %pad_add_fusion.refs_0_.core_ref.place_ref, bf16[16,32,128]{2,1,0:T(8,128)(2,1)S(1)} %shard_map.79.field_ref, bf16[8,16,32,128]{3,2,1,0:T(8,128)(2,1)} %all_to_all.35.refs_1_.own_ref, ...), custom_call_target="tpu_custom_call" | custom-call | flops 1811939328 | bytes 4194304 | tf_op jit(solution)/shard_map/pallas_call | solution.py:23
  85.9 0.8 collective-permute-start.11
  86.6 9.9 %collective-permute-done.11 = bf16[8,27,8,128]{3,2,1,0:T(8,128)(2,1)S(1)} collective-permute-done((bf16[8,27,8,128]{3,2,1,0:T(8,128)(2,1)S(1)}, bf16[8,27,8,128]{3,2,1,0:T(8,128)(2,1)S(1)}, u32[]{:S(2)}, u32[]{:S(2)}) %collective-permute-start.11) | collective-permute-done | bytes 442400 | tf_op jit(solution)/shard_map/ppermute | solution.py:247
  96.5 0.9 add_convert_fusion.2
  97.4 8.4 %all-to-all-start.3 = ((bf16[8,27,8,128]{3,2,1,0:T(8,128)(2,1)}), bf16[8,27,8,128]{3,2,1,0:T(8,128)(2,1)S(1)}, u32[]{:S(2)}, u32[]{:S(2)}) async-start(bf16[8,27,8,128]{3,2,1,0:T(8,128)(2,1)} %add_convert_fusion.2), calls=%async_computation.3 | async-start | bytes 884736 | tf_op jit(solution)/shard_map/all_to_all | solution.py:243
  105.8 6.3 %shard_map.86 = (f32[8,27,8,128]{3,2,1,0:T(8,128)S(1)}, bf16[8,27,8,128]{3,2,1,0:T(8,128)(2,1)S(1)}) custom-call(s32[3]{0:T(128)S(1)} %pad_add_fusion.refs_0_.core_ref.place_ref, bf16[16,32,128]{2,1,0:T(8,128)(2,1)S(1)} %bitcast.44, bf16[8,16,32,128]{3,2,1,0:T(8,128)(2,1)} %all-to-all-done.1.refs_1_.own_ref, ...), custom_call_target="tpu_custom_call" | custom-call | flops 1811939328 | bytes 4194304 | tf_op jit(solution)/shard_map/pallas_call | solution.py:23
  112.1 0.8 collective-permute-start.13
  112.9 8.7 %collective-permute-done.13 = bf16[8,27,8,128]{3,2,1,0:T(8,128)(2,1)S(1)} collective-permute-done((bf16[8,27,8,128]{3,2,1,0:T(8,128)(2,1)S(1)}, bf16[8,27,8,128]{3,2,1,0:T(8,128)(2,1)S(1)}, u32[]{:S(2)}, u32[]{:S(2)}) %collective-permute-start.13) | collective-permute-done | bytes 442400 | tf_op jit(solution)/shard_map/ppermute | solution.py:247
  121.6 0.9 add_convert_fusion.1
  122.4 6.9 %all-to-all-start.5 = ((bf16[8,27,8,128]{3,2,1,0:T(8,128)(2,1)}), bf16[8,27,8,128]{3,2,1,0:T(8,128)(2,1)S(1)}, u32[]{:S(2)}, u32[]{:S(2)}) async-start(bf16[8,27,8,128]{3,2,1,0:T(8,128)(2,1)} %add_convert_fusion.1), calls=%async_computation.5 | async-start | bytes 884736 | tf_op jit(solution)/shard_map/all_to_all | solution.py:243
  129.3 0.8 shard_map.84
  130.2 11.6 %all-to-all-done.5.pieces_ref = bf16[8,27,8,128]{3,2,1,0:T(8,128)(2,1)S(1)} async-done(((bf16[8,27,8,128]{3,2,1,0:T(8,128)(2,1)}), bf16[8,27,8,128]{3,2,1,0:T(8,128)(2,1)S(1)}, u32[]{:S(2)}, u32[]{:S(2)}) %all-to-all-start.5) | async-done | bytes 442400 | tf_op jit(solution)/shard_map/all_to_all | solution.py:243
  141.8 3.5 %all-to-all-start.4 = ((bf16[8,27,8,128]{3,2,1,0:T(8,128)(2,1)}), bf16[8,27,8,128]{3,2,1,0:T(8,128)(2,1)S(1)}, u32[]{:S(2)}, u32[]{:S(2)}) async-start(bf16[8,27,8,128]{3,2,1,0:T(8,128)(2,1)} %shard_map.84), calls=%async_computation.4 | async-start | bytes 884736 | tf_op jit(solution)/shard_map/all_to_all | solution.py:243
  145.2 1.3 copy.20
  146.5 1.2 copy-done
  147.7 5.6 %shard_map.80 = (f32[8,16,32,128]{3,2,1,0:T(8,128)S(1)}, bf16[8,16,32,128]{3,2,1,0:T(8,128)(2,1)}) custom-call(s32[3]{0:T(128)S(1)} %pad_add_fusion.refs_0_.core_ref.place_ref, bf16[16,32,128]{2,1,0:T(8,128)(2,1)S(1)} %shard_map.79.field_ref, bf16[512,864]{1,0:T(8,128)(2,1)S(1)} %bitcast.38), custom_call_target="tpu_custom_call" | custom-call | flops 1811939328 | bytes 4194304 | tf_op jit(solution)/shard_map/pallas_call | solution.py:23
  153.3 0.8 shard_map.87
  154.2 3.4 %all-to-all-done.4.full_ref = bf16[8,27,8,128]{3,2,1,0:T(8,128)(2,1)S(1)} async-done(((bf16[8,27,8,128]{3,2,1,0:T(8,128)(2,1)}), bf16[8,27,8,128]{3,2,1,0:T(8,128)(2,1)S(1)}, u32[]{:S(2)}, u32[]{:S(2)}) %all-to-all-start.4) | async-done | bytes 442400 | tf_op jit(solution)/shard_map/all_to_all | solution.py:243
  157.6 3.7 %all-to-all-start.6 = ((bf16[8,27,8,128]{3,2,1,0:T(8,128)(2,1)}), bf16[8,27,8,128]{3,2,1,0:T(8,128)(2,1)S(1)}, u32[]{:S(2)}, u32[]{:S(2)}) async-start(bf16[8,27,8,128]{3,2,1,0:T(8,128)(2,1)} %shard_map.87), calls=%async_computation.6 | async-start | bytes 884736 | tf_op jit(solution)/shard_map/all_to_all | solution.py:243
  161.3 2.0 shard_map.81
  163.3 0.7 copy-done.10
  164.7 2.5 %collective-permute-start.4 = (bf16[16,32,128]{2,1,0:T(8,128)(2,1)}, bf16[16,32,128]{2,1,0:T(8,128)(2,1)S(1)}, u32[]{:S(2)}, u32[]{:S(2)}) collective-permute-start(bf16[16,32,128]{2,1,0:T(8,128)(2,1)} %get-tuple-element.29), channel_id=1, source_target_pairs={{0,2},{2,0},{4,6},{6,4},{8,10},{10,8},{12,14},{14,12},{1,3},{3,1},... | collective-permute-start | bytes 393224 | tf_op jit(solution)/shard_map/ppermute | solution.py:301
  167.1 0.8 collective-permute-start.12
  167.9 9.8 %all-to-all-done.6.full_ref = bf16[8,27,8,128]{3,2,1,0:T(8,128)(2,1)S(1)} async-done(((bf16[8,27,8,128]{3,2,1,0:T(8,128)(2,1)}), bf16[8,27,8,128]{3,2,1,0:T(8,128)(2,1)S(1)}, u32[]{:S(2)}, u32[]{:S(2)}) %all-to-all-start.6) | async-done | bytes 442400 | tf_op jit(solution)/shard_map/all_to_all | solution.py:243
  177.7 0.7 collective-permute-start.14
  178.4 5.4 %collective-permute-start.5 = (bf16[16,32,128]{2,1,0:T(8,128)(2,1)}, bf16[16,32,128]{2,1,0:T(8,128)(2,1)S(1)}, u32[]{:S(2)}, u32[]{:S(2)}) collective-permute-start(bf16[16,32,128]{2,1,0:T(8,128)(2,1)} %copy-done.11), channel_id=1, source_target_pairs={{0,4},{2,6},{4,8},{6,10},{8,12},{10,14},{12,0},{14,2},{1,5},{3,7},... | collective-permute-start | bytes 393224 | tf_op jit(solution)/shard_map/ppermute | solution.py:301
  183.8 0.8 collective-permute-start.6
  184.7 3.4 %collective-permute-done.5.refs_3_ = bf16[16,32,128]{2,1,0:T(8,128)(2,1)S(1)} collective-permute-done((bf16[16,32,128]{2,1,0:T(8,128)(2,1)}, bf16[16,32,128]{2,1,0:T(8,128)(2,1)S(1)}, u32[]{:S(2)}, u32[]{:S(2)}) %collective-permute-start.5) | collective-permute-done | bytes 131104 | tf_op jit(solution)/shard_map/ppermute | solution.py:301
  188.1 2.5 %collective-permute-start.8 = (bf16[16,32,128]{2,1,0:T(8,128)(2,1)}, bf16[16,32,128]{2,1,0:T(8,128)(2,1)S(1)}, u32[]{:S(2)}, u32[]{:S(2)}) collective-permute-start(bf16[16,32,128]{2,1,0:T(8,128)(2,1)} %copy-done.8), channel_id=1, source_target_pairs={{0,10},{2,8},{4,14},{6,12},{8,2},{10,0},{12,6},{14,4},{1,11},{3,9}... | collective-permute-start | bytes 393224 | tf_op jit(solution)/shard_map/ppermute | solution.py:301
  190.6 3.2 %collective-permute-done.6.refs_4_ = bf16[16,32,128]{2,1,0:T(8,128)(2,1)S(1)} collective-permute-done((bf16[16,32,128]{2,1,0:T(8,128)(2,1)}, bf16[16,32,128]{2,1,0:T(8,128)(2,1)S(1)}, u32[]{:S(2)}, u32[]{:S(2)}) %collective-permute-start.6) | collective-permute-done | bytes 131104 | tf_op jit(solution)/shard_map/ppermute | solution.py:301
  193.8 3.0 %collective-permute-start.10 = (bf16[16,32,128]{2,1,0:T(8,128)(2,1)S(1)}, bf16[16,32,128]{2,1,0:T(8,128)(2,1)S(1)}, u32[]{:S(2)}, u32[]{:S(2)}) collective-permute-start(bf16[16,32,128]{2,1,0:T(8,128)(2,1)S(1)} %get-tuple-element.35), channel_id=1, source_target_pairs={{0,14},{2,12},{4,2},{6,0},{8,6},{10,4},{12,10},{14,8},{1,15},{3,13... | collective-permute-start | bytes 393224 | tf_op jit(solution)/shard_map/ppermute | solution.py:301
  196.9 1.0 collective-permute-done.8.refs_6_
  197.8 1.2 collective-permute-done.9.refs_7_
  199.0 4.3 %collective-permute-done.10.refs_8_ = bf16[16,32,128]{2,1,0:T(8,128)(2,1)S(1)} collective-permute-done((bf16[16,32,128]{2,1,0:T(8,128)(2,1)S(1)}, bf16[16,32,128]{2,1,0:T(8,128)(2,1)S(1)}, u32[]{:S(2)}, u32[]{:S(2)}) %collective-permute-start.10) | collective-permute-done | bytes 131104 | tf_op jit(solution)/shard_map/ppermute | solution.py:301
  203.9 0.9 copy.24
  204.8 5.0 %shard_map.77 = f32[16,32,128]{2,1,0:T(8,128)S(1)} custom-call(s32[3]{0:T(128)S(1)} %pad_add_fusion.refs_0_.core_ref.place_ref, bf16[8,16,32,128]{3,2,1,0:T(8,128)(2,1)} %all-to-all-done.1.refs_1_.own_ref, bf16[8,16,32,128]{3,2,1,0:T(8,128)(2,1)S(1)} %copy-done.6, bf16[864,512]{1,0:T(8,128)(2,1)S(1)} %bitcast.42, bf16[16,32,128]{2,1,0:T(8,128)(2,1)S(1)} %bitcast.35), custom_call_target="tpu_custom_call" | custom-call | flops 1811939328 | bytes 4194304 | tf_op jit(solution)/shard_map/pallas_call | solution.py:23
  209.8 0.9 copy.25
  210.7 2.0 shard_map.85
  212.6 2.0 shard_map.88
  (45 shorter events, 3.6 us)
Async XLA Ops:
  0.6 23.9 %copy-start.12 = (bf16[1,32,4,4,128]{4,3,2,1,0:T(4,128)(2,1)S(1)}, bf16[1,32,4,4,128]{4,3,2,1,0:T(4,128)(2,1)}, u32[]{:S(2)}) copy-start(bf16[1,32,4,4,128]{4,3,2,1,0:T(4,128)(2,1)} %param.7) | copy-start | bytes 393220
  0.6 23.9 %copy-start.3 = (bf16[32,27,512]{2,0,1:T(8,128)(2,1)S(1)}, bf16[32,27,512]{2,0,1:T(8,128)(2,1)}, u32[]{:S(2)}) copy-start(bf16[32,27,512]{2,0,1:T(8,128)(2,1)} %param.6) | copy-start | bytes 2654212
  24.5 6.9 %collective-permute-start = (bf16[8,16,32,128]{3,2,1,0:T(8,128)(2,1)}, bf16[8,16,32,128]{3,2,1,0:T(8,128)(2,1)}, u32[]{:S(2)}, u32[]{:S(2)}) collective-permute-start(bf16[8,16,32,128]{3,2,1,0:T(8,128)(2,1)} %all_to_all.35.refs_1_.own_ref), channel_id=1, source_target_pairs={{0,1},{1,0},{2,3},{3,2},{4,5},{5,4},{6,7},{7,6},{8,9},{9,8},{10,11... | collective-permute-start | bytes 3145736 | tf_op jit(solution)/shard_map/ppermute | solution.py:247
  25.3 6.2 %copy-start.1 = (bf16[32,27,512]{2,0,1:T(8,128)(2,1)S(1)}, bf16[32,27,512]{2,0,1:T(8,128)(2,1)}, u32[]{:S(2)}) copy-start(bf16[32,27,512]{2,0,1:T(8,128)(2,1)} %param.5) | copy-start | bytes 2654212
  30.9 13.0 %collective-permute-start.2 = (bf16[8,16,32,128]{3,2,1,0:T(8,128)(2,1)}, bf16[8,16,32,128]{3,2,1,0:T(8,128)(2,1)}, u32[]{:S(2)}, u32[]{:S(2)}) collective-permute-start(bf16[8,16,32,128]{3,2,1,0:T(8,128)(2,1)} %get-tuple-element.25), channel_id=1, source_target_pairs={{0,1},{1,0},{2,3},{3,2},{4,5},{5,4},{6,7},{7,6},{8,9},{9,8},{10,11... | collective-permute-start | bytes 3145736 | tf_op jit(solution)/shard_map/ppermute | solution.py:247
  38.1 21.1 %all-to-all-start.1 = ((bf16[8,16,32,128]{3,2,1,0:T(8,128)(2,1)}), bf16[8,16,32,128]{3,2,1,0:T(8,128)(2,1)}, u32[]{:S(2)}, u32[]{:S(2)}) async-start(bf16[8,16,32,128]{3,2,1,0:T(8,128)(2,1)} %get-tuple-element.22), calls=%async_computation.1 | async-start | bytes 2097152 | tf_op jit(solution)/shard_map/all_to_all | solution.py:243
  59.2 19.9 %all-to-all-start.2 = ((bf16[8,16,32,128]{3,2,1,0:T(8,128)(2,1)}), bf16[8,16,32,128]{3,2,1,0:T(8,128)(2,1)S(1)}, u32[]{:S(2)}, u32[]{:S(2)}) async-start(bf16[8,16,32,128]{3,2,1,0:T(8,128)(2,1)} %add_convert_fusion), calls=%async_computation.2 | async-start | bytes 2097152 | tf_op jit(solution)/shard_map/all_to_all | solution.py:243
  64.5 41.3 %collective-permute-start.1 = (bf16[8,16,32,128]{3,2,1,0:T(8,128)(2,1)}, bf16[8,16,32,128]{3,2,1,0:T(8,128)(2,1)S(1)}, u32[]{:S(2)}, u32[]{:S(2)}) collective-permute-start(bf16[8,16,32,128]{3,2,1,0:T(8,128)(2,1)} %all-to-all-done.1.refs_1_.own_ref), channel_id=1, source_target_pairs={{0,1},{1,0},{2,3},{3,2},{4,5},{5,4},{6,7},{7,6},{8,9},{9,8},{10,11... | collective-permute-start | bytes 3145736 | tf_op jit(solution)/shard_map/ppermute | solution.py:247
  85.9 10.6 %collective-permute-start.11 = (bf16[8,27,8,128]{3,2,1,0:T(8,128)(2,1)S(1)}, bf16[8,27,8,128]{3,2,1,0:T(8,128)(2,1)S(1)}, u32[]{:S(2)}, u32[]{:S(2)}) collective-permute-start(bf16[8,27,8,128]{3,2,1,0:T(8,128)(2,1)S(1)} %get-tuple-element.37), channel_id=1, source_target_pairs={{0,128},{128,0},{1,129},{129,1},{2,130},{130,2},{3,131},{131,3},{4... | collective-permute-start | bytes 1327112 | tf_op jit(solution)/shard_map/ppermute | solution.py:247
  97.4 25.1 %all-to-all-start.3 = ((bf16[8,27,8,128]{3,2,1,0:T(8,128)(2,1)}), bf16[8,27,8,128]{3,2,1,0:T(8,128)(2,1)S(1)}, u32[]{:S(2)}, u32[]{:S(2)}) async-start(bf16[8,27,8,128]{3,2,1,0:T(8,128)(2,1)} %add_convert_fusion.2), calls=%async_computation.3 | async-start | bytes 884736 | tf_op jit(solution)/shard_map/all_to_all | solution.py:243
  105.8 6.3 %copy-start.5 = (bf16[8,16,32,128]{3,2,1,0:T(8,128)(2,1)}, bf16[8,16,32,128]{3,2,1,0:T(8,128)(2,1)S(1)}, u32[]{:S(2)}) copy-start(bf16[8,16,32,128]{3,2,1,0:T(8,128)(2,1)S(1)} %collective-permute-done.1.refs_2_.other_ref) | copy-start | bytes 3145732
  112.1 9.5 %collective-permute-start.13 = (bf16[8,27,8,128]{3,2,1,0:T(8,128)(2,1)S(1)}, bf16[8,27,8,128]{3,2,1,0:T(8,128)(2,1)S(1)}, u32[]{:S(2)}, u32[]{:S(2)}) collective-permute-start(bf16[8,27,8,128]{3,2,1,0:T(8,128)(2,1)S(1)} %get-tuple-element.39), channel_id=1, source_target_pairs={{0,128},{128,0},{1,129},{129,1},{2,130},{130,2},{3,131},{131,3},{4... | collective-permute-start | bytes 1327112 | tf_op jit(solution)/shard_map/ppermute | solution.py:247
  121.6 23.7 %copy-start.2 = (bf16[32,27,512]{2,0,1:T(8,128)(2,1)S(1)}, bf16[32,27,512]{2,0,1:T(8,128)(2,1)}, u32[]{:S(2)}) copy-start(bf16[32,27,512]{2,0,1:T(8,128)(2,1)} %param.5) | copy-start | bytes 2654212
  122.4 19.3 %all-to-all-start.5 = ((bf16[8,27,8,128]{3,2,1,0:T(8,128)(2,1)}), bf16[8,27,8,128]{3,2,1,0:T(8,128)(2,1)S(1)}, u32[]{:S(2)}, u32[]{:S(2)}) async-start(bf16[8,27,8,128]{3,2,1,0:T(8,128)(2,1)} %add_convert_fusion.1), calls=%async_computation.5 | async-start | bytes 884736 | tf_op jit(solution)/shard_map/all_to_all | solution.py:243
  141.8 15.8 %all-to-all-start.4 = ((bf16[8,27,8,128]{3,2,1,0:T(8,128)(2,1)}), bf16[8,27,8,128]{3,2,1,0:T(8,128)(2,1)S(1)}, u32[]{:S(2)}, u32[]{:S(2)}) async-start(bf16[8,27,8,128]{3,2,1,0:T(8,128)(2,1)} %shard_map.84), calls=%async_computation.4 | async-start | bytes 884736 | tf_op jit(solution)/shard_map/all_to_all | solution.py:243
  146.5 1.2 copy-start
  153.3 8.0 %collective-permute-start.3 = (bf16[8,16,32,128]{3,2,1,0:T(8,128)(2,1)}, bf16[8,16,32,128]{3,2,1,0:T(8,128)(2,1)}, u32[]{:S(2)}, u32[]{:S(2)}) collective-permute-start(bf16[8,16,32,128]{3,2,1,0:T(8,128)(2,1)} %get-tuple-element.27), channel_id=1, source_target_pairs={{0,1},{1,0},{2,3},{3,2},{4,5},{5,4},{6,7},{7,6},{8,9},{9,8},{10,11... | collective-permute-start | bytes 3145736 | tf_op jit(solution)/shard_map/ppermute | solution.py:247
  157.6 20.1 %all-to-all-start.6 = ((bf16[8,27,8,128]{3,2,1,0:T(8,128)(2,1)}), bf16[8,27,8,128]{3,2,1,0:T(8,128)(2,1)S(1)}, u32[]{:S(2)}, u32[]{:S(2)}) async-start(bf16[8,27,8,128]{3,2,1,0:T(8,128)(2,1)} %shard_map.87), calls=%async_computation.6 | async-start | bytes 884736 | tf_op jit(solution)/shard_map/all_to_all | solution.py:243
  163.3 0.7 copy-start.10
  164.0 0.7 copy-start.11
  164.6 2.5 %copy-start.7 = (bf16[16,32,128]{2,1,0:T(8,128)(2,1)}, bf16[16,32,128]{2,1,0:T(8,128)(2,1)S(1)}, u32[]{:S(2)}) copy-start(bf16[16,32,128]{2,1,0:T(8,128)(2,1)S(1)} %get-tuple-element.34) | copy-start | bytes 393220
  164.7 2.5 %copy-start.8 = (bf16[16,32,128]{2,1,0:T(8,128)(2,1)}, bf16[16,32,128]{2,1,0:T(8,128)(2,1)S(1)}, u32[]{:S(2)}) copy-start(bf16[16,32,128]{2,1,0:T(8,128)(2,1)S(1)} %get-tuple-element.33) | copy-start | bytes 393220
  164.7 2.5 %copy-start.9 = (bf16[16,32,128]{2,1,0:T(8,128)(2,1)}, bf16[16,32,128]{2,1,0:T(8,128)(2,1)S(1)}, u32[]{:S(2)}) copy-start(bf16[16,32,128]{2,1,0:T(8,128)(2,1)S(1)} %get-tuple-element.32) | copy-start | bytes 393220
  164.7 40.1 %copy-start.4 = (bf16[32,27,512]{2,0,1:T(8,128)(2,1)S(1)}, bf16[32,27,512]{2,0,1:T(8,128)(2,1)}, u32[]{:S(2)}) copy-start(bf16[32,27,512]{2,0,1:T(8,128)(2,1)} %param.6) | copy-start | bytes 2654212
  164.7 20.0 %collective-permute-start.4 = (bf16[16,32,128]{2,1,0:T(8,128)(2,1)}, bf16[16,32,128]{2,1,0:T(8,128)(2,1)S(1)}, u32[]{:S(2)}, u32[]{:S(2)}) collective-permute-start(bf16[16,32,128]{2,1,0:T(8,128)(2,1)} %get-tuple-element.29), channel_id=1, source_target_pairs={{0,2},{2,0},{4,6},{6,4},{8,10},{10,8},{12,14},{14,12},{1,3},{3,1},... | collective-permute-start | bytes 393224 | tf_op jit(solution)/shard_map/ppermute | solution.py:301
  167.1 43.5 %collective-permute-start.12 = (bf16[8,27,8,128]{3,2,1,0:T(8,128)(2,1)S(1)}, bf16[8,27,8,128]{3,2,1,0:T(8,128)(2,1)S(1)}, u32[]{:S(2)}, u32[]{:S(2)}) collective-permute-start(bf16[8,27,8,128]{3,2,1,0:T(8,128)(2,1)S(1)} %all-to-all-done.4.full_ref), channel_id=1, source_target_pairs={{0,128},{128,0},{1,129},{129,1},{2,130},{130,2},{3,131},{131,3},{4... | collective-permute-start | bytes 1327112 | tf_op jit(solution)/shard_map/ppermute | solution.py:247
  177.7 27.1 %copy-start.6 = (bf16[8,16,32,128]{3,2,1,0:T(8,128)(2,1)S(1)}, bf16[8,16,32,128]{3,2,1,0:T(8,128)(2,1)}, u32[]{:S(2)}) copy-start(bf16[8,16,32,128]{3,2,1,0:T(8,128)(2,1)} %copy-done.5) | copy-start | bytes 3145732
  177.7 34.9 %collective-permute-start.14 = (bf16[8,27,8,128]{3,2,1,0:T(8,128)(2,1)S(1)}, bf16[8,27,8,128]{3,2,1,0:T(8,128)(2,1)S(1)}, u32[]{:S(2)}, u32[]{:S(2)}) collective-permute-start(bf16[8,27,8,128]{3,2,1,0:T(8,128)(2,1)S(1)} %all-to-all-done.6.full_ref), channel_id=1, source_target_pairs={{0,128},{128,0},{1,129},{129,1},{2,130},{130,2},{3,131},{131,3},{4... | collective-permute-start | bytes 1327112 | tf_op jit(solution)/shard_map/ppermute | solution.py:247
  178.4 9.7 %collective-permute-start.5 = (bf16[16,32,128]{2,1,0:T(8,128)(2,1)}, bf16[16,32,128]{2,1,0:T(8,128)(2,1)S(1)}, u32[]{:S(2)}, u32[]{:S(2)}) collective-permute-start(bf16[16,32,128]{2,1,0:T(8,128)(2,1)} %copy-done.11), channel_id=1, source_target_pairs={{0,4},{2,6},{4,8},{6,10},{8,12},{10,14},{12,0},{14,2},{1,5},{3,7},... | collective-permute-start | bytes 393224 | tf_op jit(solution)/shard_map/ppermute | solution.py:301
  183.8 10.0 %collective-permute-start.6 = (bf16[16,32,128]{2,1,0:T(8,128)(2,1)}, bf16[16,32,128]{2,1,0:T(8,128)(2,1)S(1)}, u32[]{:S(2)}, u32[]{:S(2)}) collective-permute-start(bf16[16,32,128]{2,1,0:T(8,128)(2,1)} %copy-done.10), channel_id=1, source_target_pairs={{0,6},{2,4},{4,10},{6,8},{8,14},{10,12},{12,2},{14,0},{1,7},{3,5},... | collective-permute-start | bytes 393224 | tf_op jit(solution)/shard_map/ppermute | solution.py:301
  184.6 9.2 %collective-permute-start.7 = (bf16[16,32,128]{2,1,0:T(8,128)(2,1)}, bf16[16,32,128]{2,1,0:T(8,128)(2,1)S(1)}, u32[]{:S(2)}, u32[]{:S(2)}) collective-permute-start(bf16[16,32,128]{2,1,0:T(8,128)(2,1)} %copy-done.9), channel_id=1, source_target_pairs={{0,8},{2,10},{4,12},{6,14},{8,0},{10,2},{12,4},{14,6},{1,9},{3,11}... | collective-permute-start | bytes 393224 | tf_op jit(solution)/shard_map/ppermute | solution.py:301
  188.1 9.7 %collective-permute-start.8 = (bf16[16,32,128]{2,1,0:T(8,128)(2,1)}, bf16[16,32,128]{2,1,0:T(8,128)(2,1)S(1)}, u32[]{:S(2)}, u32[]{:S(2)}) collective-permute-start(bf16[16,32,128]{2,1,0:T(8,128)(2,1)} %copy-done.8), channel_id=1, source_target_pairs={{0,10},{2,8},{4,14},{6,12},{8,2},{10,0},{12,6},{14,4},{1,11},{3,9}... | collective-permute-start | bytes 393224 | tf_op jit(solution)/shard_map/ppermute | solution.py:301
  193.8 5.2 %collective-permute-start.9 = (bf16[16,32,128]{2,1,0:T(8,128)(2,1)}, bf16[16,32,128]{2,1,0:T(8,128)(2,1)S(1)}, u32[]{:S(2)}, u32[]{:S(2)}) collective-permute-start(bf16[16,32,128]{2,1,0:T(8,128)(2,1)} %copy-done.7), channel_id=1, source_target_pairs={{0,12},{2,14},{4,0},{6,2},{8,4},{10,6},{12,8},{14,10},{1,13},{3,15... | collective-permute-start | bytes 393224 | tf_op jit(solution)/shard_map/ppermute | solution.py:301
  193.8 9.4 %collective-permute-start.10 = (bf16[16,32,128]{2,1,0:T(8,128)(2,1)S(1)}, bf16[16,32,128]{2,1,0:T(8,128)(2,1)S(1)}, u32[]{:S(2)}, u32[]{:S(2)}) collective-permute-start(bf16[16,32,128]{2,1,0:T(8,128)(2,1)S(1)} %get-tuple-element.35), channel_id=1, source_target_pairs={{0,14},{2,12},{4,2},{6,0},{8,6},{10,4},{12,10},{14,8},{1,15},{3,13... | collective-permute-start | bytes 393224 | tf_op jit(solution)/shard_map/ppermute | solution.py:301
where the time goes:
time: 218 us; the launch traced here: 215 us
  waiting for transfers between devices  83.6 us (38%)
  starting transfers between devices  51.5 us (24%)
  Pallas kernels  44.7 us (21%)
  blocking collectives  22.5 us (10%)
  local copies, waits for them, and re-layouts  7.21 us (3%)
  other arithmetic  4.3 us (2%)
    all_to_all x6, waiting for transfers between devices, exchange(): return lax.all_to_all(value, axes, 0, 0, tiled=True)  52 us
    pallas_call x14, Pallas kernels, call(): pl.pallas_call(body, out_shape=tuple((jax.ShapeDtypeStruct(*o) for o in o...  44.7 us
    all_to_all x6, starting transfers between devices, exchange(): return lax.all_to_all(value, axes, 0, 0, tiled=True)  33.7 us
    all_to_all x1, blocking collectives, exchange(): return lax.all_to_all(value, axes, 0, 0, tiled=True)  22.5 us
    ppermute x8, waiting for transfers between devices, swap(): return lax.ppermute(value, axis, SWAP)  18.6 us
    ppermute x7, starting transfers between devices, shards(): pieces_one.append(lax.ppermute(sends[k], XY, perm))  14.3 us
    ppermute x7, waiting for transfers between devices, shards(): pieces_one.append(lax.ppermute(sends[k], XY, perm))  13 us
  transfers between devices with their start and end apart: 21, of which 12 were waited for; matrix products, arithmetic and copies ran while one was open for 4% of the time, Pallas kernels for 20%

commit v1 on v0

--- a/solution.py
+++ b/solution.py
@@ -57,9 +57,9 @@
             out_ref[copy, cell] = value
 
 
-def pull_body(count, final, *refs):
-    field_ref, pieces = refs[0], refs[1 : 1 + count]
-    extra_ref = refs[1 + count] if final else None
+def pull_body(final, *refs):
+    field_ref, pieces = refs[0], refs[1:9]
+    extra_ref = refs[9] if final else None
     out_ref, normed_ref, down_ref = refs[-3:]
     center, scale = moments(lambda cell: field_ref[cell].astype(F32))
     first = jnp.zeros((32, 128), F32)
@@ -68,7 +68,7 @@
         normed = (field_ref[cell].astype(F32) - center) * scale
         grad = None
         for n in range(8):
-            piece = (pieces[0][n, cell] if count == 1 else pieces[n][cell]).astype(F32)
+            piece = pieces[n][cell].astype(F32)
             grad = piece if grad is None else grad + piece
         gate = jax.nn.sigmoid(normed)
         down = grad * (gate * (1.0 + normed * (1.0 - gate)))
@@ -161,21 +161,25 @@
             columns[cell // 2, index * 32 : index * 32 + 32, left : left + 128] = value
 
 
-def partial_body(core_ref, field_ref, kernel_ref, mine_ref, theirs_ref, shifted, columns):
+def partial_body(place_ref, field_ref, other_ref, kernel_ref, far_ref, *refs):
+    out_refs, (shifted, columns, far_columns, result) = refs[:8], refs[8:]
     spread(field_ref, shifted, columns)
-    first = core_ref[0] == 0
+    spread(other_ref, shifted, far_columns)
 
     def step(pair, carry):
         out = jnp.dot(kernel_ref[...], columns[pair], preferred_element_type=F32)
+        out = out + jnp.dot(far_ref[...], far_columns[pair], preferred_element_type=F32)
         for half in range(2):
-            part = out[:, half * 128 : half * 128 + 128]
             for n in range(8):
-                low, high = part[n * 64 : n * 64 + 32], part[n * 64 + 32 : n * 64 + 64]
-                mine_ref[n, pair * 2 + half] = jnp.where(first, low, high)
-                theirs_ref[n, pair * 2 + half] = jnp.where(first, high, low).astype(BF16)
+                part = out[n * 32 : n * 32 + 32, half * 128 : half * 128 + 128]
+                result[n, pair * 2 + half] = part.astype(BF16)
         return carry
 
     lax.fori_loop(0, 8, step, 0)
+    here = place_ref[2]
+    for k in range(8):
+        n = lax.rem(here // 2 + k // 2, 4) * 2 + lax.rem(here + k, 2)
+        out_refs[k][...] = result[n]
 
 
 def grad_body(place_ref, field_ref, own_ref, other_ref, mine_ref, theirs_ref, shifted, columns, acts, total):
@@ -202,15 +206,6 @@
             theirs_ref[piece, k] = jnp.where(first, high, low).astype(BF16)
 
 
-def combine_body(place_ref, mine_ref, got_ref, *out_refs):
-    here = place_ref[2]
-    for k in range(8):
-        x, y = lax.rem(here // 2 + k // 2, 4), lax.rem(here + k, 2)
-        n = x * 2 + y
-        for cell in range(16):
-            out_refs[k][cell] = (mine_ref[n, cell] + got_ref[n, cell].astype(F32)).astype(BF16)
-
-
 def total_body(pieces_ref, out_ref):
     for k in range(27):
         total = pieces_ref[0, k].astype(F32)
@@ -247,9 +242,23 @@
     return lax.ppermute(value, axis, SWAP)
 
 
-def input_partial(place, field, turned):
-    mine, theirs = call(partial_body, [(WIDE, F32), (WIDE, BF16)], COLUMNS, 16, FLOPS, place, field, turned)
-    return mine, swap(theirs, "core")
+def split_kernel(place, rows):
+    blocks = rows.T.reshape(8, 2, 32, 864)
+    first = place[0] == 0
+    near = jnp.where(first, blocks[:, 0], blocks[:, 1]).reshape(256, 864)
+    away = jnp.where(first, blocks[:, 1], blocks[:, 0]).reshape(256, 864)
+    return near, swap(away, "core")
+
+
+def input_partial(place, field, kernels):
+    other = swap(field, "core")
+    scratch = COLUMNS + [COLUMNS[1], (WIDE, BF16)]
+    sends = call(partial_body, [(FIELD, BF16)] * 8, scratch, 16, FLOPS, place, field, other, *kernels)
+    pieces = [sends[0]]
+    for k in range(1, 8):
+        perm = [(n, (n // 2 + k // 2) % 4 * 2 + (n + k) % 2) for n in range(8)]
+        pieces.append(lax.ppermute(sends[k], XY, perm))
+    return pieces
 
 
 def kernel_grad(place, field, own, other):
@@ -278,10 +287,9 @@
 
     (copies,) = call(act_body, [(WIDE, BF16)], [], 4, 1 << 20, x_in)
     own = exchange(copies, XY)
-    mine, got = input_partial(place, cot, rows_two.T)
+    split_two = split_kernel(place, rows_two)
+    pieces_two = input_partial(place, cot, split_two)
     other = swap(own, "core")
-    pair_two = (mine + got.astype(F32)).astype(BF16)
-    pieces_two = exchange(pair_two, XY)
     conv_scratch = [ACTS, ((8, 864, 256), F32)]
     hidden, copies_two = call(
         functools.partial(conv_body, False), [(FIELD, F32), (WIDE, BF16)], conv_scratch, 18, FLOPS,
@@ -289,16 +297,12 @@
     )
     own_two = exchange(copies_two, XY)
     (hidden_grad,) = call(
-        functools.partial(pull_body, 1, False), [(FIELD, BF16)], [(FIELD, F32)] * 2, 6, 1 << 20,
-        hidden, pieces_two,
+        functools.partial(pull_body, False), [(FIELD, BF16)], [(FIELD, F32)] * 2, 6, 1 << 20,
+        hidden, *pieces_two,
     )
     grad_one = kernel_grad(place, hidden_grad, own, other)
-    mine, got = input_partial(place, hidden_grad, rows_one.T)
-    sends = call(combine_body, [(FIELD, BF16)] * 8, [], 10, 1 << 20, place, mine, got)
-    pieces_one = [sends[0]]
-    for k in range(1, 8):
-        perm = [(n, (n // 2 + k // 2) % 4 * 2 + (n + k) % 2) for n in range(8)]
-        pieces_one.append(lax.ppermute(sends[k], XY, perm))
+    split_one = split_kernel(place, rows_one)
+    pieces_one = input_partial(place, hidden_grad, split_one)
     other_two = swap(own_two, "core")
     grad_two = kernel_grad(place, cot, own_two, other_two)
     out_one = reduce_clips(place, grad_one)
@@ -308,7 +312,7 @@
         place, own_two, other_two, rows_two, x_in,
     )
     (in_grad,) = call(
-        functools.partial(pull_body, 8, True), [(FIELD, F32)], [(FIELD, F32)] * 2, 6, 1 << 20,
+        functools.partial(pull_body, True), [(FIELD, F32)], [(FIELD, F32)] * 2, 6, 1 << 20,
         x_in, *pieces_one, cot,
     )
     return whole(block_out), whole(in_grad), out_one, out_two

time: 218 us -> 214 us (0.982)
  waiting for transfers between devices: 83.6 us -> 66.5 us
  starting transfers between devices: 51.5 us -> 61.1 us
  local copies, waits for them, and re-layouts: 7.21 us -> 13.8 us
    all_to_all x6 -> x5, waiting for transfers between devices: 52 us -> 24.4 us  [exchange(): return lax.all_to_all(value, axes, 0, 0, tiled=True)]
    ppermute x7 -> x14, starting transfers between devices: 14.3 us -> 28.9 us  [input_partial(): pieces.append(lax.ppermute(sends[k], XY, perm))]
    ppermute x8 -> x10, waiting for transfers between devices: 18.6 us -> 24.9 us  [swap(): return lax.ppermute(value, axis, SWAP)]
    all_to_all x6 -> x5, starting transfers between devices: 33.7 us -> 27.5 us  [exchange(): return lax.all_to_all(value, axes, 0, 0, tiled=True)]
    unnamed x26 -> x34, local copies, waits for them, and re-layouts: 2.53 us -> 8.48 us
    ppermute x7 -> x14, waiting for transfers between devices: 13 us -> 17.1 us  [input_partial(): pieces.append(lax.ppermute(sends[k], XY, perm))]
    select_n x0 -> x1, other arithmetic: none -> 2.57 us  [split_kernel(): away = jnp.where(first, blocks[:, 1], blocks[:, 0]).reshape(256, 864)]
    transpose x0 -> x2, local copies, waits for them, and re-layouts: none -> 2.56 us  [split_kernel(): blocks = rows.T.reshape(8, 2, 32, 864)]
  transfers between devices with their start and end apart: 21 -> 29, of which waited for: 12 -> 19; matrix products, arithmetic and copies ran while one was open for 4% -> 4% of each run, Pallas kernels for 20% -> 16%
where the time goes in v1:
time: 214 us; the launch traced here: 213 us
  waiting for transfers between devices  66.5 us (31%)
  starting transfers between devices  61.1 us (29%)
  Pallas kernels  43.5 us (20%)
  blocking collectives  22.5 us (11%)
  local copies, waits for them, and re-layouts  13.8 us (6%)
  other arithmetic  4.35 us (2%)
    pallas_call x13, Pallas kernels, call(): pl.pallas_call(body, out_shape=tuple((jax.ShapeDtypeStruct(*o) for o in o...  43.5 us
    ppermute x14, starting transfers between devices, input_partial(): pieces.append(lax.ppermute(sends[k], XY, perm))  28.9 us
    all_to_all x5, starting transfers between devices, exchange(): return lax.all_to_all(value, axes, 0, 0, tiled=True)  27.5 us
    ppermute x10, waiting for transfers between devices, swap(): return lax.ppermute(value, axis, SWAP)  24.9 us
    all_to_all x5, waiting for transfers between devices, exchange(): return lax.all_to_all(value, axes, 0, 0, tiled=True)  24.4 us
    all_to_all x1, blocking collectives, exchange(): return lax.all_to_all(value, axes, 0, 0, tiled=True)  22.5 us
    ppermute x14, waiting for transfers between devices, input_partial(): pieces.append(lax.ppermute(sends[k], XY, perm))  17.1 us
    unnamed x34, local copies, waits for them, and re-layouts  8.48 us
  transfers between devices with their start and end apart: 29, of which 19 were waited for; matrix products, arithmetic and copies ran while one was open for 4% of the time, Pallas kernels for 16%

profile of v1, /device:TPU:2, one launch (start us, length us, event | category | flops | bytes accessed | tf_op | source)
XLA Modules:
  0.0 212.7 jit_solution(11942735934138158032)
XLA Ops:
  0.6 1.0 copy.16
  2.0 22.5 %all_to_all.30.refs_1_.own_ref = bf16[8,16,32,128]{3,2,1,0:T(8,128)(2,1)S(1)} all-to-all(bf16[8,16,32,128]{3,2,1,0:T(8,128)(2,1)S(1)} %shard_map.75), channel_id=1, replica_groups=mesh['yl'=2,'z'=8,'x'=4,'yh'=2,'core'=2] {'x','yh'}, dimensions={0} | all-to-all | bytes 2097152 | tf_op jit(solution)/shard_map/all_to_all | solution.py:238
  24.6 1.3 copy.19
  25.9 1.3 copy.20
  27.3 6.3 %shard_map.76 = (f32[16,32,128]{2,1,0:T(8,128)S(1)}, bf16[8,16,32,128]{3,2,1,0:T(8,128)(2,1)}) custom-call(s32[3]{0:T(128)S(1)} %pad_add_fusion.refs_0_.place_ref, bf16[8,16,32,128]{3,2,1,0:T(8,128)(2,1)S(1)} %all_to_all.30.refs_1_.own_ref, bf16[8,16,32,128]{3,2,1,0:T(8,128)(2,1)} %collective-permute-done.refs_2_.other_ref, bf16[864,512]{1,0:T(8,128)(2,1)S(1)} %bitcast.46), custom_call_target="tpu_custom_call" | custom-call | flops 1811939328 | bytes 4194304 | tf_op jit(solution)/shard_map/pallas_call | solution.py:23
  33.7 5.2 %all-to-all-start.1 = ((bf16[8,16,32,128]{3,2,1,0:T(8,128)(2,1)}), bf16[8,16,32,128]{3,2,1,0:T(8,128)(2,1)S(1)}, u32[]{:S(2)}, u32[]{:S(2)}) async-start(bf16[8,16,32,128]{3,2,1,0:T(8,128)(2,1)} %get-tuple-element.26), calls=%async_computation.1 | async-start | bytes 2097152 | tf_op jit(solution)/shard_map/all_to_all | solution.py:238
  38.9 2.6 %broadcast_select_fusion = (bf16[8,1,32,864]{3,2,1,0:T(8,128)(2,1)}, bf16[8,1,32,864]{3,2,1,0:T(8,128)(2,1)}, bf16[8,1,32,864]{3,2,1,0:T(8,128)(2,1)S(1)}, bf16[8,1,32,864]{3,2,1,0:T(8,128)(2,1)S(1)}) fusion(pred[]{:T(512)S(6)} %eq.4, bf16[8,2,32,864]{3,2,1,0:T(8,128)(2,1)} %bitcast.57, bf16[8,2,32,864]{3,2,1,0:T(8,128)(2,1)} %bitcast.56), kind=kLoop, calls=%fused_computation.2 | loop fusion | flops 884736 | bytes 3538945 | tf_op jit(solution)/shard_map/jit(_where)/select_n | solution.py:249
  42.1 1.4 collective-permute-done.2.other_ref
  43.4 5.9 %shard_map.78 = (bf16[16,32,128]{2,1,0:T(8,128)(2,1)S(1)}, bf16[16,32,128]{2,1,0:T(8,128)(2,1)}, bf16[16,32,128]{2,1,0:T(8,128)(2,1)}, bf16[16,32,128]{2,1,0:T(8...) custom-call(s32[3]{0:T(128)S(1)} %pad_add_fusion.refs_0_.place_ref, ...), custom_call_target="tpu_custom_call" | custom-call | flops 1811939328 | bytes 4194304 | tf_op jit(solution)/shard_map/pallas_call | solution.py:23
  52.6 3.0 %collective-permute-start.4 = (bf16[16,32,128]{2,1,0:T(8,128)(2,1)}, bf16[16,32,128]{2,1,0:T(8,128)(2,1)}, u32[]{:S(2)}, u32[]{:S(2)}) collective-permute-start(bf16[16,32,128]{2,1,0:T(8,128)(2,1)} %get-tuple-element.29), channel_id=1, source_target_pairs={{0,2},{2,0},{4,6},{6,4},{8,10},{10,8},{12,14},{14,12},{1,3},{3,1},... | collective-permute-start | bytes 393224 | tf_op jit(solution)/shard_map/ppermute | solution.py:260
  55.6 1.5 collective-permute-start.5
  57.1 1.2 collective-permute-start.6
  58.2 1.4 collective-permute-start.7
  60.0 4.5 %collective-permute-start.8 = (bf16[16,32,128]{2,1,0:T(8,128)(2,1)}, bf16[16,32,128]{2,1,0:T(8,128)(2,1)S(1)}, u32[]{:S(2)}, u32[]{:S(2)}) collective-permute-start(bf16[16,32,128]{2,1,0:T(8,128)(2,1)} %copy-done.11), channel_id=1, source_target_pairs={{0,10},{2,8},{4,14},{6,12},{8,2},{10,0},{12,6},{14,4},{1,11},{3,9}... | collective-permute-start | bytes 393224 | tf_op jit(solution)/shard_map/ppermute | solution.py:260
  64.5 1.4 collective-permute-start.9
  65.9 2.4 %collective-permute-start.10 = (bf16[16,32,128]{2,1,0:T(8,128)(2,1)}, bf16[16,32,128]{2,1,0:T(8,128)(2,1)S(1)}, u32[]{:S(2)}, u32[]{:S(2)}) collective-permute-start(bf16[16,32,128]{2,1,0:T(8,128)(2,1)} %copy-done.8), channel_id=1, source_target_pairs={{0,14},{2,12},{4,2},{6,0},{8,6},{10,4},{12,10},{14,8},{1,15},{3,13... | collective-permute-start | bytes 393224 | tf_op jit(solution)/shard_map/ppermute | solution.py:260
  68.3 3.3 %collective-permute-done.8.refs_6_ = bf16[16,32,128]{2,1,0:T(8,128)(2,1)S(1)} collective-permute-done((bf16[16,32,128]{2,1,0:T(8,128)(2,1)}, bf16[16,32,128]{2,1,0:T(8,128)(2,1)S(1)}, u32[]{:S(2)}, u32[]{:S(2)}) %collective-permute-start.8) | collective-permute-done | bytes 131104 | tf_op jit(solution)/shard_map/ppermute | solution.py:260
  72.3 4.4 %collective-permute-done.10.refs_8_ = bf16[16,32,128]{2,1,0:T(8,128)(2,1)S(1)} collective-permute-done((bf16[16,32,128]{2,1,0:T(8,128)(2,1)}, bf16[16,32,128]{2,1,0:T(8,128)(2,1)S(1)}, u32[]{:S(2)}, u32[]{:S(2)}) %collective-permute-start.10) | collective-permute-done | bytes 131104 | tf_op jit(solution)/shard_map/ppermute | solution.py:260
  76.7 0.9 copy-done.6
  77.6 1.6 shard_map.79.field_ref
  79.3 5.9 %shard_map.82 = (f32[8,27,8,128]{3,2,1,0:T(8,128)S(1)}, bf16[8,27,8,128]{3,2,1,0:T(8,128)(2,1)S(1)}) custom-call(s32[3]{0:T(128)S(1)} %pad_add_fusion.refs_0_.place_ref, bf16[16,32,128]{2,1,0:T(8,128)(2,1)S(1)} %shard_map.79.field_ref, bf16[8,16,32,128]{3,2,1,0:T(8,128)(2,1)S(1)} %all_to_all.30.refs_1_.own_ref, ...), custom_call_target="tpu_custom_call" | custom-call | flops 1811939328 | bytes 4194304 | tf_op jit(solution)/shard_map/pallas_call | solution.py:23
  86.0 11.4 %collective-permute-done.20 = bf16[8,27,8,128]{3,2,1,0:T(8,128)(2,1)S(1)} collective-permute-done((bf16[8,27,8,128]{3,2,1,0:T(8,128)(2,1)S(1)}, bf16[8,27,8,128]{3,2,1,0:T(8,128)(2,1)S(1)}, u32[]{:S(2)}, u32[]{:S(2)}) %collective-permute-start.20) | collective-permute-done | bytes 442400 | tf_op jit(solution)/shard_map/ppermute | solution.py:242
  98.2 8.5 %all-to-all-start.2 = ((bf16[8,27,8,128]{3,2,1,0:T(8,128)(2,1)}), bf16[8,27,8,128]{3,2,1,0:T(8,128)(2,1)S(1)}, u32[]{:S(2)}, u32[]{:S(2)}) async-start(bf16[8,27,8,128]{3,2,1,0:T(8,128)(2,1)} %add_convert_fusion.1), calls=%async_computation.2 | async-start | bytes 884736 | tf_op jit(solution)/shard_map/all_to_all | solution.py:238
  106.8 5.9 %shard_map.85 = (f32[8,27,8,128]{3,2,1,0:T(8,128)S(1)}, bf16[8,27,8,128]{3,2,1,0:T(8,128)(2,1)S(1)}) custom-call(s32[3]{0:T(128)S(1)} %pad_add_fusion.refs_0_.place_ref, bf16[16,32,128]{2,1,0:T(8,128)(2,1)S(1)} %bitcast.51, bf16[8,16,32,128]{3,2,1,0:T(8,128)(2,1)S(1)} %all-to-all-done.1.refs_1_.own_ref, ...), custom_call_target="tpu_custom_call" | custom-call | flops 1811939328 | bytes 4194304 | tf_op jit(solution)/shard_map/pallas_call | solution.py:23
  113.4 10.3 %collective-permute-done.22 = bf16[8,27,8,128]{3,2,1,0:T(8,128)(2,1)S(1)} collective-permute-done((bf16[8,27,8,128]{3,2,1,0:T(8,128)(2,1)S(1)}, bf16[8,27,8,128]{3,2,1,0:T(8,128)(2,1)S(1)}, u32[]{:S(2)}, u32[]{:S(2)}) %collective-permute-start.22) | collective-permute-done | bytes 442400 | tf_op jit(solution)/shard_map/ppermute | solution.py:242
  124.5 6.9 %all-to-all-start.4 = ((bf16[8,27,8,128]{3,2,1,0:T(8,128)(2,1)}), bf16[8,27,8,128]{3,2,1,0:T(8,128)(2,1)S(1)}, u32[]{:S(2)}, u32[]{:S(2)}) async-start(bf16[8,27,8,128]{3,2,1,0:T(8,128)(2,1)} %add_convert_fusion), calls=%async_computation.4 | async-start | bytes 884736 | tf_op jit(solution)/shard_map/all_to_all | solution.py:238
  132.3 12.8 %all-to-all-done.4.pieces_ref = bf16[8,27,8,128]{3,2,1,0:T(8,128)(2,1)S(1)} async-done(((bf16[8,27,8,128]{3,2,1,0:T(8,128)(2,1)}), bf16[8,27,8,128]{3,2,1,0:T(8,128)(2,1)S(1)}, u32[]{:S(2)}, u32[]{:S(2)}) %all-to-all-start.4) | async-done | bytes 442400 | tf_op jit(solution)/shard_map/all_to_all | solution.py:238
  145.1 3.5 %all-to-all-start.3 = ((bf16[8,27,8,128]{3,2,1,0:T(8,128)(2,1)}), bf16[8,27,8,128]{3,2,1,0:T(8,128)(2,1)S(1)}, u32[]{:S(2)}, u32[]{:S(2)}) async-start(bf16[8,27,8,128]{3,2,1,0:T(8,128)(2,1)} %shard_map.83), calls=%async_computation.3 | async-start | bytes 884736 | tf_op jit(solution)/shard_map/all_to_all | solution.py:238
  149.4 11.6 %all-to-all-done.3.full_ref = bf16[8,27,8,128]{3,2,1,0:T(8,128)(2,1)S(1)} async-done(((bf16[8,27,8,128]{3,2,1,0:T(8,128)(2,1)}), bf16[8,27,8,128]{3,2,1,0:T(8,128)(2,1)S(1)}, u32[]{:S(2)}, u32[]{:S(2)}) %all-to-all-start.3) | async-done | bytes 442400 | tf_op jit(solution)/shard_map/all_to_all | solution.py:238
  161.0 3.5 %all-to-all-start.5 = ((bf16[8,27,8,128]{3,2,1,0:T(8,128)(2,1)}), bf16[8,27,8,128]{3,2,1,0:T(8,128)(2,1)S(1)}, u32[]{:S(2)}, u32[]{:S(2)}) async-start(bf16[8,27,8,128]{3,2,1,0:T(8,128)(2,1)} %shard_map.86), calls=%async_computation.5 | async-start | bytes 884736 | tf_op jit(solution)/shard_map/all_to_all | solution.py:238
  165.1 1.5 collective-permute-done.12.far_ref
  166.8 1.0 copy-done.2
  167.8 5.8 %shard_map.80 = (bf16[16,32,128]{2,1,0:T(8,128)(2,1)S(1)}, bf16[16,32,128]{2,1,0:T(8,128)(2,1)}, bf16[16,32,128]{2,1,0:T(8,128)(2,1)S(1)}, bf16[16,32,128]{2,1,0...) custom-call(s32[3]{0:T(128)S(1)} %pad_add_fusion.refs_0_.place_ref, ...), custom_call_target="tpu_custom_call" | custom-call | flops 1811939328 | bytes 4194304 | tf_op jit(solution)/shard_map/pallas_call | solution.py:23
  176.9 1.3 collective-permute-start.13
  178.9 1.3 collective-permute-start.23
  180.3 3.8 %collective-permute-start.15 = (bf16[16,32,128]{2,1,0:T(8,128)(2,1)}, bf16[16,32,128]{2,1,0:T(8,128)(2,1)S(1)}, u32[]{:S(2)}, u32[]{:S(2)}) collective-permute-start(bf16[16,32,128]{2,1,0:T(8,128)(2,1)} %copy-done.14), channel_id=1, source_target_pairs={{0,6},{2,4},{4,10},{6,8},{8,14},{10,12},{12,2},{14,0},{1,7},{3,5},... | collective-permute-start | bytes 393224 | tf_op jit(solution)/shard_map/ppermute | solution.py:260
  184.0 1.0 collective-permute-done.13.refs_2_
  185.0 1.6 collective-permute-start.16
  186.9 3.2 %collective-permute-start.17 = (bf16[16,32,128]{2,1,0:T(8,128)(2,1)}, bf16[16,32,128]{2,1,0:T(8,128)(2,1)S(1)}, u32[]{:S(2)}, u32[]{:S(2)}) collective-permute-start(bf16[16,32,128]{2,1,0:T(8,128)(2,1)} %copy-done.9), channel_id=1, source_target_pairs={{0,10},{2,8},{4,14},{6,12},{8,2},{10,0},{12,6},{14,4},{1,11},{3,9}... | collective-permute-start | bytes 393224 | tf_op jit(solution)/shard_map/ppermute | solution.py:260
  190.1 1.3 collective-permute-done.15.refs_4_
  192.1 1.1 collective-permute-done.16.refs_5_
  193.1 2.9 %collective-permute-start.19 = (bf16[16,32,128]{2,1,0:T(8,128)(2,1)S(1)}, bf16[16,32,128]{2,1,0:T(8,128)(2,1)S(1)}, u32[]{:S(2)}, u32[]{:S(2)}) collective-permute-start(bf16[16,32,128]{2,1,0:T(8,128)(2,1)S(1)} %get-tuple-element.43), channel_id=1, source_target_pairs={{0,14},{2,12},{4,2},{6,0},{8,6},{10,4},{12,10},{14,8},{1,15},{3,13... | collective-permute-start | bytes 393224 | tf_op jit(solution)/shard_map/ppermute | solution.py:260
  196.0 1.3 collective-permute-done.17.refs_6_
  197.3 1.0 collective-permute-done.18.refs_7_
  198.3 2.5 %collective-permute-done.19.refs_8_ = bf16[16,32,128]{2,1,0:T(8,128)(2,1)S(1)} collective-permute-done((bf16[16,32,128]{2,1,0:T(8,128)(2,1)S(1)}, bf16[16,32,128]{2,1,0:T(8,128)(2,1)S(1)}, u32[]{:S(2)}, u32[]{:S(2)}) %collective-permute-start.19) | collective-permute-done | bytes 131104 | tf_op jit(solution)/shard_map/ppermute | solution.py:260
  202.4 5.0 %shard_map.77 = f32[16,32,128]{2,1,0:T(8,128)S(1)} custom-call(s32[3]{0:T(128)S(1)} %pad_add_fusion.refs_0_.place_ref, bf16[8,16,32,128]{3,2,1,0:T(8,128)(2,1)S(1)} %all-to-all-done.1.refs_1_.own_ref, bf16[8,16,32,128]{3,2,1,0:T(8,128)(2,1)} %collective-permute-done.1.refs_2_.other_ref, bf16[864,512]{1,0:T(8,128)(2,1)S(1)} %bitcast.48, ...), custom_call_target="tpu_custom_call" | custom-call | flops 1811939328 | bytes 4194304 | tf_op jit(solution)/shard_map/pallas_call | solution.py:23
  208.2 2.5 %shard_map.84 = f32[27,32,512]{2,1,0:T(8,128)} custom-call(s32[3]{0:T(128)S(1)} %pad_add_fusion.refs_0_.place_ref, bf16[8,27,8,128]{3,2,1,0:T(8,128)(2,1)S(1)} %all-to-all-done.3.full_ref, bf16[8,27,8,128]{3,2,1,0:T(8,128)(2,1)} %collective-permute-done.21.other_ref), custom_call_target="tpu_custom_call" | custom-call | flops 1048576 | bytes 4194304 | tf_op jit(solution)/shard_map/pallas_call | solution.py:23
  210.7 2.0 shard_map.87
  (68 shorter events, 18.6 us)
Async XLA Ops:
  0.6 23.9 %copy-start.1 = (bf16[32,27,512]{2,0,1:T(8,128)(2,1)S(1)}, bf16[32,27,512]{2,0,1:T(8,128)(2,1)}, u32[]{:S(2)}) copy-start(bf16[32,27,512]{2,0,1:T(8,128)(2,1)} %param.6) | copy-start | bytes 2654212
  2.0 23.8 %copy-start = (bf16[32,27,512]{2,0,1:T(8,128)(2,1)S(1)}, bf16[32,27,512]{2,0,1:T(8,128)(2,1)}, u32[]{:S(2)}) copy-start(bf16[32,27,512]{2,0,1:T(8,128)(2,1)} %param.5) | copy-start | bytes 2654212
  24.6 2.8 %collective-permute-start = (bf16[8,16,32,128]{3,2,1,0:T(8,128)(2,1)S(1)}, bf16[8,16,32,128]{3,2,1,0:T(8,128)(2,1)}, u32[]{:S(2)}, u32[]{:S(2)}) collective-permute-start(bf16[8,16,32,128]{3,2,1,0:T(8,128)(2,1)S(1)} %all_to_all.30.refs_1_.own_ref), channel_id=1, source_target_pairs={{0,1},{1,0},{2,3},{3,2},{4,5},{5,4},{6,7},{7,6},{8,9},{9,8},{10,11... | collective-permute-start | bytes 3145736 | tf_op jit(solution)/shard_map/ppermute | solution.py:242
  33.7 24.5 %all-to-all-start.1 = ((bf16[8,16,32,128]{3,2,1,0:T(8,128)(2,1)}), bf16[8,16,32,128]{3,2,1,0:T(8,128)(2,1)S(1)}, u32[]{:S(2)}, u32[]{:S(2)}) async-start(bf16[8,16,32,128]{3,2,1,0:T(8,128)(2,1)} %get-tuple-element.26), calls=%async_computation.1 | async-start | bytes 2097152 | tf_op jit(solution)/shard_map/all_to_all | solution.py:238
  38.9 2.7 %copy-start.16 = (bf16[1,32,4,4,128]{4,3,2,1,0:T(4,128)(2,1)S(1)}, bf16[1,32,4,4,128]{4,3,2,1,0:T(4,128)(2,1)}, u32[]{:S(2)}) copy-start(bf16[1,32,4,4,128]{4,3,2,1,0:T(4,128)(2,1)} %param.7) | copy-start | bytes 393220
  41.4 2.0 collective-permute-start.3
  41.6 1.8 collective-permute-start.2
  49.3 0.6 copy-start.5
  50.0 0.7 copy-start.8
  50.6 0.7 copy-start.10
  51.3 0.7 copy-start.11
  52.0 0.7 copy-start.13
  52.6 7.4 %collective-permute-start.4 = (bf16[16,32,128]{2,1,0:T(8,128)(2,1)}, bf16[16,32,128]{2,1,0:T(8,128)(2,1)}, u32[]{:S(2)}, u32[]{:S(2)}) collective-permute-start(bf16[16,32,128]{2,1,0:T(8,128)(2,1)} %get-tuple-element.29), channel_id=1, source_target_pairs={{0,2},{2,0},{4,6},{6,4},{8,10},{10,8},{12,14},{14,12},{1,3},{3,1},... | collective-permute-start | bytes 393224 | tf_op jit(solution)/shard_map/ppermute | solution.py:260
  55.6 8.9 %collective-permute-start.5 = (bf16[16,32,128]{2,1,0:T(8,128)(2,1)}, bf16[16,32,128]{2,1,0:T(8,128)(2,1)}, u32[]{:S(2)}, u32[]{:S(2)}) collective-permute-start(bf16[16,32,128]{2,1,0:T(8,128)(2,1)} %get-tuple-element.30), channel_id=1, source_target_pairs={{0,4},{2,6},{4,8},{6,10},{8,12},{10,14},{12,0},{14,2},{1,5},{3,7},... | collective-permute-start | bytes 393224 | tf_op jit(solution)/shard_map/ppermute | solution.py:260
  57.1 8.9 %collective-permute-start.6 = (bf16[16,32,128]{2,1,0:T(8,128)(2,1)}, bf16[16,32,128]{2,1,0:T(8,128)(2,1)}, u32[]{:S(2)}, u32[]{:S(2)}) collective-permute-start(bf16[16,32,128]{2,1,0:T(8,128)(2,1)} %get-tuple-element.31), channel_id=1, source_target_pairs={{0,6},{2,4},{4,10},{6,8},{8,14},{10,12},{12,2},{14,0},{1,7},{3,5},... | collective-permute-start | bytes 393224 | tf_op jit(solution)/shard_map/ppermute | solution.py:260
  58.2 48.5 %collective-permute-start.1 = (bf16[8,16,32,128]{3,2,1,0:T(8,128)(2,1)S(1)}, bf16[8,16,32,128]{3,2,1,0:T(8,128)(2,1)}, u32[]{:S(2)}, u32[]{:S(2)}) collective-permute-start(bf16[8,16,32,128]{3,2,1,0:T(8,128)(2,1)S(1)} %all-to-all-done.1.refs_1_.own_ref), channel_id=1, source_target_pairs={{0,1},{1,0},{2,3},{3,2},{4,5},{5,4},{6,7},{7,6},{8,9},{9,8},{10,11... | collective-permute-start | bytes 3145736 | tf_op jit(solution)/shard_map/ppermute | solution.py:242
  58.2 10.1 %collective-permute-start.7 = (bf16[16,32,128]{2,1,0:T(8,128)(2,1)}, bf16[16,32,128]{2,1,0:T(8,128)(2,1)S(1)}, u32[]{:S(2)}, u32[]{:S(2)}) collective-permute-start(bf16[16,32,128]{2,1,0:T(8,128)(2,1)} %copy-done.13), channel_id=1, source_target_pairs={{0,8},{2,10},{4,12},{6,14},{8,0},{10,2},{12,4},{14,6},{1,9},{3,11}... | collective-permute-start | bytes 393224 | tf_op jit(solution)/shard_map/ppermute | solution.py:260
  60.0 11.6 %collective-permute-start.8 = (bf16[16,32,128]{2,1,0:T(8,128)(2,1)}, bf16[16,32,128]{2,1,0:T(8,128)(2,1)S(1)}, u32[]{:S(2)}, u32[]{:S(2)}) collective-permute-start(bf16[16,32,128]{2,1,0:T(8,128)(2,1)} %copy-done.11), channel_id=1, source_target_pairs={{0,10},{2,8},{4,14},{6,12},{8,2},{10,0},{12,6},{14,4},{1,11},{3,9}... | collective-permute-start | bytes 393224 | tf_op jit(solution)/shard_map/ppermute | solution.py:260
  64.5 7.9 %collective-permute-start.9 = (bf16[16,32,128]{2,1,0:T(8,128)(2,1)}, bf16[16,32,128]{2,1,0:T(8,128)(2,1)S(1)}, u32[]{:S(2)}, u32[]{:S(2)}) collective-permute-start(bf16[16,32,128]{2,1,0:T(8,128)(2,1)} %copy-done.10), channel_id=1, source_target_pairs={{0,12},{2,14},{4,0},{6,2},{8,4},{10,6},{12,8},{14,10},{1,13},{3,15... | collective-permute-start | bytes 393224 | tf_op jit(solution)/shard_map/ppermute | solution.py:260
  65.9 10.8 %collective-permute-start.10 = (bf16[16,32,128]{2,1,0:T(8,128)(2,1)}, bf16[16,32,128]{2,1,0:T(8,128)(2,1)S(1)}, u32[]{:S(2)}, u32[]{:S(2)}) collective-permute-start(bf16[16,32,128]{2,1,0:T(8,128)(2,1)} %copy-done.8), channel_id=1, source_target_pairs={{0,14},{2,12},{4,2},{6,0},{8,6},{10,4},{12,10},{14,8},{1,15},{3,13... | collective-permute-start | bytes 393224 | tf_op jit(solution)/shard_map/ppermute | solution.py:260
  76.7 0.9 copy-start.6
  79.3 6.0 %copy-start.3 = (bf16[16,32,128]{2,1,0:T(8,128)(2,1)}, bf16[16,32,128]{2,1,0:T(8,128)(2,1)S(1)}, u32[]{:S(2)}) copy-start(bf16[16,32,128]{2,1,0:T(8,128)(2,1)S(1)} %shard_map.79.field_ref) | copy-start | bytes 393220
  85.2 12.2 %collective-permute-start.20 = (bf16[8,27,8,128]{3,2,1,0:T(8,128)(2,1)S(1)}, bf16[8,27,8,128]{3,2,1,0:T(8,128)(2,1)S(1)}, u32[]{:S(2)}, u32[]{:S(2)}) collective-permute-start(bf16[8,27,8,128]{3,2,1,0:T(8,128)(2,1)S(1)} %get-tuple-element.45), channel_id=1, source_target_pairs={{0,128},{128,0},{1,129},{129,1},{2,130},{130,2},{3,131},{131,3},{4... | collective-permute-start | bytes 1327112 | tf_op jit(solution)/shard_map/ppermute | solution.py:242
  98.2 26.3 %all-to-all-start.2 = ((bf16[8,27,8,128]{3,2,1,0:T(8,128)(2,1)}), bf16[8,27,8,128]{3,2,1,0:T(8,128)(2,1)S(1)}, u32[]{:S(2)}, u32[]{:S(2)}) async-start(bf16[8,27,8,128]{3,2,1,0:T(8,128)(2,1)} %add_convert_fusion.1), calls=%async_computation.2 | async-start | bytes 884736 | tf_op jit(solution)/shard_map/all_to_all | solution.py:238
  112.6 11.1 %collective-permute-start.22 = (bf16[8,27,8,128]{3,2,1,0:T(8,128)(2,1)S(1)}, bf16[8,27,8,128]{3,2,1,0:T(8,128)(2,1)S(1)}, u32[]{:S(2)}, u32[]{:S(2)}) collective-permute-start(bf16[8,27,8,128]{3,2,1,0:T(8,128)(2,1)S(1)} %get-tuple-element.47), channel_id=1, source_target_pairs={{0,128},{128,0},{1,129},{129,1},{2,130},{130,2},{3,131},{131,3},{4... | collective-permute-start | bytes 1327112 | tf_op jit(solution)/shard_map/ppermute | solution.py:242
  124.5 20.6 %all-to-all-start.4 = ((bf16[8,27,8,128]{3,2,1,0:T(8,128)(2,1)}), bf16[8,27,8,128]{3,2,1,0:T(8,128)(2,1)S(1)}, u32[]{:S(2)}, u32[]{:S(2)}) async-start(bf16[8,27,8,128]{3,2,1,0:T(8,128)(2,1)} %add_convert_fusion), calls=%async_computation.4 | async-start | bytes 884736 | tf_op jit(solution)/shard_map/all_to_all | solution.py:238
  131.5 33.1 %copy-start.4 = (bf16[16,32,128]{2,1,0:T(8,128)(2,1)S(1)}, bf16[16,32,128]{2,1,0:T(8,128)(2,1)}, u32[]{:S(2)}) copy-start(bf16[16,32,128]{2,1,0:T(8,128)(2,1)} %copy-done.3) | copy-start | bytes 393220
  145.1 15.9 %all-to-all-start.3 = ((bf16[8,27,8,128]{3,2,1,0:T(8,128)(2,1)}), bf16[8,27,8,128]{3,2,1,0:T(8,128)(2,1)S(1)}, u32[]{:S(2)}, u32[]{:S(2)}) async-start(bf16[8,27,8,128]{3,2,1,0:T(8,128)(2,1)} %shard_map.83), calls=%async_computation.3 | async-start | bytes 884736 | tf_op jit(solution)/shard_map/all_to_all | solution.py:238
  161.0 17.9 %all-to-all-start.5 = ((bf16[8,27,8,128]{3,2,1,0:T(8,128)(2,1)}), bf16[8,27,8,128]{3,2,1,0:T(8,128)(2,1)S(1)}, u32[]{:S(2)}, u32[]{:S(2)}) async-start(bf16[8,27,8,128]{3,2,1,0:T(8,128)(2,1)} %shard_map.86), calls=%async_computation.5 | async-start | bytes 884736 | tf_op jit(solution)/shard_map/all_to_all | solution.py:238
  164.5 2.1 collective-permute-start.12
  164.6 2.2 %collective-permute-start.11 = (bf16[16,32,128]{2,1,0:T(8,128)(2,1)S(1)}, bf16[16,32,128]{2,1,0:T(8,128)(2,1)S(1)}, u32[]{:S(2)}, u32[]{:S(2)}) collective-permute-start(bf16[16,32,128]{2,1,0:T(8,128)(2,1)S(1)} %copy-done.4), channel_id=1, source_target_pairs={{0,1},{1,0},{2,3},{3,2},{4,5},{5,4},{6,7},{7,6},{8,9},{9,8},{10,11... | collective-permute-start | bytes 393224 | tf_op jit(solution)/shard_map/ppermute | solution.py:242
  166.8 1.0 copy-start.2
  173.7 0.7 copy-start.7
  174.3 0.6 copy-start.9
  175.0 0.6 copy-start.12
  175.6 0.7 copy-start.14
  176.3 0.7 copy-start.15
  176.9 8.1 %collective-permute-start.13 = (bf16[16,32,128]{2,1,0:T(8,128)(2,1)}, bf16[16,32,128]{2,1,0:T(8,128)(2,1)S(1)}, u32[]{:S(2)}, u32[]{:S(2)}) collective-permute-start(bf16[16,32,128]{2,1,0:T(8,128)(2,1)} %get-tuple-element.37), channel_id=1, source_target_pairs={{0,2},{2,0},{4,6},{6,4},{8,10},{10,8},{12,14},{14,12},{1,3},{3,1},... | collective-permute-start | bytes 393224 | tf_op jit(solution)/shard_map/ppermute | solution.py:260
  178.2 30.0 %collective-permute-start.21 = (bf16[8,27,8,128]{3,2,1,0:T(8,128)(2,1)S(1)}, bf16[8,27,8,128]{3,2,1,0:T(8,128)(2,1)}, u32[]{:S(2)}, u32[]{:S(2)}) collective-permute-start(bf16[8,27,8,128]{3,2,1,0:T(8,128)(2,1)S(1)} %all-to-all-done.3.full_ref), channel_id=1, source_target_pairs={{0,128},{128,0},{1,129},{129,1},{2,130},{130,2},{3,131},{131,3},{4... | collective-permute-start | bytes 1327112 | tf_op jit(solution)/shard_map/ppermute | solution.py:242
  178.9 31.8 %collective-permute-start.23 = (bf16[8,27,8,128]{3,2,1,0:T(8,128)(2,1)S(1)}, bf16[8,27,8,128]{3,2,1,0:T(8,128)(2,1)S(1)}, u32[]{:S(2)}, u32[]{:S(2)}) collective-permute-start(bf16[8,27,8,128]{3,2,1,0:T(8,128)(2,1)S(1)} %all-to-all-done.5.full_ref), channel_id=1, source_target_pairs={{0,128},{128,0},{1,129},{129,1},{2,130},{130,2},{3,131},{131,3},{4... | collective-permute-start | bytes 1327112 | tf_op jit(solution)/shard_map/ppermute | solution.py:242
  180.3 6.6 %collective-permute-start.14 = (bf16[16,32,128]{2,1,0:T(8,128)(2,1)}, bf16[16,32,128]{2,1,0:T(8,128)(2,1)S(1)}, u32[]{:S(2)}, u32[]{:S(2)}) collective-permute-start(bf16[16,32,128]{2,1,0:T(8,128)(2,1)} %copy-done.15), channel_id=1, source_target_pairs={{0,4},{2,6},{4,8},{6,10},{8,12},{10,14},{12,0},{14,2},{1,5},{3,7},... | collective-permute-start | bytes 393224 | tf_op jit(solution)/shard_map/ppermute | solution.py:260
  180.3 11.0 %collective-permute-start.15 = (bf16[16,32,128]{2,1,0:T(8,128)(2,1)}, bf16[16,32,128]{2,1,0:T(8,128)(2,1)S(1)}, u32[]{:S(2)}, u32[]{:S(2)}) collective-permute-start(bf16[16,32,128]{2,1,0:T(8,128)(2,1)} %copy-done.14), channel_id=1, source_target_pairs={{0,6},{2,4},{4,10},{6,8},{8,14},{10,12},{12,2},{14,0},{1,7},{3,5},... | collective-permute-start | bytes 393224 | tf_op jit(solution)/shard_map/ppermute | solution.py:260
  185.0 8.1 %collective-permute-start.16 = (bf16[16,32,128]{2,1,0:T(8,128)(2,1)}, bf16[16,32,128]{2,1,0:T(8,128)(2,1)S(1)}, u32[]{:S(2)}, u32[]{:S(2)}) collective-permute-start(bf16[16,32,128]{2,1,0:T(8,128)(2,1)} %copy-done.12), channel_id=1, source_target_pairs={{0,8},{2,10},{4,12},{6,14},{8,0},{10,2},{12,4},{14,6},{1,9},{3,11}... | collective-permute-start | bytes 393224 | tf_op jit(solution)/shard_map/ppermute | solution.py:260
  186.9 10.5 %collective-permute-start.17 = (bf16[16,32,128]{2,1,0:T(8,128)(2,1)}, bf16[16,32,128]{2,1,0:T(8,128)(2,1)S(1)}, u32[]{:S(2)}, u32[]{:S(2)}) collective-permute-start(bf16[16,32,128]{2,1,0:T(8,128)(2,1)} %copy-done.9), channel_id=1, source_target_pairs={{0,10},{2,8},{4,14},{6,12},{8,2},{10,0},{12,6},{14,4},{1,11},{3,9}... | collective-permute-start | bytes 393224 | tf_op jit(solution)/shard_map/ppermute | solution.py:260
  191.3 7.0 %collective-permute-start.18 = (bf16[16,32,128]{2,1,0:T(8,128)(2,1)}, bf16[16,32,128]{2,1,0:T(8,128)(2,1)S(1)}, u32[]{:S(2)}, u32[]{:S(2)}) collective-permute-start(bf16[16,32,128]{2,1,0:T(8,128)(2,1)} %copy-done.7), channel_id=1, source_target_pairs={{0,12},{2,14},{4,0},{6,2},{8,4},{10,6},{12,8},{14,10},{1,13},{3,15... | collective-permute-start | bytes 393224 | tf_op jit(solution)/shard_map/ppermute | solution.py:260
  193.1 7.8 %collective-permute-start.19 = (bf16[16,32,128]{2,1,0:T(8,128)(2,1)S(1)}, bf16[16,32,128]{2,1,0:T(8,128)(2,1)S(1)}, u32[]{:S(2)}, u32[]{:S(2)}) collective-permute-start(bf16[16,32,128]{2,1,0:T(8,128)(2,1)S(1)} %get-tuple-element.43), channel_id=1, source_target_pairs={{0,14},{2,12},{4,2},{6,0},{8,6},{10,4},{12,10},{14,8},{1,15},{3,13... | collective-permute-start | bytes 393224 | tf_op jit(solution)/shard_map/ppermute | solution.py:260

commit v2 on v1

--- a/solution.py
+++ b/solution.py
@@ -107,11 +107,8 @@
     lane = lax.broadcasted_iota(jnp.int32, (32, 128), 1)
     assemble(core_ref, own_ref, other_ref, acts)
 
-    def step(pair, carry):
+    for pair in range(8):
         products[pair] = jnp.dot(kernel_ref[...], acts[pair], preferred_element_type=F32)
-        return carry
-
-    lax.fori_loop(0, 8, step, 0)
 
     def output(cell):
         sums = []
@@ -162,20 +159,21 @@
 
 
 def partial_body(place_ref, field_ref, other_ref, kernel_ref, far_ref, *refs):
-    out_refs, (shifted, columns, far_columns, result) = refs[:8], refs[8:]
+    out_refs, (shifted, columns, far_columns, result, near, far) = refs[:8], refs[8:]
+    core = place_ref[0]
+    for n in range(8):
+        start = pl.multiple_of(n * 64 + core * 32, 32)
+        near[n * 32 : n * 32 + 32] = kernel_ref[pl.ds(start, 32)]
+        far[n * 32 : n * 32 + 32] = far_ref[pl.ds(start, 32)]
     spread(field_ref, shifted, columns)
     spread(other_ref, shifted, far_columns)
-
-    def step(pair, carry):
-        out = jnp.dot(kernel_ref[...], columns[pair], preferred_element_type=F32)
-        out = out + jnp.dot(far_ref[...], far_columns[pair], preferred_element_type=F32)
+    for pair in range(8):
+        out = jnp.dot(near[...], columns[pair], preferred_element_type=F32)
+        out = out + jnp.dot(far[...], far_columns[pair], preferred_element_type=F32)
         for half in range(2):
             for n in range(8):
                 part = out[n * 32 : n * 32 + 32, half * 128 : half * 128 + 128]
                 result[n, pair * 2 + half] = part.astype(BF16)
-        return carry
-
-    lax.fori_loop(0, 8, step, 0)
     here = place_ref[2]
     for k in range(8):
         n = lax.rem(here // 2 + k // 2, 4) * 2 + lax.rem(here + k, 2)
@@ -186,16 +184,14 @@
     spread(field_ref, shifted, columns)
     assemble(place_ref, own_ref, other_ref, acts)
     first = place_ref[1] == 0
-
-    def step(pair, carry):
-        term = lax.dot_general(
-            columns[pair], acts[pair], (((1,), (1,)), ((), ())), preferred_element_type=F32
-        )
-        total[...] += term
-        return carry
-
-    total[...] = jnp.zeros_like(total)
-    lax.fori_loop(0, 8, step, 0)
+    for left in (0, 256):
+        term = None
+        for pair in range(8):
+            more = lax.dot_general(
+                columns[pair], acts[pair, left : left + 256], (((1,), (1,)), ((), ())), preferred_element_type=F32
+            )
+            term = more if term is None else term + more
+        total[:, left : left + 256] = term
     for piece in range(8):
         left = piece % 4 * 128
         for k in range(27):
@@ -206,13 +202,32 @@
             theirs_ref[piece, k] = jnp.where(first, high, low).astype(BF16)
 
 
-def total_body(pieces_ref, out_ref):
+def join_body(mine_ref, got_ref, out_ref):
+    for n in range(8):
+        for k in range(27):
+            out_ref[n, k] = (mine_ref[n, k] + got_ref[n, k].astype(F32)).astype(BF16)
+
+
+def add_pieces(pieces_ref, row):
+    total = pieces_ref[0, row].astype(F32)
+    for n in range(1, 8):
+        total = total + pieces_ref[n, row].astype(F32)
+    return total.astype(BF16)
+
+
+def middle_body(pieces_ref, mine_ref, got_ref, out_ref):
     for k in range(27):
-        total = pieces_ref[0, k].astype(F32)
-        for n in range(1, 8):
-            total = total + pieces_ref[n, k].astype(F32)
-        value = total.astype(BF16)
+        value = add_pieces(pieces_ref, k)
         for n in range(8):
+            out_ref[n, k] = value
+            out_ref[n, 27 + k] = (mine_ref[n, k] + got_ref[n, k].astype(F32)).astype(BF16)
+
+
+def last_body(both_ref, full_ref, out_ref):
+    for k in range(27):
+        value = add_pieces(both_ref, 27 + k)
+        for n in range(8):
+            full_ref[n, k] = both_ref[n, k]
             out_ref[n, k] = value
 
 
@@ -242,18 +257,11 @@
     return lax.ppermute(value, axis, SWAP)
 
 
-def split_kernel(place, rows):
-    blocks = rows.T.reshape(8, 2, 32, 864)
-    first = place[0] == 0
-    near = jnp.where(first, blocks[:, 0], blocks[:, 1]).reshape(256, 864)
-    away = jnp.where(first, blocks[:, 1], blocks[:, 0]).reshape(256, 864)
-    return near, swap(away, "core")
-
-
-def input_partial(place, field, kernels):
+def input_partial(place, field, rows):
+    far = swap(rows, "core")
     other = swap(field, "core")
-    scratch = COLUMNS + [COLUMNS[1], (WIDE, BF16)]
-    sends = call(partial_body, [(FIELD, BF16)] * 8, scratch, 16, FLOPS, place, field, other, *kernels)
+    scratch = COLUMNS + [COLUMNS[1], (WIDE, BF16), ((256, 864), BF16), ((256, 864), BF16)]
+    sends = call(partial_body, [(FIELD, BF16)] * 8, scratch, 18, FLOPS, place, field, other, rows.T, far.T)
     pieces = [sends[0]]
     for k in range(1, 8):
         perm = [(n, (n // 2 + k // 2) % 4 * 2 + (n + k) % 2) for n in range(8)]
@@ -264,16 +272,21 @@
 def kernel_grad(place, field, own, other):
     scratch = COLUMNS + [ACTS, ((864, 512), F32)]
     mine, theirs = call(grad_body, [(PIECES, F32), (PIECES, BF16)], scratch, 20, FLOPS, place, field, own, other)
-    got = swap(theirs, "yl")
-    return (mine + got.astype(F32)).astype(BF16)
-
-
-def reduce_clips(place, pair):
-    (copies,) = call(total_body, [(PIECES, BF16)], [], 4, 1 << 20, exchange(pair, "z"))
-    full = exchange(copies, "z")
-    other = swap(full, "yl")
-    (out,) = call(finish_body, [((27, 32, 512), F32)], [], 6, 1 << 20, place, full, other)
-    return out.transpose(1, 0, 2)
+    return mine, swap(theirs, "yl")
+
+
+def reduce_clips(place, grad_one, grad_two):
+    (pair,) = call(join_body, [(PIECES, BF16)], [], 8, 1 << 20, *grad_one)
+    pieces = exchange(pair, "z")
+    double = (8, 54, 8, 128)
+    (both,) = call(middle_body, [(double, BF16)], [], 8, 1 << 20, pieces, *grad_two)
+    full_one, copies = call(last_body, [(PIECES, BF16)] * 2, [], 6, 1 << 20, exchange(both, "z"))
+    full_two = exchange(copies, "z")
+    outs = []
+    for full in (full_one, full_two):
+        other = swap(full, "yl")
+        outs += call(finish_body, [((27, 32, 512), F32)], [], 6, 1 << 20, place, full, other)
+    return [out.transpose(1, 0, 2) for out in outs]
 
 
 def shards(block_in, conv_one, conv_two, out_cotangent):
@@ -283,12 +296,12 @@
     core, yl = lax.axis_index("core"), lax.axis_index("yl")
     place = jnp.stack([core, yl, lax.axis_index(XY)]).astype(jnp.int32)
     x_in, cot = cells(block_in), cells(out_cotangent)
-    rows_one, rows_two = rows(conv_one), rows(conv_two)
+    rows_two = rows(conv_two)
+    rows_one = rows(conv_one)
 
     (copies,) = call(act_body, [(WIDE, BF16)], [], 4, 1 << 20, x_in)
     own = exchange(copies, XY)
-    split_two = split_kernel(place, rows_two)
-    pieces_two = input_partial(place, cot, split_two)
+    pieces_two = input_partial(place, cot, rows_two)
     other = swap(own, "core")
     conv_scratch = [ACTS, ((8, 864, 256), F32)]
     hidden, copies_two = call(
@@ -301,12 +314,10 @@
         hidden, *pieces_two,
     )
     grad_one = kernel_grad(place, hidden_grad, own, other)
-    split_one = split_kernel(place, rows_one)
-    pieces_one = input_partial(place, hidden_grad, split_one)
+    pieces_one = input_partial(place, hidden_grad, rows_one)
     other_two = swap(own_two, "core")
     grad_two = kernel_grad(place, cot, own_two, other_two)
-    out_one = reduce_clips(place, grad_one)
-    out_two = reduce_clips(place, grad_two)
+    out_one, out_two = reduce_clips(place, grad_one, grad_two)
     (block_out,) = call(
         functools.partial(conv_body, True), [(FIELD, F32)], conv_scratch, 18, FLOPS,
         place, own_two, other_two, rows_two, x_in,

time: 214 us -> 209 us (0.977)
  Pallas kernels: 43.5 us -> 35.7 us
  waiting for transfers between devices: 66.5 us -> 71.8 us
  other arithmetic: 4.35 us -> 0.08 us
  local copies, waits for them, and re-layouts: 13.8 us -> 18 us
  starting transfers between devices: 61.1 us -> 58 us
    all_to_all x5 -> x4, waiting for transfers between devices: 24.4 us -> 38.6 us  [exchange(): return lax.all_to_all(value, axes, 0, 0, tiled=True)]
    ppermute x10, waiting for transfers between devices: 24.9 us -> 13.2 us  [swap(): return lax.ppermute(value, axis, SWAP)]
    pallas_call x13 -> x14, Pallas kernels: 43.5 us -> 35.7 us  [call(): pl.pallas_call(body, out_shape=tuple((jax.ShapeDtypeStruct(*o) for o in o...]
    ppermute x0 -> x2, local copies, waits for them, and re-layouts: none -> 3.75 us  [swap(): return lax.ppermute(value, axis, SWAP)]
    all_to_all x5 -> x4, starting transfers between devices: 27.5 us -> 24.2 us  [exchange(): return lax.all_to_all(value, axes, 0, 0, tiled=True)]
    ppermute x14, waiting for transfers between devices: 17.1 us -> 20 us  [input_partial(): pieces.append(lax.ppermute(sends[k], XY, perm))]
    select_n x1 -> x0, other arithmetic: 2.57 us -> none  [split_kernel(): away = jnp.where(first, blocks[:, 1], blocks[:, 0]).reshape(256, 864)]
    transpose x2 -> x0, local copies, waits for them, and re-layouts: 2.56 us -> none  [split_kernel(): blocks = rows.T.reshape(8, 2, 32, 864)]
  transfers between devices with their start and end apart: 29 -> 28, of which waited for: 19 -> 17; matrix products, arithmetic and copies ran while one was open for 4% -> 4% of each run, Pallas kernels for 16% -> 14%
where the time goes in v2:
time: 209 us; the launch traced here: 207 us
  waiting for transfers between devices  71.8 us (34%)
  starting transfers between devices  58 us (28%)
  Pallas kernels  35.7 us (17%)
  blocking collectives  22.4 us (11%)
  local copies, waits for them, and re-layouts  18 us (9%)
    all_to_all x4, waiting for transfers between devices, exchange(): return lax.all_to_all(value, axes, 0, 0, tiled=True)  38.6 us
    pallas_call x14, Pallas kernels, call(): pl.pallas_call(body, out_shape=tuple((jax.ShapeDtypeStruct(*o) for o in o...  35.7 us
    ppermute x14, starting transfers between devices, input_partial(): pieces.append(lax.ppermute(sends[k], XY, perm))  29.8 us
    all_to_all x4, starting transfers between devices, exchange(): return lax.all_to_all(value, axes, 0, 0, tiled=True)  24.2 us
    all_to_all x1, blocking collectives, exchange(): return lax.all_to_all(value, axes, 0, 0, tiled=True)  22.4 us
    ppermute x14, waiting for transfers between devices, input_partial(): pieces.append(lax.ppermute(sends[k], XY, perm))  20 us
    ppermute x10, waiting for transfers between devices, swap(): return lax.ppermute(value, axis, SWAP)  13.2 us
    unnamed x36, local copies, waits for them, and re-layouts  9.32 us
  transfers between devices with their start and end apart: 28, of which 17 were waited for; matrix products, arithmetic and copies ran while one was open for 4% of the time, Pallas kernels for 14%

profile of v2, /device:TPU:2, one launch (start us, length us, event | category | flops | bytes accessed | tf_op | source)
XLA Modules:
  0.0 206.7 jit_solution(17573434154183197200)
XLA Ops:
  0.6 1.0 copy.24
  2.0 22.4 %all_to_all.25.refs_1_.own_ref = bf16[8,16,32,128]{3,2,1,0:T(8,128)(2,1)S(1)} all-to-all(bf16[8,16,32,128]{3,2,1,0:T(8,128)(2,1)S(1)} %shard_map.75), channel_id=1, replica_groups=mesh['yl'=2,'z'=8,'x'=4,'yh'=2,'core'=2] {'x','yh'}, dimensions={0} | all-to-all | bytes 2097152 | tf_op jit(solution)/shard_map/all_to_all | solution.py:253
  24.5 2.6 %collective-permute-done.refs_2_.other_ref = bf16[8,16,32,128]{3,2,1,0:T(8,128)(2,1)S(1)} collective-permute-done((bf16[8,16,32,128]{3,2,1,0:T(8,128)(2,1)S(1)}, bf16[8,16,32,128]{3,2,1,0:T(8,128)(2,1)S(1)}, u32[]{:S(2)}, u32[]{:S(2)}) %collective-permute-start) | collective-permute-done | bytes 1048608 | tf_op jit(solution)/shard_map/ppermute | solution.py:257
  27.1 4.4 %shard_map.76 = (f32[16,32,128]{2,1,0:T(8,128)S(1)}, bf16[8,16,32,128]{3,2,1,0:T(8,128)(2,1)}) custom-call(s32[3]{0:T(128)S(1)} %pad_add_fusion.refs_0_.place_ref, bf16[8,16,32,128]{3,2,1,0:T(8,128)(2,1)S(1)} %all_to_all.25.refs_1_.own_ref, bf16[8,16,32,128]{3,2,1,0:T(8,128)(2,1)S(1)} %collective-permute-done.refs_2_.other_ref, bf16[864,512]{1,0:T(8,128)(2,1)S(1)} %bitcast.43), custom_call_target="tpu_custom_call" | custom-call | flops 1811939328 | bytes 4194304 | tf_op jit(solution)/shard_map/pallas_call | solution.py:23
  31.4 5.3 %all-to-all-start.1 = ((bf16[8,16,32,128]{3,2,1,0:T(8,128)(2,1)}), bf16[8,16,32,128]{3,2,1,0:T(8,128)(2,1)S(1)}, u32[]{:S(2)}, u32[]{:S(2)}) async-start(bf16[8,16,32,128]{3,2,1,0:T(8,128)(2,1)} %get-tuple-element.28), calls=%async_computation.1 | async-start | bytes 2097152 | tf_op jit(solution)/shard_map/all_to_all | solution.py:253
  37.4 1.5 copy.27
  39.5 2.2 %copy.28 = bf16[864,512]{0,1:T(8,128)(2,1)} copy(bf16[864,512]{1,0:T(8,128)(2,1)} %collective-permute-done.3) | data formatting | bytes 1769472 | tf_op jit(solution)/shard_map/ppermute | solution.py:257
  41.8 10.3 %all-to-all-done.1.refs_1_.own_ref = bf16[8,16,32,128]{3,2,1,0:T(8,128)(2,1)S(1)} async-done(((bf16[8,16,32,128]{3,2,1,0:T(8,128)(2,1)}), bf16[8,16,32,128]{3,2,1,0:T(8,128)(2,1)S(1)}, u32[]{:S(2)}, u32[]{:S(2)}) %all-to-all-start.1) | async-done | bytes 1048608 | tf_op jit(solution)/shard_map/all_to_all | solution.py:253
  52.1 1.2 copy-done
  53.3 4.1 %shard_map.78 = (bf16[16,32,128]{2,1,0:T(8,128)(2,1)S(1)}, bf16[16,32,128]{2,1,0:T(8,128)(2,1)S(1)}, bf16[16,32,128]{2,1,0:T(8,128)(2,1)S(1)}, bf16[16,32,128]{2...) custom-call(s32[3]{0:T(128)S(1)} %pad_add_fusion.refs_0_.place_ref, ...), custom_call_target="tpu_custom_call" | custom-call | flops 1811939328 | bytes 4194304 | tf_op jit(solution)/shard_map/pallas_call | solution.py:23
  57.4 2.7 %collective-permute-start.4 = (bf16[16,32,128]{2,1,0:T(8,128)(2,1)S(1)}, bf16[16,32,128]{2,1,0:T(8,128)(2,1)S(1)}, u32[]{:S(2)}, u32[]{:S(2)}) collective-permute-start(bf16[16,32,128]{2,1,0:T(8,128)(2,1)S(1)} %get-tuple-element.31), channel_id=1, source_target_pairs={{0,2},{2,0},{4,6},{6,4},{8,10},{10,8},{12,14},{14,12},{1,3},{3,1},... | collective-permute-start | bytes 393224 | tf_op jit(solution)/shard_map/ppermute | solution.py:268
  60.1 2.8 %collective-permute-start.6 = (bf16[16,32,128]{2,1,0:T(8,128)(2,1)S(1)}, bf16[16,32,128]{2,1,0:T(8,128)(2,1)S(1)}, u32[]{:S(2)}, u32[]{:S(2)}) collective-permute-start(bf16[16,32,128]{2,1,0:T(8,128)(2,1)S(1)} %get-tuple-element.33), channel_id=1, source_target_pairs={{0,6},{2,4},{4,10},{6,8},{8,14},{10,12},{12,2},{14,0},{1,7},{3,5},... | collective-permute-start | bytes 393224 | tf_op jit(solution)/shard_map/ppermute | solution.py:268
  62.9 1.6 collective-permute-start.7
  64.9 2.9 %collective-permute-start.8 = (bf16[16,32,128]{2,1,0:T(8,128)(2,1)S(1)}, bf16[16,32,128]{2,1,0:T(8,128)(2,1)S(1)}, u32[]{:S(2)}, u32[]{:S(2)}) collective-permute-start(bf16[16,32,128]{2,1,0:T(8,128)(2,1)S(1)} %get-tuple-element.35), channel_id=1, source_target_pairs={{0,10},{2,8},{4,14},{6,12},{8,2},{10,0},{12,6},{14,4},{1,11},{3,9}... | collective-permute-start | bytes 393224 | tf_op jit(solution)/shard_map/ppermute | solution.py:268
  67.8 1.2 collective-permute-start.9
  69.3 10.0 %collective-permute-start.10 = (bf16[16,32,128]{2,1,0:T(8,128)(2,1)S(1)}, bf16[16,32,128]{2,1,0:T(8,128)(2,1)S(1)}, u32[]{:S(2)}, u32[]{:S(2)}) collective-permute-start(bf16[16,32,128]{2,1,0:T(8,128)(2,1)S(1)} %get-tuple-element.37), channel_id=1, source_target_pairs={{0,14},{2,12},{4,2},{6,0},{8,6},{10,4},{12,10},{14,8},{1,15},{3,13... | collective-permute-start | bytes 393224 | tf_op jit(solution)/shard_map/ppermute | solution.py:268
  79.3 2.5 %collective-permute-done.10.refs_8_ = bf16[16,32,128]{2,1,0:T(8,128)(2,1)S(1)} collective-permute-done((bf16[16,32,128]{2,1,0:T(8,128)(2,1)S(1)}, bf16[16,32,128]{2,1,0:T(8,128)(2,1)S(1)}, u32[]{:S(2)}, u32[]{:S(2)}) %collective-permute-start.10) | collective-permute-done | bytes 131104 | tf_op jit(solution)/shard_map/ppermute | solution.py:268
  81.9 1.3 shard_map.79.field_ref
  83.1 3.9 %shard_map.82 = (f32[8,27,8,128]{3,2,1,0:T(8,128)S(1)}, bf16[8,27,8,128]{3,2,1,0:T(8,128)(2,1)S(1)}) custom-call(s32[3]{0:T(128)S(1)} %pad_add_fusion.refs_0_.place_ref, bf16[16,32,128]{2,1,0:T(8,128)(2,1)} %shard_map.79.field_ref, bf16[8,16,32,128]{3,2,1,0:T(8,128)(2,1)S(1)} %all_to_all.25.refs_1_.own_ref, bf16[8,16,32,128]{3,2,1,0:T(8,128)(2,1)S(1)} %copy-done.10), custom_call_target="tpu_custom_call" | custom-call | flops 1811939328 | bytes 4194304 | tf_op jit(solution)/shard_map/pallas_call | solution.py:23
  87.8 9.1 %collective-permute-done.20.got_ref = bf16[8,27,8,128]{3,2,1,0:T(8,128)(2,1)S(1)} collective-permute-done((bf16[8,27,8,128]{3,2,1,0:T(8,128)(2,1)S(1)}, bf16[8,27,8,128]{3,2,1,0:T(8,128)(2,1)S(1)}, u32[]{:S(2)}, u32[]{:S(2)}) %collective-permute-start.20) | collective-permute-done | bytes 442400 | tf_op jit(solution)/shard_map/ppermute | solution.py:257
  97.7 8.5 %all-to-all-start.2 = ((bf16[8,27,8,128]{3,2,1,0:T(8,128)(2,1)}), bf16[8,27,8,128]{3,2,1,0:T(8,128)(2,1)S(1)}, u32[]{:S(2)}, u32[]{:S(2)}) async-start(bf16[8,27,8,128]{3,2,1,0:T(8,128)(2,1)} %shard_map.83), calls=%async_computation.2 | async-start | bytes 884736 | tf_op jit(solution)/shard_map/all_to_all | solution.py:253
  106.2 5.0 %shard_map.84 = (f32[8,27,8,128]{3,2,1,0:T(8,128)S(1)}, bf16[8,27,8,128]{3,2,1,0:T(8,128)(2,1)}) custom-call(s32[3]{0:T(128)S(1)} %pad_add_fusion.refs_0_.place_ref, bf16[16,32,128]{2,1,0:T(8,128)(2,1)S(1)} %bitcast.48, bf16[8,16,32,128]{3,2,1,0:T(8,128)(2,1)S(1)} %all-to-all-done.1.refs_1_.own_ref, ...), custom_call_target="tpu_custom_call" | custom-call | flops 1811939328 | bytes 4194304 | tf_op jit(solution)/shard_map/pallas_call | solution.py:23
  111.9 7.3 %all-to-all-done.2.pieces_ref = bf16[8,27,8,128]{3,2,1,0:T(8,128)(2,1)S(1)} async-done(((bf16[8,27,8,128]{3,2,1,0:T(8,128)(2,1)}), bf16[8,27,8,128]{3,2,1,0:T(8,128)(2,1)S(1)}, u32[]{:S(2)}, u32[]{:S(2)}) %all-to-all-start.2) | async-done | bytes 442400 | tf_op jit(solution)/shard_map/all_to_all | solution.py:253
  119.2 0.9 collective-permute-done.21.got_ref
  120.9 1.0 copy-done.6
  121.9 1.1 shard_map.85
  122.9 6.9 %all-to-all-start.3 = ((bf16[8,54,8,128]{3,2,1,0:T(8,128)(2,1)}), bf16[8,54,8,128]{3,2,1,0:T(8,128)(2,1)S(1)}, u32[]{:S(2)}, u32[]{:S(2)}) async-start(bf16[8,54,8,128]{3,2,1,0:T(8,128)(2,1)} %shard_map.85), calls=%async_computation.3 | async-start | bytes 1769472 | tf_op jit(solution)/shard_map/all_to_all | solution.py:253
  130.0 20.8 %all-to-all-done.3.both_ref = bf16[8,54,8,128]{3,2,1,0:T(8,128)(2,1)S(1)} async-done(((bf16[8,54,8,128]{3,2,1,0:T(8,128)(2,1)}), bf16[8,54,8,128]{3,2,1,0:T(8,128)(2,1)S(1)}, u32[]{:S(2)}, u32[]{:S(2)}) %all-to-all-start.3) | async-done | bytes 884768 | tf_op jit(solution)/shard_map/all_to_all | solution.py:253
  150.7 1.0 shard_map.86
  151.7 3.5 %all-to-all-start.4 = ((bf16[8,27,8,128]{3,2,1,0:T(8,128)(2,1)}), bf16[8,27,8,128]{3,2,1,0:T(8,128)(2,1)S(1)}, u32[]{:S(2)}, u32[]{:S(2)}) async-start(bf16[8,27,8,128]{3,2,1,0:T(8,128)(2,1)} %get-tuple-element.51), calls=%async_computation.4 | async-start | bytes 884736 | tf_op jit(solution)/shard_map/all_to_all | solution.py:253
  155.9 1.5 copy.30
  157.4 4.8 %shard_map.80 = (bf16[16,32,128]{2,1,0:T(8,128)(2,1)S(1)}, bf16[16,32,128]{2,1,0:T(8,128)(2,1)}, bf16[16,32,128]{2,1,0:T(8,128)(2,1)S(1)}, bf16[16,32,128]{2,1,0...) custom-call(s32[3]{0:T(128)S(1)} %pad_add_fusion.refs_0_.place_ref, ...), custom_call_target="tpu_custom_call" | custom-call | flops 1811939328 | bytes 4194304 | tf_op jit(solution)/shard_map/pallas_call | solution.py:23
  167.8 1.1 collective-permute-start.23
  168.9 4.3 %collective-permute-start.14 = (bf16[16,32,128]{2,1,0:T(8,128)(2,1)}, bf16[16,32,128]{2,1,0:T(8,128)(2,1)S(1)}, u32[]{:S(2)}, u32[]{:S(2)}) collective-permute-start(bf16[16,32,128]{2,1,0:T(8,128)(2,1)} %copy-done.16), channel_id=1, source_target_pairs={{0,4},{2,6},{4,8},{6,10},{8,12},{10,14},{12,0},{14,2},{1,5},{3,7},... | collective-permute-start | bytes 393224 | tf_op jit(solution)/shard_map/ppermute | solution.py:268
  173.3 1.5 collective-permute-done.13.refs_2_
  174.8 1.0 collective-permute-start.16
  175.8 1.5 collective-permute-done.14.refs_3_
  177.4 2.0 collective-permute-start.17
  179.4 5.2 %collective-permute-done.15.refs_4_ = bf16[16,32,128]{2,1,0:T(8,128)(2,1)S(1)} collective-permute-done((bf16[16,32,128]{2,1,0:T(8,128)(2,1)}, bf16[16,32,128]{2,1,0:T(8,128)(2,1)S(1)}, u32[]{:S(2)}, u32[]{:S(2)}) %collective-permute-start.15) | collective-permute-done | bytes 131104 | tf_op jit(solution)/shard_map/ppermute | solution.py:268
  184.5 1.1 collective-permute-start.19
  185.6 2.4 %collective-permute-done.17.refs_6_ = bf16[16,32,128]{2,1,0:T(8,128)(2,1)S(1)} collective-permute-done((bf16[16,32,128]{2,1,0:T(8,128)(2,1)}, bf16[16,32,128]{2,1,0:T(8,128)(2,1)S(1)}, u32[]{:S(2)}, u32[]{:S(2)}) %collective-permute-start.17) | collective-permute-done | bytes 131104 | tf_op jit(solution)/shard_map/ppermute | solution.py:268
  188.0 1.7 collective-permute-done.18.refs_7_
  189.7 4.4 %collective-permute-done.19.refs_8_ = bf16[16,32,128]{2,1,0:T(8,128)(2,1)S(1)} collective-permute-done((bf16[16,32,128]{2,1,0:T(8,128)(2,1)}, bf16[16,32,128]{2,1,0:T(8,128)(2,1)S(1)}, u32[]{:S(2)}, u32[]{:S(2)}) %collective-permute-start.19) | collective-permute-done | bytes 131104 | tf_op jit(solution)/shard_map/ppermute | solution.py:268
  194.1 0.9 copy-done.4
  195.1 0.9 copy-done.8
  197.4 4.0 %shard_map.77 = f32[16,32,128]{2,1,0:T(8,128)S(1)} custom-call(s32[3]{0:T(128)S(1)} %pad_add_fusion.refs_0_.place_ref, bf16[8,16,32,128]{3,2,1,0:T(8,128)(2,1)S(1)} %all-to-all-done.1.refs_1_.own_ref, bf16[8,16,32,128]{3,2,1,0:T(8,128)(2,1)} %collective-permute-done.1.refs_2_.other_ref, bf16[864,512]{1,0:T(8,128)(2,1)} %bitcast.9.refs_3_, ...), custom_call_target="tpu_custom_call" | custom-call | flops 1811939328 | bytes 4194304 | tf_op jit(solution)/shard_map/pallas_call | solution.py:23
  202.3 2.5 %shard_map.87 = f32[27,32,512]{2,1,0:T(8,128)} custom-call(s32[3]{0:T(128)S(1)} %pad_add_fusion.refs_0_.place_ref, bf16[8,27,8,128]{3,2,1,0:T(8,128)(2,1)} %get-tuple-element.50.full_ref, bf16[8,27,8,128]{3,2,1,0:T(8,128)(2,1)S(1)} %collective-permute-done.22.other_ref), custom_call_target="tpu_custom_call" | custom-call | flops 1048576 | bytes 4194304 | tf_op jit(solution)/shard_map/pallas_call | solution.py:23
  204.8 2.0 shard_map.88
  (68 shorter events, 14.3 us)
Async XLA Ops:
  0.6 26.4 %copy-start.1 = (bf16[32,27,512]{2,0,1:T(8,128)(2,1)S(1)}, bf16[32,27,512]{2,0,1:T(8,128)(2,1)}, u32[]{:S(2)}) copy-start(bf16[32,27,512]{2,0,1:T(8,128)(2,1)} %param.5) | copy-start | bytes 2654212
  24.4 2.7 %collective-permute-start = (bf16[8,16,32,128]{3,2,1,0:T(8,128)(2,1)S(1)}, bf16[8,16,32,128]{3,2,1,0:T(8,128)(2,1)S(1)}, u32[]{:S(2)}, u32[]{:S(2)}) collective-permute-start(bf16[8,16,32,128]{3,2,1,0:T(8,128)(2,1)S(1)} %all_to_all.25.refs_1_.own_ref), channel_id=1, source_target_pairs={{0,1},{1,0},{2,3},{3,2},{4,5},{5,4},{6,7},{7,6},{8,9},{9,8},{10,11... | collective-permute-start | bytes 3145736 | tf_op jit(solution)/shard_map/ppermute | solution.py:257
  27.1 4.4 %copy-start.9 = (bf16[8,16,32,128]{3,2,1,0:T(8,128)(2,1)}, bf16[8,16,32,128]{3,2,1,0:T(8,128)(2,1)S(1)}, u32[]{:S(2)}) copy-start(bf16[8,16,32,128]{3,2,1,0:T(8,128)(2,1)S(1)} %collective-permute-done.refs_2_.other_ref) | copy-start | bytes 3145732
  31.4 5.3 %copy-start.17 = (bf16[1,32,4,4,128]{4,3,2,1,0:T(4,128)(2,1)S(1)}, bf16[1,32,4,4,128]{4,3,2,1,0:T(4,128)(2,1)}, u32[]{:S(2)}) copy-start(bf16[1,32,4,4,128]{4,3,2,1,0:T(4,128)(2,1)} %param.7) | copy-start | bytes 393220
  31.4 20.6 %all-to-all-start.1 = ((bf16[8,16,32,128]{3,2,1,0:T(8,128)(2,1)}), bf16[8,16,32,128]{3,2,1,0:T(8,128)(2,1)S(1)}, u32[]{:S(2)}, u32[]{:S(2)}) async-start(bf16[8,16,32,128]{3,2,1,0:T(8,128)(2,1)} %get-tuple-element.28), calls=%async_computation.1 | async-start | bytes 2097152 | tf_op jit(solution)/shard_map/all_to_all | solution.py:253
  36.8 2.8 %collective-permute-start.3 = (bf16[864,512]{1,0:T(8,128)(2,1)}, bf16[864,512]{1,0:T(8,128)(2,1)}, u32[]{:S(2)}, u32[]{:S(2)}) collective-permute-start(bf16[864,512]{1,0:T(8,128)(2,1)} %bitcast.9.refs_3_), channel_id=1, source_target_pairs={{0,1},{1,0},{2,3},{3,2},{4,5},{5,4},{6,7},{7,6},{8,9},{9,8},{10,11... | collective-permute-start | bytes 2654216 | tf_op jit(solution)/shard_map/ppermute | solution.py:257
  36.8 69.4 %copy-start.3 = (bf16[4,4,32,128]{3,2,1,0:T(8,128)(2,1)}, bf16[4,4,32,128]{3,2,1,0:T(8,128)(2,1)S(1)}, u32[]{:S(2)}) copy-start(bf16[4,4,32,128]{3,2,1,0:T(8,128)(2,1)S(1)} %copy.26) | copy-start | bytes 393220
  36.8 15.3 %collective-permute-start.2 = (bf16[16,32,128]{2,1,0:T(8,128)(2,1)S(1)}, bf16[16,32,128]{2,1,0:T(8,128)(2,1)}, u32[]{:S(2)}, u32[]{:S(2)}) collective-permute-start(bf16[16,32,128]{2,1,0:T(8,128)(2,1)S(1)} %bitcast.46), channel_id=1, source_target_pairs={{0,1},{1,0},{2,3},{3,2},{4,5},{5,4},{6,7},{7,6},{8,9},{9,8},{10,11... | collective-permute-start | bytes 393224 | tf_op jit(solution)/shard_map/ppermute | solution.py:257
  52.1 54.1 %collective-permute-start.1 = (bf16[8,16,32,128]{3,2,1,0:T(8,128)(2,1)S(1)}, bf16[8,16,32,128]{3,2,1,0:T(8,128)(2,1)}, u32[]{:S(2)}, u32[]{:S(2)}) collective-permute-start(bf16[8,16,32,128]{3,2,1,0:T(8,128)(2,1)S(1)} %all-to-all-done.1.refs_1_.own_ref), channel_id=1, source_target_pairs={{0,1},{1,0},{2,3},{3,2},{4,5},{5,4},{6,7},{7,6},{8,9},{9,8},{10,11... | collective-permute-start | bytes 3145736 | tf_op jit(solution)/shard_map/ppermute | solution.py:257
  52.1 1.2 copy-start
  53.3 29.8 %copy-start.10 = (bf16[8,16,32,128]{3,2,1,0:T(8,128)(2,1)S(1)}, bf16[8,16,32,128]{3,2,1,0:T(8,128)(2,1)}, u32[]{:S(2)}) copy-start(bf16[8,16,32,128]{3,2,1,0:T(8,128)(2,1)} %copy-done.9) | copy-start | bytes 3145732
  57.4 7.5 %collective-permute-start.4 = (bf16[16,32,128]{2,1,0:T(8,128)(2,1)S(1)}, bf16[16,32,128]{2,1,0:T(8,128)(2,1)S(1)}, u32[]{:S(2)}, u32[]{:S(2)}) collective-permute-start(bf16[16,32,128]{2,1,0:T(8,128)(2,1)S(1)} %get-tuple-element.31), channel_id=1, source_target_pairs={{0,2},{2,0},{4,6},{6,4},{8,10},{10,8},{12,14},{14,12},{1,3},{3,1},... | collective-permute-start | bytes 393224 | tf_op jit(solution)/shard_map/ppermute | solution.py:268
  60.1 7.7 %collective-permute-start.5 = (bf16[16,32,128]{2,1,0:T(8,128)(2,1)S(1)}, bf16[16,32,128]{2,1,0:T(8,128)(2,1)S(1)}, u32[]{:S(2)}, u32[]{:S(2)}) collective-permute-start(bf16[16,32,128]{2,1,0:T(8,128)(2,1)S(1)} %get-tuple-element.32), channel_id=1, source_target_pairs={{0,4},{2,6},{4,8},{6,10},{8,12},{10,14},{12,0},{14,2},{1,5},{3,7},... | collective-permute-start | bytes 393224 | tf_op jit(solution)/shard_map/ppermute | solution.py:268
  60.1 9.1 %collective-permute-start.6 = (bf16[16,32,128]{2,1,0:T(8,128)(2,1)S(1)}, bf16[16,32,128]{2,1,0:T(8,128)(2,1)S(1)}, u32[]{:S(2)}, u32[]{:S(2)}) collective-permute-start(bf16[16,32,128]{2,1,0:T(8,128)(2,1)S(1)} %get-tuple-element.33), channel_id=1, source_target_pairs={{0,6},{2,4},{4,10},{6,8},{8,14},{10,12},{12,2},{14,0},{1,7},{3,5},... | collective-permute-start | bytes 393224 | tf_op jit(solution)/shard_map/ppermute | solution.py:268
  62.9 16.4 %collective-permute-start.7 = (bf16[16,32,128]{2,1,0:T(8,128)(2,1)S(1)}, bf16[16,32,128]{2,1,0:T(8,128)(2,1)S(1)}, u32[]{:S(2)}, u32[]{:S(2)}) collective-permute-start(bf16[16,32,128]{2,1,0:T(8,128)(2,1)S(1)} %get-tuple-element.34), channel_id=1, source_target_pairs={{0,8},{2,10},{4,12},{6,14},{8,0},{10,2},{12,4},{14,6},{1,9},{3,11}... | collective-permute-start | bytes 393224 | tf_op jit(solution)/shard_map/ppermute | solution.py:268
  64.9 14.4 %collective-permute-start.8 = (bf16[16,32,128]{2,1,0:T(8,128)(2,1)S(1)}, bf16[16,32,128]{2,1,0:T(8,128)(2,1)S(1)}, u32[]{:S(2)}, u32[]{:S(2)}) collective-permute-start(bf16[16,32,128]{2,1,0:T(8,128)(2,1)S(1)} %get-tuple-element.35), channel_id=1, source_target_pairs={{0,10},{2,8},{4,14},{6,12},{8,2},{10,0},{12,6},{14,4},{1,11},{3,9}... | collective-permute-start | bytes 393224 | tf_op jit(solution)/shard_map/ppermute | solution.py:268
  67.8 11.5 %collective-permute-start.9 = (bf16[16,32,128]{2,1,0:T(8,128)(2,1)S(1)}, bf16[16,32,128]{2,1,0:T(8,128)(2,1)S(1)}, u32[]{:S(2)}, u32[]{:S(2)}) collective-permute-start(bf16[16,32,128]{2,1,0:T(8,128)(2,1)S(1)} %get-tuple-element.36), channel_id=1, source_target_pairs={{0,12},{2,14},{4,0},{6,2},{8,4},{10,6},{12,8},{14,10},{1,13},{3,15... | collective-permute-start | bytes 393224 | tf_op jit(solution)/shard_map/ppermute | solution.py:268
  69.3 12.6 %collective-permute-start.10 = (bf16[16,32,128]{2,1,0:T(8,128)(2,1)S(1)}, bf16[16,32,128]{2,1,0:T(8,128)(2,1)S(1)}, u32[]{:S(2)}, u32[]{:S(2)}) collective-permute-start(bf16[16,32,128]{2,1,0:T(8,128)(2,1)S(1)} %get-tuple-element.37), channel_id=1, source_target_pairs={{0,14},{2,12},{4,2},{6,0},{8,6},{10,4},{12,10},{14,8},{1,15},{3,13... | collective-permute-start | bytes 393224 | tf_op jit(solution)/shard_map/ppermute | solution.py:268
  87.0 9.9 %collective-permute-start.20 = (bf16[8,27,8,128]{3,2,1,0:T(8,128)(2,1)S(1)}, bf16[8,27,8,128]{3,2,1,0:T(8,128)(2,1)S(1)}, u32[]{:S(2)}, u32[]{:S(2)}) collective-permute-start(bf16[8,27,8,128]{3,2,1,0:T(8,128)(2,1)S(1)} %get-tuple-element.47), channel_id=1, source_target_pairs={{0,128},{128,0},{1,129},{129,1},{2,130},{130,2},{3,131},{131,3},{4... | collective-permute-start | bytes 1327112 | tf_op jit(solution)/shard_map/ppermute | solution.py:257
  97.7 21.4 %all-to-all-start.2 = ((bf16[8,27,8,128]{3,2,1,0:T(8,128)(2,1)}), bf16[8,27,8,128]{3,2,1,0:T(8,128)(2,1)S(1)}, u32[]{:S(2)}, u32[]{:S(2)}) async-start(bf16[8,27,8,128]{3,2,1,0:T(8,128)(2,1)} %shard_map.83), calls=%async_computation.2 | async-start | bytes 884736 | tf_op jit(solution)/shard_map/all_to_all | solution.py:253
  111.2 8.9 %collective-permute-start.21 = (bf16[8,27,8,128]{3,2,1,0:T(8,128)(2,1)}, bf16[8,27,8,128]{3,2,1,0:T(8,128)(2,1)S(1)}, u32[]{:S(2)}, u32[]{:S(2)}) collective-permute-start(bf16[8,27,8,128]{3,2,1,0:T(8,128)(2,1)} %get-tuple-element.49), channel_id=1, source_target_pairs={{0,128},{128,0},{1,129},{129,1},{2,130},{130,2},{3,131},{131,3},{4... | collective-permute-start | bytes 1327112 | tf_op jit(solution)/shard_map/ppermute | solution.py:257
  120.1 0.8 copy-start.5
  120.9 1.0 copy-start.6
  121.9 8.0 %copy-start.2 = (bf16[32,27,512]{2,0,1:T(8,128)(2,1)S(1)}, bf16[32,27,512]{2,0,1:T(8,128)(2,1)}, u32[]{:S(2)}) copy-start(bf16[32,27,512]{2,0,1:T(8,128)(2,1)} %param.5) | copy-start | bytes 2654212
  122.9 27.8 %all-to-all-start.3 = ((bf16[8,54,8,128]{3,2,1,0:T(8,128)(2,1)}), bf16[8,54,8,128]{3,2,1,0:T(8,128)(2,1)S(1)}, u32[]{:S(2)}, u32[]{:S(2)}) async-start(bf16[8,54,8,128]{3,2,1,0:T(8,128)(2,1)} %shard_map.85), calls=%async_computation.3 | async-start | bytes 1769472 | tf_op jit(solution)/shard_map/all_to_all | solution.py:253
  129.9 26.0 %collective-permute-start.12 = (bf16[864,512]{1,0:T(8,128)(2,1)S(1)}, bf16[864,512]{1,0:T(8,128)(2,1)}, u32[]{:S(2)}, u32[]{:S(2)}) collective-permute-start(bf16[864,512]{1,0:T(8,128)(2,1)S(1)} %bitcast.44), channel_id=1, source_target_pairs={{0,1},{1,0},{2,3},{3,2},{4,5},{5,4},{6,7},{7,6},{8,9},{9,8},{10,11... | collective-permute-start | bytes 2654216 | tf_op jit(solution)/shard_map/ppermute | solution.py:257
  151.7 16.1 %all-to-all-start.4 = ((bf16[8,27,8,128]{3,2,1,0:T(8,128)(2,1)}), bf16[8,27,8,128]{3,2,1,0:T(8,128)(2,1)S(1)}, u32[]{:S(2)}, u32[]{:S(2)}) async-start(bf16[8,27,8,128]{3,2,1,0:T(8,128)(2,1)} %get-tuple-element.51), calls=%async_computation.4 | async-start | bytes 884736 | tf_op jit(solution)/shard_map/all_to_all | solution.py:253
  155.2 2.3 %collective-permute-start.11 = (bf16[16,32,128]{2,1,0:T(8,128)(2,1)}, bf16[16,32,128]{2,1,0:T(8,128)(2,1)}, u32[]{:S(2)}, u32[]{:S(2)}) collective-permute-start(bf16[16,32,128]{2,1,0:T(8,128)(2,1)} %shard_map.79.field_ref), channel_id=1, source_target_pairs={{0,1},{1,0},{2,3},{3,2},{4,5},{5,4},{6,7},{7,6},{8,9},{9,8},{10,11... | collective-permute-start | bytes 393224 | tf_op jit(solution)/shard_map/ppermute | solution.py:257
  162.2 0.7 copy-start.7
  162.9 0.7 copy-start.11
  163.5 0.7 copy-start.12
  164.2 0.6 copy-start.13
  164.8 0.6 copy-start.14
  165.5 0.7 copy-start.15
  166.1 0.6 copy-start.16
  166.7 8.1 %collective-permute-start.13 = (bf16[16,32,128]{2,1,0:T(8,128)(2,1)}, bf16[16,32,128]{2,1,0:T(8,128)(2,1)S(1)}, u32[]{:S(2)}, u32[]{:S(2)}) collective-permute-start(bf16[16,32,128]{2,1,0:T(8,128)(2,1)} %get-tuple-element.39), channel_id=1, source_target_pairs={{0,2},{2,0},{4,6},{6,4},{8,10},{10,8},{12,14},{14,12},{1,3},{3,1},... | collective-permute-start | bytes 393224 | tf_op jit(solution)/shard_map/ppermute | solution.py:268
  166.9 35.4 %collective-permute-start.22 = (bf16[8,27,8,128]{3,2,1,0:T(8,128)(2,1)}, bf16[8,27,8,128]{3,2,1,0:T(8,128)(2,1)S(1)}, u32[]{:S(2)}, u32[]{:S(2)}) collective-permute-start(bf16[8,27,8,128]{3,2,1,0:T(8,128)(2,1)} %get-tuple-element.50.full_ref), channel_id=1, source_target_pairs={{0,128},{128,0},{1,129},{129,1},{2,130},{130,2},{3,131},{131,3},{4... | collective-permute-start | bytes 1327112 | tf_op jit(solution)/shard_map/ppermute | solution.py:257
  167.8 37.0 %collective-permute-start.23 = (bf16[8,27,8,128]{3,2,1,0:T(8,128)(2,1)S(1)}, bf16[8,27,8,128]{3,2,1,0:T(8,128)(2,1)S(1)}, u32[]{:S(2)}, u32[]{:S(2)}) collective-permute-start(bf16[8,27,8,128]{3,2,1,0:T(8,128)(2,1)S(1)} %all-to-all-done.4.full_ref), channel_id=1, source_target_pairs={{0,128},{128,0},{1,129},{129,1},{2,130},{130,2},{3,131},{131,3},{4... | collective-permute-start | bytes 1327112 | tf_op jit(solution)/shard_map/ppermute | solution.py:257
  168.9 8.5 %collective-permute-start.14 = (bf16[16,32,128]{2,1,0:T(8,128)(2,1)}, bf16[16,32,128]{2,1,0:T(8,128)(2,1)S(1)}, u32[]{:S(2)}, u32[]{:S(2)}) collective-permute-start(bf16[16,32,128]{2,1,0:T(8,128)(2,1)} %copy-done.16), channel_id=1, source_target_pairs={{0,4},{2,6},{4,8},{6,10},{8,12},{10,14},{12,0},{14,2},{1,5},{3,7},... | collective-permute-start | bytes 393224 | tf_op jit(solution)/shard_map/ppermute | solution.py:268
  173.2 11.3 %collective-permute-start.15 = (bf16[16,32,128]{2,1,0:T(8,128)(2,1)}, bf16[16,32,128]{2,1,0:T(8,128)(2,1)S(1)}, u32[]{:S(2)}, u32[]{:S(2)}) collective-permute-start(bf16[16,32,128]{2,1,0:T(8,128)(2,1)} %copy-done.15), channel_id=1, source_target_pairs={{0,6},{2,4},{4,10},{6,8},{8,14},{10,12},{12,2},{14,0},{1,7},{3,5},... | collective-permute-start | bytes 393224 | tf_op jit(solution)/shard_map/ppermute | solution.py:268
  174.8 9.7 %collective-permute-start.16 = (bf16[16,32,128]{2,1,0:T(8,128)(2,1)}, bf16[16,32,128]{2,1,0:T(8,128)(2,1)S(1)}, u32[]{:S(2)}, u32[]{:S(2)}) collective-permute-start(bf16[16,32,128]{2,1,0:T(8,128)(2,1)} %copy-done.14), channel_id=1, source_target_pairs={{0,8},{2,10},{4,12},{6,14},{8,0},{10,2},{12,4},{14,6},{1,9},{3,11}... | collective-permute-start | bytes 393224 | tf_op jit(solution)/shard_map/ppermute | solution.py:268
  177.4 10.6 %collective-permute-start.17 = (bf16[16,32,128]{2,1,0:T(8,128)(2,1)}, bf16[16,32,128]{2,1,0:T(8,128)(2,1)S(1)}, u32[]{:S(2)}, u32[]{:S(2)}) collective-permute-start(bf16[16,32,128]{2,1,0:T(8,128)(2,1)} %copy-done.13), channel_id=1, source_target_pairs={{0,10},{2,8},{4,14},{6,12},{8,2},{10,0},{12,6},{14,4},{1,11},{3,9}... | collective-permute-start | bytes 393224 | tf_op jit(solution)/shard_map/ppermute | solution.py:268
  184.5 5.2 %collective-permute-start.18 = (bf16[16,32,128]{2,1,0:T(8,128)(2,1)}, bf16[16,32,128]{2,1,0:T(8,128)(2,1)S(1)}, u32[]{:S(2)}, u32[]{:S(2)}) collective-permute-start(bf16[16,32,128]{2,1,0:T(8,128)(2,1)} %copy-done.12), channel_id=1, source_target_pairs={{0,12},{2,14},{4,0},{6,2},{8,4},{10,6},{12,8},{14,10},{1,13},{3,15... | collective-permute-start | bytes 393224 | tf_op jit(solution)/shard_map/ppermute | solution.py:268
  184.5 9.6 %collective-permute-start.19 = (bf16[16,32,128]{2,1,0:T(8,128)(2,1)}, bf16[16,32,128]{2,1,0:T(8,128)(2,1)S(1)}, u32[]{:S(2)}, u32[]{:S(2)}) collective-permute-start(bf16[16,32,128]{2,1,0:T(8,128)(2,1)} %copy-done.11), channel_id=1, source_target_pairs={{0,14},{2,12},{4,2},{6,0},{8,6},{10,4},{12,10},{14,8},{1,15},{3,13... | collective-permute-start | bytes 393224 | tf_op jit(solution)/shard_map/ppermute | solution.py:268
  194.1 0.9 copy-start.4
  195.0 0.9 copy-start.8

commit v3 on v2

--- a/solution.py
+++ b/solution.py
@@ -15,17 +15,17 @@
 TAPS = [(i, j, k) for i in range(3) for j in range(3) for k in range(3)]
 COUNT = 16 * 16 * 128
 FIELD = (16, 32, 128)
-SMEM_SPEC = pl.BlockSpec(memory_space=pltpu.SMEM)
+ANY_SPEC = pl.BlockSpec(memory_space=pl.ANY)
 VMEM_SPEC = pl.BlockSpec(memory_space=pltpu.VMEM)
 
 
-def call(body, outs, scratch, limit, flops, *args):
+def call(body, outs, scratch, limit, flops, *args, specs=None):
     return pl.pallas_call(
         body,
         out_shape=tuple(jax.ShapeDtypeStruct(*o) for o in outs),
-        in_specs=[SMEM_SPEC if a.dtype == jnp.int32 else VMEM_SPEC for a in args],
+        in_specs=[VMEM_SPEC] * len(args) if specs is None else specs,
         out_specs=(VMEM_SPEC,) * len(outs),
-        scratch_shapes=[pltpu.VMEM(*s) for s in scratch],
+        scratch_shapes=[pltpu.VMEM(*s) if isinstance(s, tuple) else s for s in scratch],
         compiler_params=pltpu.CompilerParams(vmem_limit_bytes=limit << 20),
         cost_estimate=pl.CostEstimate(flops=flops, bytes_accessed=4 << 20, transcendentals=0),
     )(*args)
@@ -86,8 +86,8 @@
             out_ref[cell] = value.astype(BF16)
 
 
-def assemble(core_ref, own_ref, other_ref, acts):
-    core = core_ref[0]
+def assemble(own_ref, other_ref, acts):
+    core = lax.axis_index("core")
 
     def step(n, carry):
         low = pl.multiple_of(n * 64 + core * 32, 32)
@@ -102,10 +102,13 @@
 
 
 def conv_body(final, *refs):
-    core_ref, own_ref, other_ref, kernel_ref = refs[:4]
-    acts, products = refs[-2:]
+    own_ref, other_ref, rows_ref = refs[:3]
+    acts, products, kernel_ref, arrived = refs[-4:]
+    fetch = pltpu.make_async_copy(rows_ref, kernel_ref, arrived)
+    fetch.start()
     lane = lax.broadcasted_iota(jnp.int32, (32, 128), 1)
-    assemble(core_ref, own_ref, other_ref, acts)
+    assemble(own_ref, other_ref, acts)
+    fetch.wait()
 
     for pair in range(8):
         products[pair] = jnp.dot(kernel_ref[...], acts[pair], preferred_element_type=F32)
@@ -129,11 +132,11 @@
         return behind + sums[1] + ahead
 
     if final:
-        extra_ref, out_ref = refs[4], refs[5]
+        extra_ref, out_ref = refs[3], refs[4]
         for cell in range(16):
             out_ref[cell] = extra_ref[cell].astype(F32) + output(cell)
     else:
-        hidden_ref, out_ref = refs[4], refs[5]
+        hidden_ref, out_ref = refs[3], refs[4]
         for cell in range(16):
             hidden_ref[cell] = output(cell)
         act_body(hidden_ref, out_ref)
@@ -158,9 +161,9 @@
             columns[cell // 2, index * 32 : index * 32 + 32, left : left + 128] = value
 
 
-def partial_body(place_ref, field_ref, other_ref, kernel_ref, far_ref, *refs):
+def partial_body(field_ref, other_ref, kernel_ref, far_ref, *refs):
     out_refs, (shifted, columns, far_columns, result, near, far) = refs[:8], refs[8:]
-    core = place_ref[0]
+    core = lax.axis_index("core")
     for n in range(8):
         start = pl.multiple_of(n * 64 + core * 32, 32)
         near[n * 32 : n * 32 + 32] = kernel_ref[pl.ds(start, 32)]
@@ -174,16 +177,16 @@
             for n in range(8):
                 part = out[n * 32 : n * 32 + 32, half * 128 : half * 128 + 128]
                 result[n, pair * 2 + half] = part.astype(BF16)
-    here = place_ref[2]
+    x, y = lax.axis_index("x"), lax.axis_index("yh")
     for k in range(8):
-        n = lax.rem(here // 2 + k // 2, 4) * 2 + lax.rem(here + k, 2)
+        n = lax.rem(x + k // 2, 4) * 2 + lax.rem(y + k, 2)
         out_refs[k][...] = result[n]
 
 
-def grad_body(place_ref, field_ref, own_ref, other_ref, mine_ref, theirs_ref, shifted, columns, acts, total):
+def grad_body(field_ref, own_ref, other_ref, mine_ref, theirs_ref, shifted, columns, acts, total):
     spread(field_ref, shifted, columns)
-    assemble(place_ref, own_ref, other_ref, acts)
-    first = place_ref[1] == 0
+    assemble(own_ref, other_ref, acts)
+    first = lax.axis_index("yl") == 0
     for left in (0, 256):
         term = None
         for pair in range(8):
@@ -231,15 +234,34 @@
             out_ref[n, k] = value
 
 
-def finish_body(place_ref, full_ref, other_ref, out_ref):
-    yl = place_ref[1]
+def half_body(far, pieces_ref, *refs):
+    out_ref, wide, sent = refs[-3:]
+    yl = lax.axis_index("yl")
+    half = 1 - yl if far else yl
     for piece in range(8):
-        left = piece % 4 * 128
-        low = pl.multiple_of((yl * 2 + piece // 4) * 8, 8)
-        high = pl.multiple_of((2 - yl * 2 + piece // 4) * 8, 8)
+        top, left = piece // 4 * 8, piece % 4 * 128
         for k in range(27):
-            out_ref[k, pl.ds(low, 8), left : left + 128] = full_ref[piece, k].astype(F32)
-            out_ref[k, pl.ds(high, 8), left : left + 128] = other_ref[piece, k].astype(F32)
+            wide[k, top : top + 8, left : left + 128] = pieces_ref[piece, k].astype(F32)
+    put = pltpu.make_async_copy(wide, out_ref.at[:, pl.ds(pl.multiple_of(half * 16, 16), 16), :], sent)
+    put.start()
+    put.wait()
+
+
+def finish(full, other):
+    out = None
+    for far, pieces in enumerate((full, other)):
+        kernel = pl.pallas_call(
+            functools.partial(half_body, far),
+            out_shape=jax.ShapeDtypeStruct((27, 32, 512), F32),
+            in_specs=[VMEM_SPEC, ANY_SPEC][: 1 + far],
+            out_specs=ANY_SPEC,
+            scratch_shapes=[pltpu.VMEM((27, 16, 512), F32), pltpu.SemaphoreType.DMA],
+            input_output_aliases={1: 0} if far else {},
+            compiler_params=pltpu.CompilerParams(vmem_limit_bytes=6 << 20),
+            cost_estimate=pl.CostEstimate(flops=1 << 20, bytes_accessed=2 << 20, transcendentals=0),
+        )
+        out = kernel(pieces, out) if far else kernel(pieces)
+    return out.transpose(1, 0, 2)
 
 
 FLOPS = 2 * 512 * 864 * 2048
@@ -257,11 +279,11 @@
     return lax.ppermute(value, axis, SWAP)
 
 
-def input_partial(place, field, rows):
+def input_partial(field, rows):
     far = swap(rows, "core")
     other = swap(field, "core")
     scratch = COLUMNS + [COLUMNS[1], (WIDE, BF16), ((256, 864), BF16), ((256, 864), BF16)]
-    sends = call(partial_body, [(FIELD, BF16)] * 8, scratch, 18, FLOPS, place, field, other, rows.T, far.T)
+    sends = call(partial_body, [(FIELD, BF16)] * 8, scratch, 18, FLOPS, field, other, rows.T, far.T)
     pieces = [sends[0]]
     for k in range(1, 8):
         perm = [(n, (n // 2 + k // 2) % 4 * 2 + (n + k) % 2) for n in range(8)]
@@ -269,13 +291,13 @@
     return pieces
 
 
-def kernel_grad(place, field, own, other):
+def kernel_grad(field, own, other):
     scratch = COLUMNS + [ACTS, ((864, 512), F32)]
-    mine, theirs = call(grad_body, [(PIECES, F32), (PIECES, BF16)], scratch, 20, FLOPS, place, field, own, other)
+    mine, theirs = call(grad_body, [(PIECES, F32), (PIECES, BF16)], scratch, 20, FLOPS, field, own, other)
     return mine, swap(theirs, "yl")
 
 
-def reduce_clips(place, grad_one, grad_two):
+def reduce_clips(grad_one, grad_two):
     (pair,) = call(join_body, [(PIECES, BF16)], [], 8, 1 << 20, *grad_one)
     pieces = exchange(pair, "z")
     double = (8, 54, 8, 128)
@@ -284,43 +306,41 @@
     full_two = exchange(copies, "z")
     outs = []
     for full in (full_one, full_two):
-        other = swap(full, "yl")
-        outs += call(finish_body, [((27, 32, 512), F32)], [], 6, 1 << 20, place, full, other)
-    return [out.transpose(1, 0, 2) for out in outs]
+        outs.append(finish(full, swap(full, "yl")))
+    return outs
 
 
 def shards(block_in, conv_one, conv_two, out_cotangent):
     cells = lambda v: v[0].transpose(1, 2, 0, 3).reshape(FIELD)
     whole = lambda v: v.reshape(4, 4, 32, 128).transpose(2, 0, 1, 3)[None]
     rows = lambda w: w.transpose(1, 0, 2).reshape(864, 512)
-    core, yl = lax.axis_index("core"), lax.axis_index("yl")
-    place = jnp.stack([core, yl, lax.axis_index(XY)]).astype(jnp.int32)
     x_in, cot = cells(block_in), cells(out_cotangent)
     rows_two = rows(conv_two)
     rows_one = rows(conv_one)
 
     (copies,) = call(act_body, [(WIDE, BF16)], [], 4, 1 << 20, x_in)
     own = exchange(copies, XY)
-    pieces_two = input_partial(place, cot, rows_two)
+    pieces_two = input_partial(cot, rows_two)
     other = swap(own, "core")
-    conv_scratch = [ACTS, ((8, 864, 256), F32)]
+    conv_scratch = [ACTS, ((8, 864, 256), F32), ((864, 512), BF16), pltpu.SemaphoreType.DMA]
+    conv_specs = [VMEM_SPEC, VMEM_SPEC, ANY_SPEC, VMEM_SPEC]
     hidden, copies_two = call(
         functools.partial(conv_body, False), [(FIELD, F32), (WIDE, BF16)], conv_scratch, 18, FLOPS,
-        place, own, other, rows_one,
+        own, other, rows_one, specs=conv_specs[:3],
     )
     own_two = exchange(copies_two, XY)
     (hidden_grad,) = call(
         functools.partial(pull_body, False), [(FIELD, BF16)], [(FIELD, F32)] * 2, 6, 1 << 20,
         hidden, *pieces_two,
     )
-    grad_one = kernel_grad(place, hidden_grad, own, other)
-    pieces_one = input_partial(place, hidden_grad, rows_one)
+    grad_one = kernel_grad(hidden_grad, own, other)
+    pieces_one = input_partial(hidden_grad, rows_one)
     other_two = swap(own_two, "core")
-    grad_two = kernel_grad(place, cot, own_two, other_two)
-    out_one, out_two = reduce_clips(place, grad_one, grad_two)
+    grad_two = kernel_grad(cot, own_two, other_two)
+    out_one, out_two = reduce_clips(grad_one, grad_two)
     (block_out,) = call(
         functools.partial(conv_body, True), [(FIELD, F32)], conv_scratch, 18, FLOPS,
-        place, own_two, other_two, rows_two, x_in,
+        own_two, other_two, rows_two, x_in, specs=conv_specs,
     )
     (in_grad,) = call(
         functools.partial(pull_body, True), [(FIELD, F32)], [(FIELD, F32)] * 2, 6, 1 << 20,

time: 209 us -> 210 us (level)
    pallas_call x0 -> x4, Pallas kernels: none -> 5.11 us  [finish(): out = kernel(pieces, out) if far else kernel(pieces)]
    pallas_call x14 -> x12, Pallas kernels: 35.7 us -> 31.5 us  [call(): pl.pallas_call(body, out_shape=tuple((jax.ShapeDtypeStruct(*o) for o in o...]
where the time goes in v3:
time: 210 us; the launch traced here: 208 us
  waiting for transfers between devices  71.6 us (34%)
  starting transfers between devices  58.2 us (28%)
  Pallas kernels  36.6 us (17%)
  blocking collectives  22.4 us (11%)
  local copies, waits for them, and re-layouts  18 us (9%)
    all_to_all x4, waiting for transfers between devices, exchange(): return lax.all_to_all(value, axes, 0, 0, tiled=True)  38.5 us
    pallas_call x12, Pallas kernels, call(): pl.pallas_call(body, out_shape=tuple((jax.ShapeDtypeStruct(*o) for o in o...  31.5 us
    ppermute x14, starting transfers between devices, input_partial(): pieces.append(lax.ppermute(sends[k], XY, perm))  29.9 us
    all_to_all x4, starting transfers between devices, exchange(): return lax.all_to_all(value, axes, 0, 0, tiled=True)  24.2 us
    all_to_all x1, blocking collectives, exchange(): return lax.all_to_all(value, axes, 0, 0, tiled=True)  22.4 us
    ppermute x14, waiting for transfers between devices, input_partial(): pieces.append(lax.ppermute(sends[k], XY, perm))  19.8 us
    ppermute x10, waiting for transfers between devices, swap(): return lax.ppermute(value, axis, SWAP)  13.3 us
    unnamed x36, local copies, waits for them, and re-layouts  9.32 us
  transfers between devices with their start and end apart: 28, of which 17 were waited for; matrix products, arithmetic and copies ran while one was open for 4% of the time, Pallas kernels for 14%

profile of v3, /device:TPU:2, one launch (start us, length us, event | category | flops | bytes accessed | tf_op | source)
XLA Modules:
  0.0 207.8 jit_solution(1999768178446432494)
XLA Ops:
  0.6 1.0 copy.26
  2.0 22.4 %all_to_all.25.refs_0_.own_ref = bf16[8,16,32,128]{3,2,1,0:T(8,128)(2,1)S(1)} all-to-all(bf16[8,16,32,128]{3,2,1,0:T(8,128)(2,1)S(1)} %shard_map.75), channel_id=1, replica_groups=mesh['yl'=2,'z'=8,'x'=4,'yh'=2,'core'=2] {'x','yh'}, dimensions={0} | all-to-all | bytes 2097152 | tf_op jit(solution)/shard_map/all_to_all | solution.py:275
  24.4 2.7 %collective-permute-done.refs_1_.other_ref = bf16[8,16,32,128]{3,2,1,0:T(8,128)(2,1)S(1)} collective-permute-done((bf16[8,16,32,128]{3,2,1,0:T(8,128)(2,1)S(1)}, bf16[8,16,32,128]{3,2,1,0:T(8,128)(2,1)S(1)}, u32[]{:S(2)}, u32[]{:S(2)}) %collective-permute-start) | collective-permute-done | bytes 1048608 | tf_op jit(solution)/shard_map/ppermute | solution.py:279
  27.1 4.0 %shard_map.76 = (f32[16,32,128]{2,1,0:T(8,128)S(1)}, bf16[8,16,32,128]{3,2,1,0:T(8,128)(2,1)}) custom-call(bf16[8,16,32,128]{3,2,1,0:T(8,128)(2,1)S(1)} %all_to_all.25.refs_0_.own_ref, bf16[8,16,32,128]{3,2,1,0:T(8,128)(2,1)S(1)} %collective-permute-done.refs_1_.other_ref, bf16[864,512]{1,0:T(8,128)(2,1)S(1)} %bitcast.40), custom_call_target="tpu_custom_call" | custom-call | flops 1811939328 | bytes 4194304 | tf_op jit(solution)/shard_map/pallas_call | solution.py:23
  31.1 5.3 %all-to-all-start.1 = ((bf16[8,16,32,128]{3,2,1,0:T(8,128)(2,1)}), bf16[8,16,32,128]{3,2,1,0:T(8,128)(2,1)S(1)}, u32[]{:S(2)}, u32[]{:S(2)}) async-start(bf16[8,16,32,128]{3,2,1,0:T(8,128)(2,1)} %get-tuple-element.28), calls=%async_computation.1 | async-start | bytes 2097152 | tf_op jit(solution)/shard_map/all_to_all | solution.py:275
  37.1 1.5 copy.29
  39.2 2.2 %copy.30 = bf16[864,512]{0,1:T(8,128)(2,1)} copy(bf16[864,512]{1,0:T(8,128)(2,1)} %collective-permute-done.3) | data formatting | bytes 1769472 | tf_op jit(solution)/shard_map/ppermute | solution.py:279
  41.5 10.3 %all-to-all-done.1.refs_0_.own_ref = bf16[8,16,32,128]{3,2,1,0:T(8,128)(2,1)S(1)} async-done(((bf16[8,16,32,128]{3,2,1,0:T(8,128)(2,1)}), bf16[8,16,32,128]{3,2,1,0:T(8,128)(2,1)S(1)}, u32[]{:S(2)}, u32[]{:S(2)}) %all-to-all-start.1) | async-done | bytes 1048608 | tf_op jit(solution)/shard_map/all_to_all | solution.py:275
  51.8 1.2 copy-done
  53.0 4.2 %shard_map.78 = (bf16[16,32,128]{2,1,0:T(8,128)(2,1)S(1)}, bf16[16,32,128]{2,1,0:T(8,128)(2,1)S(1)}, bf16[16,32,128]{2,1,0:T(8,128)(2,1)S(1)}, bf16[16,32,128]{2...) custom-call(bf16[16,32,128]{2,1,0:T(8,128)(2,1)S(1)} %bitcast.44, ...), custom_call_target="tpu_custom_call" | custom-call | flops 1811939328 | bytes 4194304 | tf_op jit(solution)/shard_map/pallas_call | solution.py:23
  57.1 2.7 %collective-permute-start.4 = (bf16[16,32,128]{2,1,0:T(8,128)(2,1)S(1)}, bf16[16,32,128]{2,1,0:T(8,128)(2,1)S(1)}, u32[]{:S(2)}, u32[]{:S(2)}) collective-permute-start(bf16[16,32,128]{2,1,0:T(8,128)(2,1)S(1)} %get-tuple-element.31), channel_id=1, source_target_pairs={{0,2},{2,0},{4,6},{6,4},{8,10},{10,8},{12,14},{14,12},{1,3},{3,1},... | collective-permute-start | bytes 393224 | tf_op jit(solution)/shard_map/ppermute | solution.py:290
  59.9 2.8 %collective-permute-start.6 = (bf16[16,32,128]{2,1,0:T(8,128)(2,1)S(1)}, bf16[16,32,128]{2,1,0:T(8,128)(2,1)S(1)}, u32[]{:S(2)}, u32[]{:S(2)}) collective-permute-start(bf16[16,32,128]{2,1,0:T(8,128)(2,1)S(1)} %get-tuple-element.33), channel_id=1, source_target_pairs={{0,6},{2,4},{4,10},{6,8},{8,14},{10,12},{12,2},{14,0},{1,7},{3,5},... | collective-permute-start | bytes 393224 | tf_op jit(solution)/shard_map/ppermute | solution.py:290
  62.7 1.6 collective-permute-start.7
  64.7 2.9 %collective-permute-start.8 = (bf16[16,32,128]{2,1,0:T(8,128)(2,1)S(1)}, bf16[16,32,128]{2,1,0:T(8,128)(2,1)S(1)}, u32[]{:S(2)}, u32[]{:S(2)}) collective-permute-start(bf16[16,32,128]{2,1,0:T(8,128)(2,1)S(1)} %get-tuple-element.35), channel_id=1, source_target_pairs={{0,10},{2,8},{4,14},{6,12},{8,2},{10,0},{12,6},{14,4},{1,11},{3,9}... | collective-permute-start | bytes 393224 | tf_op jit(solution)/shard_map/ppermute | solution.py:290
  67.5 1.2 collective-permute-start.9
  69.0 10.1 %collective-permute-start.10 = (bf16[16,32,128]{2,1,0:T(8,128)(2,1)S(1)}, bf16[16,32,128]{2,1,0:T(8,128)(2,1)S(1)}, u32[]{:S(2)}, u32[]{:S(2)}) collective-permute-start(bf16[16,32,128]{2,1,0:T(8,128)(2,1)S(1)} %get-tuple-element.37), channel_id=1, source_target_pairs={{0,14},{2,12},{4,2},{6,0},{8,6},{10,4},{12,10},{14,8},{1,15},{3,13... | collective-permute-start | bytes 393224 | tf_op jit(solution)/shard_map/ppermute | solution.py:290
  79.1 2.5 %collective-permute-done.10.refs_8_ = bf16[16,32,128]{2,1,0:T(8,128)(2,1)S(1)} collective-permute-done((bf16[16,32,128]{2,1,0:T(8,128)(2,1)S(1)}, bf16[16,32,128]{2,1,0:T(8,128)(2,1)S(1)}, u32[]{:S(2)}, u32[]{:S(2)}) %collective-permute-start.10) | collective-permute-done | bytes 131104 | tf_op jit(solution)/shard_map/ppermute | solution.py:290
  81.6 1.3 shard_map.79.field_ref
  82.9 3.9 %shard_map.82 = (f32[8,27,8,128]{3,2,1,0:T(8,128)S(1)}, bf16[8,27,8,128]{3,2,1,0:T(8,128)(2,1)S(1)}) custom-call(bf16[16,32,128]{2,1,0:T(8,128)(2,1)} %shard_map.79.field_ref, bf16[8,16,32,128]{3,2,1,0:T(8,128)(2,1)S(1)} %all_to_all.25.refs_0_.own_ref, bf16[8,16,32,128]{3,2,1,0:T(8,128)(2,1)S(1)} %copy-done.10), custom_call_target="tpu_custom_call" | custom-call | flops 1811939328 | bytes 4194304 | tf_op jit(solution)/shard_map/pallas_call | solution.py:23
  87.5 9.1 %collective-permute-done.20.got_ref = bf16[8,27,8,128]{3,2,1,0:T(8,128)(2,1)S(1)} collective-permute-done((bf16[8,27,8,128]{3,2,1,0:T(8,128)(2,1)S(1)}, bf16[8,27,8,128]{3,2,1,0:T(8,128)(2,1)S(1)}, u32[]{:S(2)}, u32[]{:S(2)}) %collective-permute-start.20) | collective-permute-done | bytes 442400 | tf_op jit(solution)/shard_map/ppermute | solution.py:279
  97.4 8.5 %all-to-all-start.2 = ((bf16[8,27,8,128]{3,2,1,0:T(8,128)(2,1)}), bf16[8,27,8,128]{3,2,1,0:T(8,128)(2,1)S(1)}, u32[]{:S(2)}, u32[]{:S(2)}) async-start(bf16[8,27,8,128]{3,2,1,0:T(8,128)(2,1)} %shard_map.83), calls=%async_computation.2 | async-start | bytes 884736 | tf_op jit(solution)/shard_map/all_to_all | solution.py:275
  105.9 5.0 %shard_map.84 = (f32[8,27,8,128]{3,2,1,0:T(8,128)S(1)}, bf16[8,27,8,128]{3,2,1,0:T(8,128)(2,1)}) custom-call(bf16[16,32,128]{2,1,0:T(8,128)(2,1)S(1)} %bitcast.45, bf16[8,16,32,128]{3,2,1,0:T(8,128)(2,1)S(1)} %all-to-all-done.1.refs_0_.own_ref, bf16[8,16,32,128]{3,2,1,0:T(8,128)(2,1)} %collective-permute-done.1.refs_1_.other_ref), custom_call_target="tpu_custom_call" | custom-call | flops 1811939328 | bytes 4194304 | tf_op jit(solution)/shard_map/pallas_call | solution.py:23
  111.6 7.2 %all-to-all-done.2.pieces_ref = bf16[8,27,8,128]{3,2,1,0:T(8,128)(2,1)S(1)} async-done(((bf16[8,27,8,128]{3,2,1,0:T(8,128)(2,1)}), bf16[8,27,8,128]{3,2,1,0:T(8,128)(2,1)S(1)}, u32[]{:S(2)}, u32[]{:S(2)}) %all-to-all-start.2) | async-done | bytes 442400 | tf_op jit(solution)/shard_map/all_to_all | solution.py:275
  118.8 0.9 collective-permute-done.21.got_ref
  120.5 1.0 copy-done.6
  121.5 1.1 shard_map.85
  122.6 6.9 %all-to-all-start.3 = ((bf16[8,54,8,128]{3,2,1,0:T(8,128)(2,1)}), bf16[8,54,8,128]{3,2,1,0:T(8,128)(2,1)S(1)}, u32[]{:S(2)}, u32[]{:S(2)}) async-start(bf16[8,54,8,128]{3,2,1,0:T(8,128)(2,1)} %shard_map.85), calls=%async_computation.3 | async-start | bytes 1769472 | tf_op jit(solution)/shard_map/all_to_all | solution.py:275
  129.6 20.7 %all-to-all-done.3.both_ref = bf16[8,54,8,128]{3,2,1,0:T(8,128)(2,1)S(1)} async-done(((bf16[8,54,8,128]{3,2,1,0:T(8,128)(2,1)}), bf16[8,54,8,128]{3,2,1,0:T(8,128)(2,1)S(1)}, u32[]{:S(2)}, u32[]{:S(2)}) %all-to-all-start.3) | async-done | bytes 884768 | tf_op jit(solution)/shard_map/all_to_all | solution.py:275
  150.4 1.0 shard_map.86
  151.3 3.5 %all-to-all-start.4 = ((bf16[8,27,8,128]{3,2,1,0:T(8,128)(2,1)}), bf16[8,27,8,128]{3,2,1,0:T(8,128)(2,1)S(1)}, u32[]{:S(2)}, u32[]{:S(2)}) async-start(bf16[8,27,8,128]{3,2,1,0:T(8,128)(2,1)} %get-tuple-element.51), calls=%async_computation.4 | async-start | bytes 884736 | tf_op jit(solution)/shard_map/all_to_all | solution.py:275
  155.5 1.5 copy.32
  157.1 4.8 %shard_map.80 = (bf16[16,32,128]{2,1,0:T(8,128)(2,1)S(1)}, bf16[16,32,128]{2,1,0:T(8,128)(2,1)}, bf16[16,32,128]{2,1,0:T(8,128)(2,1)S(1)}, bf16[16,32,128]{2,1,0...) custom-call(bf16[16,32,128]{2,1,0:T(8,128)(2,1)} %shard_map.79.field, ...), custom_call_target="tpu_custom_call" | custom-call | flops 1811939328 | bytes 4194304 | tf_op jit(solution)/shard_map/pallas_call | solution.py:23
  167.4 1.2 collective-permute-start.23
  168.6 4.2 %collective-permute-start.14 = (bf16[16,32,128]{2,1,0:T(8,128)(2,1)}, bf16[16,32,128]{2,1,0:T(8,128)(2,1)S(1)}, u32[]{:S(2)}, u32[]{:S(2)}) collective-permute-start(bf16[16,32,128]{2,1,0:T(8,128)(2,1)} %copy-done.16), channel_id=1, source_target_pairs={{0,4},{2,6},{4,8},{6,10},{8,12},{10,14},{12,0},{14,2},{1,5},{3,7},... | collective-permute-start | bytes 393224 | tf_op jit(solution)/shard_map/ppermute | solution.py:290
  173.0 1.5 collective-permute-done.13.refs_2_
  174.5 1.0 collective-permute-start.16
  175.5 1.5 collective-permute-done.14.refs_3_
  177.1 2.0 collective-permute-start.17
  179.1 5.1 %collective-permute-done.15.refs_4_ = bf16[16,32,128]{2,1,0:T(8,128)(2,1)S(1)} collective-permute-done((bf16[16,32,128]{2,1,0:T(8,128)(2,1)}, bf16[16,32,128]{2,1,0:T(8,128)(2,1)S(1)}, u32[]{:S(2)}, u32[]{:S(2)}) %collective-permute-start.15) | collective-permute-done | bytes 131104 | tf_op jit(solution)/shard_map/ppermute | solution.py:290
  184.2 1.1 collective-permute-start.19
  185.3 2.4 %collective-permute-done.17.refs_6_ = bf16[16,32,128]{2,1,0:T(8,128)(2,1)S(1)} collective-permute-done((bf16[16,32,128]{2,1,0:T(8,128)(2,1)}, bf16[16,32,128]{2,1,0:T(8,128)(2,1)S(1)}, u32[]{:S(2)}, u32[]{:S(2)}) %collective-permute-start.17) | collective-permute-done | bytes 131104 | tf_op jit(solution)/shard_map/ppermute | solution.py:290
  187.7 1.7 collective-permute-done.18.refs_7_
  189.4 4.4 %collective-permute-done.19.refs_8_ = bf16[16,32,128]{2,1,0:T(8,128)(2,1)S(1)} collective-permute-done((bf16[16,32,128]{2,1,0:T(8,128)(2,1)}, bf16[16,32,128]{2,1,0:T(8,128)(2,1)S(1)}, u32[]{:S(2)}, u32[]{:S(2)}) %collective-permute-start.19) | collective-permute-done | bytes 131104 | tf_op jit(solution)/shard_map/ppermute | solution.py:290
  197.1 4.5 %shard_map.77 = f32[16,32,128]{2,1,0:T(8,128)S(1)} custom-call(bf16[8,16,32,128]{3,2,1,0:T(8,128)(2,1)S(1)} %all-to-all-done.1.refs_0_.own_ref, bf16[8,16,32,128]{3,2,1,0:T(8,128)(2,1)} %collective-permute-done.1.refs_1_.other_ref, bf16[864,512]{1,0:T(8,128)(2,1)} %bitcast.6.refs_2_, bf16[16,32,128]{2,1,0:T(8,128)(2,1)S(1)} %bitcast.34), custom_call_target="tpu_custom_call" | custom-call | flops 1811939328 | bytes 4194304 | tf_op jit(solution)/shard_map/pallas_call | solution.py:23
  202.5 2.0 shard_map.87.refs_0_
  204.5 1.0 shard_map.88
  205.5 1.0 shard_map.89.refs_0_
  206.6 1.0 shard_map.90
  (69 shorter events, 16.0 us)
Async XLA Ops:
  0.6 26.4 %copy-start.1 = (bf16[32,27,512]{2,0,1:T(8,128)(2,1)S(1)}, bf16[32,27,512]{2,0,1:T(8,128)(2,1)}, u32[]{:S(2)}) copy-start(bf16[32,27,512]{2,0,1:T(8,128)(2,1)} %param.5) | copy-start | bytes 2654212
  24.4 2.7 %collective-permute-start = (bf16[8,16,32,128]{3,2,1,0:T(8,128)(2,1)S(1)}, bf16[8,16,32,128]{3,2,1,0:T(8,128)(2,1)S(1)}, u32[]{:S(2)}, u32[]{:S(2)}) collective-permute-start(bf16[8,16,32,128]{3,2,1,0:T(8,128)(2,1)S(1)} %all_to_all.25.refs_0_.own_ref), channel_id=1, source_target_pairs={{0,1},{1,0},{2,3},{3,2},{4,5},{5,4},{6,7},{7,6},{8,9},{9,8},{10,11... | collective-permute-start | bytes 3145736 | tf_op jit(solution)/shard_map/ppermute | solution.py:279
  27.1 4.0 %copy-start.9 = (bf16[8,16,32,128]{3,2,1,0:T(8,128)(2,1)}, bf16[8,16,32,128]{3,2,1,0:T(8,128)(2,1)S(1)}, u32[]{:S(2)}) copy-start(bf16[8,16,32,128]{3,2,1,0:T(8,128)(2,1)S(1)} %collective-permute-done.refs_1_.other_ref) | copy-start | bytes 3145732
  31.1 5.4 %copy-start.17 = (bf16[1,32,4,4,128]{4,3,2,1,0:T(4,128)(2,1)S(1)}, bf16[1,32,4,4,128]{4,3,2,1,0:T(4,128)(2,1)}, u32[]{:S(2)}) copy-start(bf16[1,32,4,4,128]{4,3,2,1,0:T(4,128)(2,1)} %param.7) | copy-start | bytes 393220
  31.1 20.7 %all-to-all-start.1 = ((bf16[8,16,32,128]{3,2,1,0:T(8,128)(2,1)}), bf16[8,16,32,128]{3,2,1,0:T(8,128)(2,1)S(1)}, u32[]{:S(2)}, u32[]{:S(2)}) async-start(bf16[8,16,32,128]{3,2,1,0:T(8,128)(2,1)} %get-tuple-element.28), calls=%async_computation.1 | async-start | bytes 2097152 | tf_op jit(solution)/shard_map/all_to_all | solution.py:275
  36.5 2.8 %collective-permute-start.3 = (bf16[864,512]{1,0:T(8,128)(2,1)}, bf16[864,512]{1,0:T(8,128)(2,1)}, u32[]{:S(2)}, u32[]{:S(2)}) collective-permute-start(bf16[864,512]{1,0:T(8,128)(2,1)} %bitcast.6.refs_2_), channel_id=1, source_target_pairs={{0,1},{1,0},{2,3},{3,2},{4,5},{5,4},{6,7},{7,6},{8,9},{9,8},{10,11... | collective-permute-start | bytes 2654216 | tf_op jit(solution)/shard_map/ppermute | solution.py:279
  36.5 69.4 %copy-start.3 = (bf16[4,4,32,128]{3,2,1,0:T(8,128)(2,1)}, bf16[4,4,32,128]{3,2,1,0:T(8,128)(2,1)S(1)}, u32[]{:S(2)}) copy-start(bf16[4,4,32,128]{3,2,1,0:T(8,128)(2,1)S(1)} %copy.28) | copy-start | bytes 393220
  36.5 15.3 %collective-permute-start.2 = (bf16[16,32,128]{2,1,0:T(8,128)(2,1)S(1)}, bf16[16,32,128]{2,1,0:T(8,128)(2,1)}, u32[]{:S(2)}, u32[]{:S(2)}) collective-permute-start(bf16[16,32,128]{2,1,0:T(8,128)(2,1)S(1)} %bitcast.43), channel_id=1, source_target_pairs={{0,1},{1,0},{2,3},{3,2},{4,5},{5,4},{6,7},{7,6},{8,9},{9,8},{10,11... | collective-permute-start | bytes 393224 | tf_op jit(solution)/shard_map/ppermute | solution.py:279
  51.8 54.1 %collective-permute-start.1 = (bf16[8,16,32,128]{3,2,1,0:T(8,128)(2,1)S(1)}, bf16[8,16,32,128]{3,2,1,0:T(8,128)(2,1)}, u32[]{:S(2)}, u32[]{:S(2)}) collective-permute-start(bf16[8,16,32,128]{3,2,1,0:T(8,128)(2,1)S(1)} %all-to-all-done.1.refs_0_.own_ref), channel_id=1, source_target_pairs={{0,1},{1,0},{2,3},{3,2},{4,5},{5,4},{6,7},{7,6},{8,9},{9,8},{10,11... | collective-permute-start | bytes 3145736 | tf_op jit(solution)/shard_map/ppermute | solution.py:279
  51.8 1.2 copy-start
  53.0 29.9 %copy-start.10 = (bf16[8,16,32,128]{3,2,1,0:T(8,128)(2,1)S(1)}, bf16[8,16,32,128]{3,2,1,0:T(8,128)(2,1)}, u32[]{:S(2)}) copy-start(bf16[8,16,32,128]{3,2,1,0:T(8,128)(2,1)} %copy-done.9) | copy-start | bytes 3145732
  57.1 7.5 %collective-permute-start.4 = (bf16[16,32,128]{2,1,0:T(8,128)(2,1)S(1)}, bf16[16,32,128]{2,1,0:T(8,128)(2,1)S(1)}, u32[]{:S(2)}, u32[]{:S(2)}) collective-permute-start(bf16[16,32,128]{2,1,0:T(8,128)(2,1)S(1)} %get-tuple-element.31), channel_id=1, source_target_pairs={{0,2},{2,0},{4,6},{6,4},{8,10},{10,8},{12,14},{14,12},{1,3},{3,1},... | collective-permute-start | bytes 393224 | tf_op jit(solution)/shard_map/ppermute | solution.py:290
  59.9 7.7 %collective-permute-start.5 = (bf16[16,32,128]{2,1,0:T(8,128)(2,1)S(1)}, bf16[16,32,128]{2,1,0:T(8,128)(2,1)S(1)}, u32[]{:S(2)}, u32[]{:S(2)}) collective-permute-start(bf16[16,32,128]{2,1,0:T(8,128)(2,1)S(1)} %get-tuple-element.32), channel_id=1, source_target_pairs={{0,4},{2,6},{4,8},{6,10},{8,12},{10,14},{12,0},{14,2},{1,5},{3,7},... | collective-permute-start | bytes 393224 | tf_op jit(solution)/shard_map/ppermute | solution.py:290
  59.9 9.1 %collective-permute-start.6 = (bf16[16,32,128]{2,1,0:T(8,128)(2,1)S(1)}, bf16[16,32,128]{2,1,0:T(8,128)(2,1)S(1)}, u32[]{:S(2)}, u32[]{:S(2)}) collective-permute-start(bf16[16,32,128]{2,1,0:T(8,128)(2,1)S(1)} %get-tuple-element.33), channel_id=1, source_target_pairs={{0,6},{2,4},{4,10},{6,8},{8,14},{10,12},{12,2},{14,0},{1,7},{3,5},... | collective-permute-start | bytes 393224 | tf_op jit(solution)/shard_map/ppermute | solution.py:290
  62.7 16.4 %collective-permute-start.7 = (bf16[16,32,128]{2,1,0:T(8,128)(2,1)S(1)}, bf16[16,32,128]{2,1,0:T(8,128)(2,1)S(1)}, u32[]{:S(2)}, u32[]{:S(2)}) collective-permute-start(bf16[16,32,128]{2,1,0:T(8,128)(2,1)S(1)} %get-tuple-element.34), channel_id=1, source_target_pairs={{0,8},{2,10},{4,12},{6,14},{8,0},{10,2},{12,4},{14,6},{1,9},{3,11}... | collective-permute-start | bytes 393224 | tf_op jit(solution)/shard_map/ppermute | solution.py:290
  64.7 14.4 %collective-permute-start.8 = (bf16[16,32,128]{2,1,0:T(8,128)(2,1)S(1)}, bf16[16,32,128]{2,1,0:T(8,128)(2,1)S(1)}, u32[]{:S(2)}, u32[]{:S(2)}) collective-permute-start(bf16[16,32,128]{2,1,0:T(8,128)(2,1)S(1)} %get-tuple-element.35), channel_id=1, source_target_pairs={{0,10},{2,8},{4,14},{6,12},{8,2},{10,0},{12,6},{14,4},{1,11},{3,9}... | collective-permute-start | bytes 393224 | tf_op jit(solution)/shard_map/ppermute | solution.py:290
  67.5 11.5 %collective-permute-start.9 = (bf16[16,32,128]{2,1,0:T(8,128)(2,1)S(1)}, bf16[16,32,128]{2,1,0:T(8,128)(2,1)S(1)}, u32[]{:S(2)}, u32[]{:S(2)}) collective-permute-start(bf16[16,32,128]{2,1,0:T(8,128)(2,1)S(1)} %get-tuple-element.36), channel_id=1, source_target_pairs={{0,12},{2,14},{4,0},{6,2},{8,4},{10,6},{12,8},{14,10},{1,13},{3,15... | collective-permute-start | bytes 393224 | tf_op jit(solution)/shard_map/ppermute | solution.py:290
  69.0 12.6 %collective-permute-start.10 = (bf16[16,32,128]{2,1,0:T(8,128)(2,1)S(1)}, bf16[16,32,128]{2,1,0:T(8,128)(2,1)S(1)}, u32[]{:S(2)}, u32[]{:S(2)}) collective-permute-start(bf16[16,32,128]{2,1,0:T(8,128)(2,1)S(1)} %get-tuple-element.37), channel_id=1, source_target_pairs={{0,14},{2,12},{4,2},{6,0},{8,6},{10,4},{12,10},{14,8},{1,15},{3,13... | collective-permute-start | bytes 393224 | tf_op jit(solution)/shard_map/ppermute | solution.py:290
  86.8 9.8 %collective-permute-start.20 = (bf16[8,27,8,128]{3,2,1,0:T(8,128)(2,1)S(1)}, bf16[8,27,8,128]{3,2,1,0:T(8,128)(2,1)S(1)}, u32[]{:S(2)}, u32[]{:S(2)}) collective-permute-start(bf16[8,27,8,128]{3,2,1,0:T(8,128)(2,1)S(1)} %get-tuple-element.47), channel_id=1, source_target_pairs={{0,128},{128,0},{1,129},{129,1},{2,130},{130,2},{3,131},{131,3},{4... | collective-permute-start | bytes 1327112 | tf_op jit(solution)/shard_map/ppermute | solution.py:279
  97.4 21.4 %all-to-all-start.2 = ((bf16[8,27,8,128]{3,2,1,0:T(8,128)(2,1)}), bf16[8,27,8,128]{3,2,1,0:T(8,128)(2,1)S(1)}, u32[]{:S(2)}, u32[]{:S(2)}) async-start(bf16[8,27,8,128]{3,2,1,0:T(8,128)(2,1)} %shard_map.83), calls=%async_computation.2 | async-start | bytes 884736 | tf_op jit(solution)/shard_map/all_to_all | solution.py:275
  110.9 8.8 %collective-permute-start.21 = (bf16[8,27,8,128]{3,2,1,0:T(8,128)(2,1)}, bf16[8,27,8,128]{3,2,1,0:T(8,128)(2,1)S(1)}, u32[]{:S(2)}, u32[]{:S(2)}) collective-permute-start(bf16[8,27,8,128]{3,2,1,0:T(8,128)(2,1)} %get-tuple-element.49), channel_id=1, source_target_pairs={{0,128},{128,0},{1,129},{129,1},{2,130},{130,2},{3,131},{131,3},{4... | collective-permute-start | bytes 1327112 | tf_op jit(solution)/shard_map/ppermute | solution.py:279
  119.8 0.8 copy-start.5
  120.5 1.0 copy-start.6
  121.5 8.0 %copy-start.2 = (bf16[32,27,512]{2,0,1:T(8,128)(2,1)S(1)}, bf16[32,27,512]{2,0,1:T(8,128)(2,1)}, u32[]{:S(2)}) copy-start(bf16[32,27,512]{2,0,1:T(8,128)(2,1)} %param.5) | copy-start | bytes 2654212
  122.6 27.8 %all-to-all-start.3 = ((bf16[8,54,8,128]{3,2,1,0:T(8,128)(2,1)}), bf16[8,54,8,128]{3,2,1,0:T(8,128)(2,1)S(1)}, u32[]{:S(2)}, u32[]{:S(2)}) async-start(bf16[8,54,8,128]{3,2,1,0:T(8,128)(2,1)} %shard_map.85), calls=%async_computation.3 | async-start | bytes 1769472 | tf_op jit(solution)/shard_map/all_to_all | solution.py:275
  129.5 26.0 %collective-permute-start.12 = (bf16[864,512]{1,0:T(8,128)(2,1)S(1)}, bf16[864,512]{1,0:T(8,128)(2,1)}, u32[]{:S(2)}, u32[]{:S(2)}) collective-permute-start(bf16[864,512]{1,0:T(8,128)(2,1)S(1)} %bitcast.41), channel_id=1, source_target_pairs={{0,1},{1,0},{2,3},{3,2},{4,5},{5,4},{6,7},{7,6},{8,9},{9,8},{10,11... | collective-permute-start | bytes 2654216 | tf_op jit(solution)/shard_map/ppermute | solution.py:279
  151.3 16.1 %all-to-all-start.4 = ((bf16[8,27,8,128]{3,2,1,0:T(8,128)(2,1)}), bf16[8,27,8,128]{3,2,1,0:T(8,128)(2,1)S(1)}, u32[]{:S(2)}, u32[]{:S(2)}) async-start(bf16[8,27,8,128]{3,2,1,0:T(8,128)(2,1)} %get-tuple-element.51), calls=%async_computation.4 | async-start | bytes 884736 | tf_op jit(solution)/shard_map/all_to_all | solution.py:275
  154.8 2.3 %collective-permute-start.11 = (bf16[16,32,128]{2,1,0:T(8,128)(2,1)}, bf16[16,32,128]{2,1,0:T(8,128)(2,1)}, u32[]{:S(2)}, u32[]{:S(2)}) collective-permute-start(bf16[16,32,128]{2,1,0:T(8,128)(2,1)} %shard_map.79.field_ref), channel_id=1, source_target_pairs={{0,1},{1,0},{2,3},{3,2},{4,5},{5,4},{6,7},{7,6},{8,9},{9,8},{10,11... | collective-permute-start | bytes 393224 | tf_op jit(solution)/shard_map/ppermute | solution.py:279
  161.9 0.7 copy-start.7
  162.5 0.7 copy-start.11
  163.2 0.7 copy-start.12
  163.8 0.6 copy-start.13
  164.5 0.6 copy-start.14
  165.1 0.7 copy-start.15
  165.8 0.6 copy-start.16
  166.4 8.1 %collective-permute-start.13 = (bf16[16,32,128]{2,1,0:T(8,128)(2,1)}, bf16[16,32,128]{2,1,0:T(8,128)(2,1)S(1)}, u32[]{:S(2)}, u32[]{:S(2)}) collective-permute-start(bf16[16,32,128]{2,1,0:T(8,128)(2,1)} %get-tuple-element.39), channel_id=1, source_target_pairs={{0,2},{2,0},{4,6},{6,4},{8,10},{10,8},{12,14},{14,12},{1,3},{3,1},... | collective-permute-start | bytes 393224 | tf_op jit(solution)/shard_map/ppermute | solution.py:290
  166.6 37.9 %collective-permute-start.22 = (bf16[8,27,8,128]{3,2,1,0:T(8,128)(2,1)}, bf16[8,27,8,128]{3,2,1,0:T(8,128)(2,1)S(1)}, u32[]{:S(2)}, u32[]{:S(2)}) collective-permute-start(bf16[8,27,8,128]{3,2,1,0:T(8,128)(2,1)} %get-tuple-element.50.pieces_ref), channel_id=1, source_target_pairs={{0,128},{128,0},{1,129},{129,1},{2,130},{130,2},{3,131},{131,3},{4... | collective-permute-start | bytes 1327112 | tf_op jit(solution)/shard_map/ppermute | solution.py:279
  167.4 39.2 %collective-permute-start.23 = (bf16[8,27,8,128]{3,2,1,0:T(8,128)(2,1)S(1)}, bf16[8,27,8,128]{3,2,1,0:T(8,128)(2,1)S(1)}, u32[]{:S(2)}, u32[]{:S(2)}) collective-permute-start(bf16[8,27,8,128]{3,2,1,0:T(8,128)(2,1)S(1)} %all-to-all-done.4.pieces_ref), channel_id=1, source_target_pairs={{0,128},{128,0},{1,129},{129,1},{2,130},{130,2},{3,131},{131,3},{4... | collective-permute-start | bytes 1327112 | tf_op jit(solution)/shard_map/ppermute | solution.py:279
  168.6 8.4 %collective-permute-start.14 = (bf16[16,32,128]{2,1,0:T(8,128)(2,1)}, bf16[16,32,128]{2,1,0:T(8,128)(2,1)S(1)}, u32[]{:S(2)}, u32[]{:S(2)}) collective-permute-start(bf16[16,32,128]{2,1,0:T(8,128)(2,1)} %copy-done.16), channel_id=1, source_target_pairs={{0,4},{2,6},{4,8},{6,10},{8,12},{10,14},{12,0},{14,2},{1,5},{3,7},... | collective-permute-start | bytes 393224 | tf_op jit(solution)/shard_map/ppermute | solution.py:290
  172.9 11.3 %collective-permute-start.15 = (bf16[16,32,128]{2,1,0:T(8,128)(2,1)}, bf16[16,32,128]{2,1,0:T(8,128)(2,1)S(1)}, u32[]{:S(2)}, u32[]{:S(2)}) collective-permute-start(bf16[16,32,128]{2,1,0:T(8,128)(2,1)} %copy-done.15), channel_id=1, source_target_pairs={{0,6},{2,4},{4,10},{6,8},{8,14},{10,12},{12,2},{14,0},{1,7},{3,5},... | collective-permute-start | bytes 393224 | tf_op jit(solution)/shard_map/ppermute | solution.py:290
  174.5 9.7 %collective-permute-start.16 = (bf16[16,32,128]{2,1,0:T(8,128)(2,1)}, bf16[16,32,128]{2,1,0:T(8,128)(2,1)S(1)}, u32[]{:S(2)}, u32[]{:S(2)}) collective-permute-start(bf16[16,32,128]{2,1,0:T(8,128)(2,1)} %copy-done.14), channel_id=1, source_target_pairs={{0,8},{2,10},{4,12},{6,14},{8,0},{10,2},{12,4},{14,6},{1,9},{3,11}... | collective-permute-start | bytes 393224 | tf_op jit(solution)/shard_map/ppermute | solution.py:290
  177.1 10.6 %collective-permute-start.17 = (bf16[16,32,128]{2,1,0:T(8,128)(2,1)}, bf16[16,32,128]{2,1,0:T(8,128)(2,1)S(1)}, u32[]{:S(2)}, u32[]{:S(2)}) collective-permute-start(bf16[16,32,128]{2,1,0:T(8,128)(2,1)} %copy-done.13), channel_id=1, source_target_pairs={{0,10},{2,8},{4,14},{6,12},{8,2},{10,0},{12,6},{14,4},{1,11},{3,9}... | collective-permute-start | bytes 393224 | tf_op jit(solution)/shard_map/ppermute | solution.py:290
  184.2 5.2 %collective-permute-start.18 = (bf16[16,32,128]{2,1,0:T(8,128)(2,1)}, bf16[16,32,128]{2,1,0:T(8,128)(2,1)S(1)}, u32[]{:S(2)}, u32[]{:S(2)}) collective-permute-start(bf16[16,32,128]{2,1,0:T(8,128)(2,1)} %copy-done.12), channel_id=1, source_target_pairs={{0,12},{2,14},{4,0},{6,2},{8,4},{10,6},{12,8},{14,10},{1,13},{3,15... | collective-permute-start | bytes 393224 | tf_op jit(solution)/shard_map/ppermute | solution.py:290
  184.2 9.6 %collective-permute-start.19 = (bf16[16,32,128]{2,1,0:T(8,128)(2,1)}, bf16[16,32,128]{2,1,0:T(8,128)(2,1)S(1)}, u32[]{:S(2)}, u32[]{:S(2)}) collective-permute-start(bf16[16,32,128]{2,1,0:T(8,128)(2,1)} %copy-done.11), channel_id=1, source_target_pairs={{0,14},{2,12},{4,2},{6,0},{8,6},{10,4},{12,10},{14,8},{1,15},{3,13... | collective-permute-start | bytes 393224 | tf_op jit(solution)/shard_map/ppermute | solution.py:290
  193.8 0.9 copy-start.4
  194.7 0.9 copy-start.8

commit v4 on v3

--- a/solution.py
+++ b/solution.py
@@ -10,6 +10,7 @@
 
 XY = ("x", "yh")
 SWAP = [(0, 1), (1, 0)]
+RINGS = [[z * 2 for z in range(8)], [(z + 4) % 8 * 2 + 1 for z in range(8)]]
 F32 = jnp.float32
 BF16 = jnp.bfloat16
 TAPS = [(i, j, k) for i in range(3) for j in range(3) for k in range(3)]
@@ -272,7 +273,9 @@
 
 
 def exchange(value, axes):
-    return lax.all_to_all(value, axes, 0, 0, tiled=True)
+    groups = RINGS if axes == "z" else None
+    axes = ("z", "core") if axes == "z" else axes
+    return lax.all_to_all(value, axes, 0, 0, axis_index_groups=groups, tiled=True)
 
 
 def swap(value, axis):

time: 210 us -> 212 us (level)
  starting transfers between devices: 58.2 us -> 64.4 us
  waiting for transfers between devices: 71.6 us -> 68.5 us
    ppermute x14, waiting for transfers between devices: 19.8 us -> 15.4 us  [input_partial(): pieces.append(lax.ppermute(sends[k], XY, perm))]
    ppermute x14, starting transfers between devices: 29.9 us -> 33.1 us  [input_partial(): pieces.append(lax.ppermute(sends[k], XY, perm))]
    ppermute x10, waiting for transfers between devices: 13.3 us -> 15.8 us  [swap(): return lax.ppermute(value, axis, SWAP)]
  transfers between devices with their start and end apart: 28 -> 28, of which waited for: 17 -> 13; matrix products, arithmetic and copies ran while one was open for 4% -> 4% of each run, Pallas kernels for 14% -> 14%
where the time goes in v4:
time: 212 us; the launch traced here: 211 us
  waiting for transfers between devices  68.5 us (32%)
  starting transfers between devices  64.4 us (30%)
  Pallas kernels  36.6 us (17%)
  blocking collectives  22.4 us (11%)
  local copies, waits for them, and re-layouts  18 us (8%)
    all_to_all x4, waiting for transfers between devices, exchange(): lax.all_to_all(value, axes, 0, 0, axis_index_groups=groups, tiled=True)  37.3 us
    ppermute x14, starting transfers between devices, input_partial(): pieces.append(lax.ppermute(sends[k], XY, perm))  33.1 us
    pallas_call x12, Pallas kernels, call(): pl.pallas_call(body, out_shape=tuple((jax.ShapeDtypeStruct(*o) for o in o...  31.5 us
    all_to_all x4, starting transfers between devices, exchange(): lax.all_to_all(value, axes, 0, 0, axis_index_groups=groups, tiled=True)  25.3 us
    all_to_all x1, blocking collectives, exchange(): lax.all_to_all(value, axes, 0, 0, axis_index_groups=groups, tiled=True)  22.4 us
    ppermute x10, waiting for transfers between devices, swap(): return lax.ppermute(value, axis, SWAP)  15.8 us
    ppermute x14, waiting for transfers between devices, input_partial(): pieces.append(lax.ppermute(sends[k], XY, perm))  15.4 us
    unnamed x36, local copies, waits for them, and re-layouts  9.32 us
  transfers between devices with their start and end apart: 28, of which 13 were waited for; matrix products, arithmetic and copies ran while one was open for 4% of the time, Pallas kernels for 14%

profile of v4, /device:TPU:2, one launch (start us, length us, event | category | flops | bytes accessed | tf_op | source)
XLA Modules:
  0.0 210.9 jit_solution(4653341732945808012)
XLA Ops:
  0.6 1.0 copy.26
  2.0 22.4 %all_to_all.25.refs_0_.own_ref = bf16[8,16,32,128]{3,2,1,0:T(8,128)(2,1)S(1)} all-to-all(bf16[8,16,32,128]{3,2,1,0:T(8,128)(2,1)S(1)} %shard_map.75), channel_id=1, replica_groups=mesh['yl'=2,'z'=8,'x'=4,'yh'=2,'core'=2] {'x','yh'}, dimensions={0} | all-to-all | bytes 2097152 | tf_op jit(solution)/shard_map/all_to_all | solution.py:278
  24.4 2.7 %collective-permute-done.refs_1_.other_ref = bf16[8,16,32,128]{3,2,1,0:T(8,128)(2,1)S(1)} collective-permute-done((bf16[8,16,32,128]{3,2,1,0:T(8,128)(2,1)S(1)}, bf16[8,16,32,128]{3,2,1,0:T(8,128)(2,1)S(1)}, u32[]{:S(2)}, u32[]{:S(2)}) %collective-permute-start) | collective-permute-done | bytes 1048608 | tf_op jit(solution)/shard_map/ppermute | solution.py:282
  27.1 4.0 %shard_map.76 = (f32[16,32,128]{2,1,0:T(8,128)S(1)}, bf16[8,16,32,128]{3,2,1,0:T(8,128)(2,1)}) custom-call(bf16[8,16,32,128]{3,2,1,0:T(8,128)(2,1)S(1)} %all_to_all.25.refs_0_.own_ref, bf16[8,16,32,128]{3,2,1,0:T(8,128)(2,1)S(1)} %collective-permute-done.refs_1_.other_ref, bf16[864,512]{1,0:T(8,128)(2,1)S(1)} %bitcast.40), custom_call_target="tpu_custom_call" | custom-call | flops 1811939328 | bytes 4194304 | tf_op jit(solution)/shard_map/pallas_call | solution.py:24
  31.1 5.3 %all-to-all-start.1 = ((bf16[8,16,32,128]{3,2,1,0:T(8,128)(2,1)}), bf16[8,16,32,128]{3,2,1,0:T(8,128)(2,1)S(1)}, u32[]{:S(2)}, u32[]{:S(2)}) async-start(bf16[8,16,32,128]{3,2,1,0:T(8,128)(2,1)} %get-tuple-element.28), calls=%async_computation.1 | async-start | bytes 2097152 | tf_op jit(solution)/shard_map/all_to_all | solution.py:278
  37.1 1.5 copy.29
  39.2 2.2 %copy.30 = bf16[864,512]{0,1:T(8,128)(2,1)} copy(bf16[864,512]{1,0:T(8,128)(2,1)} %collective-permute-done.3) | data formatting | bytes 1769472 | tf_op jit(solution)/shard_map/ppermute | solution.py:282
  41.5 10.3 %all-to-all-done.1.refs_0_.own_ref = bf16[8,16,32,128]{3,2,1,0:T(8,128)(2,1)S(1)} async-done(((bf16[8,16,32,128]{3,2,1,0:T(8,128)(2,1)}), bf16[8,16,32,128]{3,2,1,0:T(8,128)(2,1)S(1)}, u32[]{:S(2)}, u32[]{:S(2)}) %all-to-all-start.1) | async-done | bytes 1048608 | tf_op jit(solution)/shard_map/all_to_all | solution.py:278
  51.8 1.2 copy-done
  53.0 4.2 %shard_map.78 = (bf16[16,32,128]{2,1,0:T(8,128)(2,1)S(1)}, bf16[16,32,128]{2,1,0:T(8,128)(2,1)S(1)}, bf16[16,32,128]{2,1,0:T(8,128)(2,1)S(1)}, bf16[16,32,128]{2...) custom-call(bf16[16,32,128]{2,1,0:T(8,128)(2,1)S(1)} %bitcast.44, ...), custom_call_target="tpu_custom_call" | custom-call | flops 1811939328 | bytes 4194304 | tf_op jit(solution)/shard_map/pallas_call | solution.py:24
  57.1 2.7 %collective-permute-start.4 = (bf16[16,32,128]{2,1,0:T(8,128)(2,1)S(1)}, bf16[16,32,128]{2,1,0:T(8,128)(2,1)S(1)}, u32[]{:S(2)}, u32[]{:S(2)}) collective-permute-start(bf16[16,32,128]{2,1,0:T(8,128)(2,1)S(1)} %get-tuple-element.31), channel_id=1, source_target_pairs={{0,2},{2,0},{4,6},{6,4},{8,10},{10,8},{12,14},{14,12},{1,3},{3,1},... | collective-permute-start | bytes 393224 | tf_op jit(solution)/shard_map/ppermute | solution.py:293
  59.9 2.8 %collective-permute-start.6 = (bf16[16,32,128]{2,1,0:T(8,128)(2,1)S(1)}, bf16[16,32,128]{2,1,0:T(8,128)(2,1)S(1)}, u32[]{:S(2)}, u32[]{:S(2)}) collective-permute-start(bf16[16,32,128]{2,1,0:T(8,128)(2,1)S(1)} %get-tuple-element.33), channel_id=1, source_target_pairs={{0,6},{2,4},{4,10},{6,8},{8,14},{10,12},{12,2},{14,0},{1,7},{3,5},... | collective-permute-start | bytes 393224 | tf_op jit(solution)/shard_map/ppermute | solution.py:293
  62.7 1.6 collective-permute-start.7
  64.7 2.9 %collective-permute-start.8 = (bf16[16,32,128]{2,1,0:T(8,128)(2,1)S(1)}, bf16[16,32,128]{2,1,0:T(8,128)(2,1)S(1)}, u32[]{:S(2)}, u32[]{:S(2)}) collective-permute-start(bf16[16,32,128]{2,1,0:T(8,128)(2,1)S(1)} %get-tuple-element.35), channel_id=1, source_target_pairs={{0,10},{2,8},{4,14},{6,12},{8,2},{10,0},{12,6},{14,4},{1,11},{3,9}... | collective-permute-start | bytes 393224 | tf_op jit(solution)/shard_map/ppermute | solution.py:293
  67.5 1.2 collective-permute-start.9
  69.0 10.1 %collective-permute-start.10 = (bf16[16,32,128]{2,1,0:T(8,128)(2,1)S(1)}, bf16[16,32,128]{2,1,0:T(8,128)(2,1)S(1)}, u32[]{:S(2)}, u32[]{:S(2)}) collective-permute-start(bf16[16,32,128]{2,1,0:T(8,128)(2,1)S(1)} %get-tuple-element.37), channel_id=1, source_target_pairs={{0,14},{2,12},{4,2},{6,0},{8,6},{10,4},{12,10},{14,8},{1,15},{3,13... | collective-permute-start | bytes 393224 | tf_op jit(solution)/shard_map/ppermute | solution.py:293
  79.1 2.5 %collective-permute-done.10.refs_8_ = bf16[16,32,128]{2,1,0:T(8,128)(2,1)S(1)} collective-permute-done((bf16[16,32,128]{2,1,0:T(8,128)(2,1)S(1)}, bf16[16,32,128]{2,1,0:T(8,128)(2,1)S(1)}, u32[]{:S(2)}, u32[]{:S(2)}) %collective-permute-start.10) | collective-permute-done | bytes 131104 | tf_op jit(solution)/shard_map/ppermute | solution.py:293
  81.6 1.3 shard_map.79.field_ref
  82.9 3.9 %shard_map.82 = (f32[8,27,8,128]{3,2,1,0:T(8,128)S(1)}, bf16[8,27,8,128]{3,2,1,0:T(8,128)(2,1)S(1)}) custom-call(bf16[16,32,128]{2,1,0:T(8,128)(2,1)} %shard_map.79.field_ref, bf16[8,16,32,128]{3,2,1,0:T(8,128)(2,1)S(1)} %all_to_all.25.refs_0_.own_ref, bf16[8,16,32,128]{3,2,1,0:T(8,128)(2,1)S(1)} %copy-done.10), custom_call_target="tpu_custom_call" | custom-call | flops 1811939328 | bytes 4194304 | tf_op jit(solution)/shard_map/pallas_call | solution.py:24
  87.5 9.1 %collective-permute-done.20.got_ref = bf16[8,27,8,128]{3,2,1,0:T(8,128)(2,1)S(1)} collective-permute-done((bf16[8,27,8,128]{3,2,1,0:T(8,128)(2,1)S(1)}, bf16[8,27,8,128]{3,2,1,0:T(8,128)(2,1)S(1)}, u32[]{:S(2)}, u32[]{:S(2)}) %collective-permute-start.20) | collective-permute-done | bytes 442400 | tf_op jit(solution)/shard_map/ppermute | solution.py:282
  97.4 8.5 %all-to-all-start.2 = ((bf16[8,27,8,128]{3,2,1,0:T(8,128)(2,1)}), bf16[8,27,8,128]{3,2,1,0:T(8,128)(2,1)S(1)}, u32[]{:S(2)}, u32[]{:S(2)}) async-start(bf16[8,27,8,128]{3,2,1,0:T(8,128)(2,1)} %shard_map.83), calls=%async_computation.2 | async-start | bytes 884736 | tf_op jit(solution)/shard_map/all_to_all | solution.py:278
  105.9 5.0 %shard_map.84 = (f32[8,27,8,128]{3,2,1,0:T(8,128)S(1)}, bf16[8,27,8,128]{3,2,1,0:T(8,128)(2,1)}) custom-call(bf16[16,32,128]{2,1,0:T(8,128)(2,1)S(1)} %bitcast.45, bf16[8,16,32,128]{3,2,1,0:T(8,128)(2,1)S(1)} %all-to-all-done.1.refs_0_.own_ref, bf16[8,16,32,128]{3,2,1,0:T(8,128)(2,1)} %collective-permute-done.1.refs_1_.other_ref), custom_call_target="tpu_custom_call" | custom-call | flops 1811939328 | bytes 4194304 | tf_op jit(solution)/shard_map/pallas_call | solution.py:24
  111.6 6.8 %all-to-all-done.2.pieces_ref = bf16[8,27,8,128]{3,2,1,0:T(8,128)(2,1)S(1)} async-done(((bf16[8,27,8,128]{3,2,1,0:T(8,128)(2,1)}), bf16[8,27,8,128]{3,2,1,0:T(8,128)(2,1)S(1)}, u32[]{:S(2)}, u32[]{:S(2)}) %all-to-all-start.2) | async-done | bytes 442400 | tf_op jit(solution)/shard_map/all_to_all | solution.py:278
  118.4 3.4 %collective-permute-done.21.got_ref = bf16[8,27,8,128]{3,2,1,0:T(8,128)(2,1)S(1)} collective-permute-done((bf16[8,27,8,128]{3,2,1,0:T(8,128)(2,1)}, bf16[8,27,8,128]{3,2,1,0:T(8,128)(2,1)S(1)}, u32[]{:S(2)}, u32[]{:S(2)}) %collective-permute-start.21) | collective-permute-done | bytes 442400 | tf_op jit(solution)/shard_map/ppermute | solution.py:282
  122.6 1.0 copy-done.6
  123.6 1.1 shard_map.85
  124.7 4.8 %all-to-all-start.3 = ((bf16[8,54,8,128]{3,2,1,0:T(8,128)(2,1)}), bf16[8,54,8,128]{3,2,1,0:T(8,128)(2,1)S(1)}, u32[]{:S(2)}, u32[]{:S(2)}) async-start(bf16[8,54,8,128]{3,2,1,0:T(8,128)(2,1)} %shard_map.85), calls=%async_computation.3 | async-start | bytes 1769472 | tf_op jit(solution)/shard_map/all_to_all | solution.py:278
  129.6 20.1 %all-to-all-done.3.both_ref = bf16[8,54,8,128]{3,2,1,0:T(8,128)(2,1)S(1)} async-done(((bf16[8,54,8,128]{3,2,1,0:T(8,128)(2,1)}), bf16[8,54,8,128]{3,2,1,0:T(8,128)(2,1)S(1)}, u32[]{:S(2)}, u32[]{:S(2)}) %all-to-all-start.3) | async-done | bytes 884768 | tf_op jit(solution)/shard_map/all_to_all | solution.py:278
  149.7 1.0 shard_map.86
  150.7 6.7 %all-to-all-start.4 = ((bf16[8,27,8,128]{3,2,1,0:T(8,128)(2,1)}), bf16[8,27,8,128]{3,2,1,0:T(8,128)(2,1)S(1)}, u32[]{:S(2)}, u32[]{:S(2)}) async-start(bf16[8,27,8,128]{3,2,1,0:T(8,128)(2,1)} %get-tuple-element.51), calls=%async_computation.4 | async-start | bytes 884736 | tf_op jit(solution)/shard_map/all_to_all | solution.py:278
  157.4 1.9 collective-permute-start.11
  159.9 1.5 copy.32
  161.4 4.8 %shard_map.80 = (bf16[16,32,128]{2,1,0:T(8,128)(2,1)S(1)}, bf16[16,32,128]{2,1,0:T(8,128)(2,1)}, bf16[16,32,128]{2,1,0:T(8,128)(2,1)S(1)}, bf16[16,32,128]{2,1,0...) custom-call(bf16[16,32,128]{2,1,0:T(8,128)(2,1)} %shard_map.79.field, ...), custom_call_target="tpu_custom_call" | custom-call | flops 1811939328 | bytes 4194304 | tf_op jit(solution)/shard_map/pallas_call | solution.py:24
  171.4 1.4 collective-permute-start.23
  172.8 2.0 collective-permute-start.14
  174.9 3.9 %collective-permute-done.13.refs_2_ = bf16[16,32,128]{2,1,0:T(8,128)(2,1)S(1)} collective-permute-done((bf16[16,32,128]{2,1,0:T(8,128)(2,1)}, bf16[16,32,128]{2,1,0:T(8,128)(2,1)S(1)}, u32[]{:S(2)}, u32[]{:S(2)}) %collective-permute-start.13) | collective-permute-done | bytes 131104 | tf_op jit(solution)/shard_map/ppermute | solution.py:293
  178.8 1.0 collective-permute-start.16
  179.9 2.0 collective-permute-start.17
  181.8 3.5 %collective-permute-done.15.refs_4_ = bf16[16,32,128]{2,1,0:T(8,128)(2,1)S(1)} collective-permute-done((bf16[16,32,128]{2,1,0:T(8,128)(2,1)}, bf16[16,32,128]{2,1,0:T(8,128)(2,1)S(1)}, u32[]{:S(2)}, u32[]{:S(2)}) %collective-permute-start.15) | collective-permute-done | bytes 131104 | tf_op jit(solution)/shard_map/ppermute | solution.py:293
  185.3 3.9 %collective-permute-start.18 = (bf16[16,32,128]{2,1,0:T(8,128)(2,1)}, bf16[16,32,128]{2,1,0:T(8,128)(2,1)S(1)}, u32[]{:S(2)}, u32[]{:S(2)}) collective-permute-start(bf16[16,32,128]{2,1,0:T(8,128)(2,1)} %copy-done.12), channel_id=1, source_target_pairs={{0,12},{2,14},{4,0},{6,2},{8,4},{10,6},{12,8},{14,10},{1,13},{3,15... | collective-permute-start | bytes 393224 | tf_op jit(solution)/shard_map/ppermute | solution.py:293
  189.2 2.9 %collective-permute-start.19 = (bf16[16,32,128]{2,1,0:T(8,128)(2,1)}, bf16[16,32,128]{2,1,0:T(8,128)(2,1)S(1)}, u32[]{:S(2)}, u32[]{:S(2)}) collective-permute-start(bf16[16,32,128]{2,1,0:T(8,128)(2,1)} %copy-done.11), channel_id=1, source_target_pairs={{0,14},{2,12},{4,2},{6,0},{8,6},{10,4},{12,10},{14,8},{1,15},{3,13... | collective-permute-start | bytes 393224 | tf_op jit(solution)/shard_map/ppermute | solution.py:293
  192.1 4.8 %collective-permute-done.19.refs_8_ = bf16[16,32,128]{2,1,0:T(8,128)(2,1)S(1)} collective-permute-done((bf16[16,32,128]{2,1,0:T(8,128)(2,1)}, bf16[16,32,128]{2,1,0:T(8,128)(2,1)S(1)}, u32[]{:S(2)}, u32[]{:S(2)}) %collective-permute-start.19) | collective-permute-done | bytes 131104 | tf_op jit(solution)/shard_map/ppermute | solution.py:293
  196.9 0.9 copy-done.4
  200.2 4.5 %shard_map.77 = f32[16,32,128]{2,1,0:T(8,128)S(1)} custom-call(bf16[8,16,32,128]{3,2,1,0:T(8,128)(2,1)S(1)} %all-to-all-done.1.refs_0_.own_ref, bf16[8,16,32,128]{3,2,1,0:T(8,128)(2,1)} %collective-permute-done.1.refs_1_.other_ref, bf16[864,512]{1,0:T(8,128)(2,1)} %bitcast.6.refs_2_, bf16[16,32,128]{2,1,0:T(8,128)(2,1)S(1)} %bitcast.34), custom_call_target="tpu_custom_call" | custom-call | flops 1811939328 | bytes 4194304 | tf_op jit(solution)/shard_map/pallas_call | solution.py:24
  205.6 2.0 shard_map.87.refs_0_
  207.6 1.0 shard_map.88
  208.6 1.0 shard_map.89.refs_0_
  209.7 1.0 shard_map.90
  (69 shorter events, 14.6 us)
Async XLA Ops:
  0.6 26.4 %copy-start.1 = (bf16[32,27,512]{2,0,1:T(8,128)(2,1)S(1)}, bf16[32,27,512]{2,0,1:T(8,128)(2,1)}, u32[]{:S(2)}) copy-start(bf16[32,27,512]{2,0,1:T(8,128)(2,1)} %param.5) | copy-start | bytes 2654212
  24.4 2.7 %collective-permute-start = (bf16[8,16,32,128]{3,2,1,0:T(8,128)(2,1)S(1)}, bf16[8,16,32,128]{3,2,1,0:T(8,128)(2,1)S(1)}, u32[]{:S(2)}, u32[]{:S(2)}) collective-permute-start(bf16[8,16,32,128]{3,2,1,0:T(8,128)(2,1)S(1)} %all_to_all.25.refs_0_.own_ref), channel_id=1, source_target_pairs={{0,1},{1,0},{2,3},{3,2},{4,5},{5,4},{6,7},{7,6},{8,9},{9,8},{10,11... | collective-permute-start | bytes 3145736 | tf_op jit(solution)/shard_map/ppermute | solution.py:282
  27.1 4.0 %copy-start.9 = (bf16[8,16,32,128]{3,2,1,0:T(8,128)(2,1)}, bf16[8,16,32,128]{3,2,1,0:T(8,128)(2,1)S(1)}, u32[]{:S(2)}) copy-start(bf16[8,16,32,128]{3,2,1,0:T(8,128)(2,1)S(1)} %collective-permute-done.refs_1_.other_ref) | copy-start | bytes 3145732
  31.1 5.4 %copy-start.17 = (bf16[1,32,4,4,128]{4,3,2,1,0:T(4,128)(2,1)S(1)}, bf16[1,32,4,4,128]{4,3,2,1,0:T(4,128)(2,1)}, u32[]{:S(2)}) copy-start(bf16[1,32,4,4,128]{4,3,2,1,0:T(4,128)(2,1)} %param.7) | copy-start | bytes 393220
  31.1 20.7 %all-to-all-start.1 = ((bf16[8,16,32,128]{3,2,1,0:T(8,128)(2,1)}), bf16[8,16,32,128]{3,2,1,0:T(8,128)(2,1)S(1)}, u32[]{:S(2)}, u32[]{:S(2)}) async-start(bf16[8,16,32,128]{3,2,1,0:T(8,128)(2,1)} %get-tuple-element.28), calls=%async_computation.1 | async-start | bytes 2097152 | tf_op jit(solution)/shard_map/all_to_all | solution.py:278
  36.5 2.8 %collective-permute-start.3 = (bf16[864,512]{1,0:T(8,128)(2,1)}, bf16[864,512]{1,0:T(8,128)(2,1)}, u32[]{:S(2)}, u32[]{:S(2)}) collective-permute-start(bf16[864,512]{1,0:T(8,128)(2,1)} %bitcast.6.refs_2_), channel_id=1, source_target_pairs={{0,1},{1,0},{2,3},{3,2},{4,5},{5,4},{6,7},{7,6},{8,9},{9,8},{10,11... | collective-permute-start | bytes 2654216 | tf_op jit(solution)/shard_map/ppermute | solution.py:282
  36.5 69.4 %copy-start.3 = (bf16[4,4,32,128]{3,2,1,0:T(8,128)(2,1)}, bf16[4,4,32,128]{3,2,1,0:T(8,128)(2,1)S(1)}, u32[]{:S(2)}) copy-start(bf16[4,4,32,128]{3,2,1,0:T(8,128)(2,1)S(1)} %copy.28) | copy-start | bytes 393220
  36.5 15.3 %collective-permute-start.2 = (bf16[16,32,128]{2,1,0:T(8,128)(2,1)S(1)}, bf16[16,32,128]{2,1,0:T(8,128)(2,1)}, u32[]{:S(2)}, u32[]{:S(2)}) collective-permute-start(bf16[16,32,128]{2,1,0:T(8,128)(2,1)S(1)} %bitcast.43), channel_id=1, source_target_pairs={{0,1},{1,0},{2,3},{3,2},{4,5},{5,4},{6,7},{7,6},{8,9},{9,8},{10,11... | collective-permute-start | bytes 393224 | tf_op jit(solution)/shard_map/ppermute | solution.py:282
  51.8 54.1 %collective-permute-start.1 = (bf16[8,16,32,128]{3,2,1,0:T(8,128)(2,1)S(1)}, bf16[8,16,32,128]{3,2,1,0:T(8,128)(2,1)}, u32[]{:S(2)}, u32[]{:S(2)}) collective-permute-start(bf16[8,16,32,128]{3,2,1,0:T(8,128)(2,1)S(1)} %all-to-all-done.1.refs_0_.own_ref), channel_id=1, source_target_pairs={{0,1},{1,0},{2,3},{3,2},{4,5},{5,4},{6,7},{7,6},{8,9},{9,8},{10,11... | collective-permute-start | bytes 3145736 | tf_op jit(solution)/shard_map/ppermute | solution.py:282
  51.8 1.2 copy-start
  53.0 29.9 %copy-start.10 = (bf16[8,16,32,128]{3,2,1,0:T(8,128)(2,1)S(1)}, bf16[8,16,32,128]{3,2,1,0:T(8,128)(2,1)}, u32[]{:S(2)}) copy-start(bf16[8,16,32,128]{3,2,1,0:T(8,128)(2,1)} %copy-done.9) | copy-start | bytes 3145732
  57.1 7.5 %collective-permute-start.4 = (bf16[16,32,128]{2,1,0:T(8,128)(2,1)S(1)}, bf16[16,32,128]{2,1,0:T(8,128)(2,1)S(1)}, u32[]{:S(2)}, u32[]{:S(2)}) collective-permute-start(bf16[16,32,128]{2,1,0:T(8,128)(2,1)S(1)} %get-tuple-element.31), channel_id=1, source_target_pairs={{0,2},{2,0},{4,6},{6,4},{8,10},{10,8},{12,14},{14,12},{1,3},{3,1},... | collective-permute-start | bytes 393224 | tf_op jit(solution)/shard_map/ppermute | solution.py:293
  59.9 7.7 %collective-permute-start.5 = (bf16[16,32,128]{2,1,0:T(8,128)(2,1)S(1)}, bf16[16,32,128]{2,1,0:T(8,128)(2,1)S(1)}, u32[]{:S(2)}, u32[]{:S(2)}) collective-permute-start(bf16[16,32,128]{2,1,0:T(8,128)(2,1)S(1)} %get-tuple-element.32), channel_id=1, source_target_pairs={{0,4},{2,6},{4,8},{6,10},{8,12},{10,14},{12,0},{14,2},{1,5},{3,7},... | collective-permute-start | bytes 393224 | tf_op jit(solution)/shard_map/ppermute | solution.py:293
  59.9 9.1 %collective-permute-start.6 = (bf16[16,32,128]{2,1,0:T(8,128)(2,1)S(1)}, bf16[16,32,128]{2,1,0:T(8,128)(2,1)S(1)}, u32[]{:S(2)}, u32[]{:S(2)}) collective-permute-start(bf16[16,32,128]{2,1,0:T(8,128)(2,1)S(1)} %get-tuple-element.33), channel_id=1, source_target_pairs={{0,6},{2,4},{4,10},{6,8},{8,14},{10,12},{12,2},{14,0},{1,7},{3,5},... | collective-permute-start | bytes 393224 | tf_op jit(solution)/shard_map/ppermute | solution.py:293
  62.7 16.4 %collective-permute-start.7 = (bf16[16,32,128]{2,1,0:T(8,128)(2,1)S(1)}, bf16[16,32,128]{2,1,0:T(8,128)(2,1)S(1)}, u32[]{:S(2)}, u32[]{:S(2)}) collective-permute-start(bf16[16,32,128]{2,1,0:T(8,128)(2,1)S(1)} %get-tuple-element.34), channel_id=1, source_target_pairs={{0,8},{2,10},{4,12},{6,14},{8,0},{10,2},{12,4},{14,6},{1,9},{3,11}... | collective-permute-start | bytes 393224 | tf_op jit(solution)/shard_map/ppermute | solution.py:293
  64.7 14.4 %collective-permute-start.8 = (bf16[16,32,128]{2,1,0:T(8,128)(2,1)S(1)}, bf16[16,32,128]{2,1,0:T(8,128)(2,1)S(1)}, u32[]{:S(2)}, u32[]{:S(2)}) collective-permute-start(bf16[16,32,128]{2,1,0:T(8,128)(2,1)S(1)} %get-tuple-element.35), channel_id=1, source_target_pairs={{0,10},{2,8},{4,14},{6,12},{8,2},{10,0},{12,6},{14,4},{1,11},{3,9}... | collective-permute-start | bytes 393224 | tf_op jit(solution)/shard_map/ppermute | solution.py:293
  67.5 11.5 %collective-permute-start.9 = (bf16[16,32,128]{2,1,0:T(8,128)(2,1)S(1)}, bf16[16,32,128]{2,1,0:T(8,128)(2,1)S(1)}, u32[]{:S(2)}, u32[]{:S(2)}) collective-permute-start(bf16[16,32,128]{2,1,0:T(8,128)(2,1)S(1)} %get-tuple-element.36), channel_id=1, source_target_pairs={{0,12},{2,14},{4,0},{6,2},{8,4},{10,6},{12,8},{14,10},{1,13},{3,15... | collective-permute-start | bytes 393224 | tf_op jit(solution)/shard_map/ppermute | solution.py:293
  69.0 12.6 %collective-permute-start.10 = (bf16[16,32,128]{2,1,0:T(8,128)(2,1)S(1)}, bf16[16,32,128]{2,1,0:T(8,128)(2,1)S(1)}, u32[]{:S(2)}, u32[]{:S(2)}) collective-permute-start(bf16[16,32,128]{2,1,0:T(8,128)(2,1)S(1)} %get-tuple-element.37), channel_id=1, source_target_pairs={{0,14},{2,12},{4,2},{6,0},{8,6},{10,4},{12,10},{14,8},{1,15},{3,13... | collective-permute-start | bytes 393224 | tf_op jit(solution)/shard_map/ppermute | solution.py:293
  86.8 9.8 %collective-permute-start.20 = (bf16[8,27,8,128]{3,2,1,0:T(8,128)(2,1)S(1)}, bf16[8,27,8,128]{3,2,1,0:T(8,128)(2,1)S(1)}, u32[]{:S(2)}, u32[]{:S(2)}) collective-permute-start(bf16[8,27,8,128]{3,2,1,0:T(8,128)(2,1)S(1)} %get-tuple-element.47), channel_id=1, source_target_pairs={{0,128},{128,0},{1,129},{129,1},{2,130},{130,2},{3,131},{131,3},{4... | collective-permute-start | bytes 1327112 | tf_op jit(solution)/shard_map/ppermute | solution.py:282
  97.4 21.0 %all-to-all-start.2 = ((bf16[8,27,8,128]{3,2,1,0:T(8,128)(2,1)}), bf16[8,27,8,128]{3,2,1,0:T(8,128)(2,1)S(1)}, u32[]{:S(2)}, u32[]{:S(2)}) async-start(bf16[8,27,8,128]{3,2,1,0:T(8,128)(2,1)} %shard_map.83), calls=%async_computation.2 | async-start | bytes 884736 | tf_op jit(solution)/shard_map/all_to_all | solution.py:278
  110.9 10.9 %collective-permute-start.21 = (bf16[8,27,8,128]{3,2,1,0:T(8,128)(2,1)}, bf16[8,27,8,128]{3,2,1,0:T(8,128)(2,1)S(1)}, u32[]{:S(2)}, u32[]{:S(2)}) collective-permute-start(bf16[8,27,8,128]{3,2,1,0:T(8,128)(2,1)} %get-tuple-element.49), channel_id=1, source_target_pairs={{0,128},{128,0},{1,129},{129,1},{2,130},{130,2},{3,131},{131,3},{4... | collective-permute-start | bytes 1327112 | tf_op jit(solution)/shard_map/ppermute | solution.py:282
  121.9 0.8 copy-start.5
  122.6 1.0 copy-start.6
  123.6 5.8 %copy-start.2 = (bf16[32,27,512]{2,0,1:T(8,128)(2,1)S(1)}, bf16[32,27,512]{2,0,1:T(8,128)(2,1)}, u32[]{:S(2)}) copy-start(bf16[32,27,512]{2,0,1:T(8,128)(2,1)} %param.5) | copy-start | bytes 2654212
  124.7 25.0 %all-to-all-start.3 = ((bf16[8,54,8,128]{3,2,1,0:T(8,128)(2,1)}), bf16[8,54,8,128]{3,2,1,0:T(8,128)(2,1)S(1)}, u32[]{:S(2)}, u32[]{:S(2)}) async-start(bf16[8,54,8,128]{3,2,1,0:T(8,128)(2,1)} %shard_map.85), calls=%async_computation.3 | async-start | bytes 1769472 | tf_op jit(solution)/shard_map/all_to_all | solution.py:278
  129.5 30.4 %collective-permute-start.12 = (bf16[864,512]{1,0:T(8,128)(2,1)S(1)}, bf16[864,512]{1,0:T(8,128)(2,1)}, u32[]{:S(2)}, u32[]{:S(2)}) collective-permute-start(bf16[864,512]{1,0:T(8,128)(2,1)S(1)} %bitcast.41), channel_id=1, source_target_pairs={{0,1},{1,0},{2,3},{3,2},{4,5},{5,4},{6,7},{7,6},{8,9},{9,8},{10,11... | collective-permute-start | bytes 2654216 | tf_op jit(solution)/shard_map/ppermute | solution.py:282
  150.7 20.7 %all-to-all-start.4 = ((bf16[8,27,8,128]{3,2,1,0:T(8,128)(2,1)}), bf16[8,27,8,128]{3,2,1,0:T(8,128)(2,1)S(1)}, u32[]{:S(2)}, u32[]{:S(2)}) async-start(bf16[8,27,8,128]{3,2,1,0:T(8,128)(2,1)} %get-tuple-element.51), calls=%async_computation.4 | async-start | bytes 884736 | tf_op jit(solution)/shard_map/all_to_all | solution.py:278
  157.4 4.0 %collective-permute-start.11 = (bf16[16,32,128]{2,1,0:T(8,128)(2,1)}, bf16[16,32,128]{2,1,0:T(8,128)(2,1)}, u32[]{:S(2)}, u32[]{:S(2)}) collective-permute-start(bf16[16,32,128]{2,1,0:T(8,128)(2,1)} %shard_map.79.field_ref), channel_id=1, source_target_pairs={{0,1},{1,0},{2,3},{3,2},{4,5},{5,4},{6,7},{7,6},{8,9},{9,8},{10,11... | collective-permute-start | bytes 393224 | tf_op jit(solution)/shard_map/ppermute | solution.py:282
  166.2 0.7 copy-start.7
  166.9 0.7 copy-start.11
  167.5 0.7 copy-start.12
  168.2 0.6 copy-start.13
  168.8 0.6 copy-start.14
  169.5 0.7 copy-start.15
  170.1 0.6 copy-start.16
  170.8 8.1 %collective-permute-start.13 = (bf16[16,32,128]{2,1,0:T(8,128)(2,1)}, bf16[16,32,128]{2,1,0:T(8,128)(2,1)S(1)}, u32[]{:S(2)}, u32[]{:S(2)}) collective-permute-start(bf16[16,32,128]{2,1,0:T(8,128)(2,1)} %get-tuple-element.39), channel_id=1, source_target_pairs={{0,2},{2,0},{4,6},{6,4},{8,10},{10,8},{12,14},{14,12},{1,3},{3,1},... | collective-permute-start | bytes 393224 | tf_op jit(solution)/shard_map/ppermute | solution.py:293
  170.8 36.8 %collective-permute-start.22 = (bf16[8,27,8,128]{3,2,1,0:T(8,128)(2,1)}, bf16[8,27,8,128]{3,2,1,0:T(8,128)(2,1)S(1)}, u32[]{:S(2)}, u32[]{:S(2)}) collective-permute-start(bf16[8,27,8,128]{3,2,1,0:T(8,128)(2,1)} %get-tuple-element.50.pieces_ref), channel_id=1, source_target_pairs={{0,128},{128,0},{1,129},{129,1},{2,130},{130,2},{3,131},{131,3},{4... | collective-permute-start | bytes 1327112 | tf_op jit(solution)/shard_map/ppermute | solution.py:282
  171.4 38.3 %collective-permute-start.23 = (bf16[8,27,8,128]{3,2,1,0:T(8,128)(2,1)S(1)}, bf16[8,27,8,128]{3,2,1,0:T(8,128)(2,1)S(1)}, u32[]{:S(2)}, u32[]{:S(2)}) collective-permute-start(bf16[8,27,8,128]{3,2,1,0:T(8,128)(2,1)S(1)} %all-to-all-done.4.pieces_ref), channel_id=1, source_target_pairs={{0,128},{128,0},{1,129},{129,1},{2,130},{130,2},{3,131},{131,3},{4... | collective-permute-start | bytes 1327112 | tf_op jit(solution)/shard_map/ppermute | solution.py:282
  172.8 7.1 %collective-permute-start.14 = (bf16[16,32,128]{2,1,0:T(8,128)(2,1)}, bf16[16,32,128]{2,1,0:T(8,128)(2,1)S(1)}, u32[]{:S(2)}, u32[]{:S(2)}) collective-permute-start(bf16[16,32,128]{2,1,0:T(8,128)(2,1)} %copy-done.16), channel_id=1, source_target_pairs={{0,4},{2,6},{4,8},{6,10},{8,12},{10,14},{12,0},{14,2},{1,5},{3,7},... | collective-permute-start | bytes 393224 | tf_op jit(solution)/shard_map/ppermute | solution.py:293
  174.8 10.5 %collective-permute-start.15 = (bf16[16,32,128]{2,1,0:T(8,128)(2,1)}, bf16[16,32,128]{2,1,0:T(8,128)(2,1)S(1)}, u32[]{:S(2)}, u32[]{:S(2)}) collective-permute-start(bf16[16,32,128]{2,1,0:T(8,128)(2,1)} %copy-done.15), channel_id=1, source_target_pairs={{0,6},{2,4},{4,10},{6,8},{8,14},{10,12},{12,2},{14,0},{1,7},{3,5},... | collective-permute-start | bytes 393224 | tf_op jit(solution)/shard_map/ppermute | solution.py:293
  178.8 10.4 %collective-permute-start.16 = (bf16[16,32,128]{2,1,0:T(8,128)(2,1)}, bf16[16,32,128]{2,1,0:T(8,128)(2,1)S(1)}, u32[]{:S(2)}, u32[]{:S(2)}) collective-permute-start(bf16[16,32,128]{2,1,0:T(8,128)(2,1)} %copy-done.14), channel_id=1, source_target_pairs={{0,8},{2,10},{4,12},{6,14},{8,0},{10,2},{12,4},{14,6},{1,9},{3,11}... | collective-permute-start | bytes 393224 | tf_op jit(solution)/shard_map/ppermute | solution.py:293
  179.9 12.2 %collective-permute-start.17 = (bf16[16,32,128]{2,1,0:T(8,128)(2,1)}, bf16[16,32,128]{2,1,0:T(8,128)(2,1)S(1)}, u32[]{:S(2)}, u32[]{:S(2)}) collective-permute-start(bf16[16,32,128]{2,1,0:T(8,128)(2,1)} %copy-done.13), channel_id=1, source_target_pairs={{0,10},{2,8},{4,14},{6,12},{8,2},{10,0},{12,6},{14,4},{1,11},{3,9}... | collective-permute-start | bytes 393224 | tf_op jit(solution)/shard_map/ppermute | solution.py:293
  185.3 6.8 %collective-permute-start.18 = (bf16[16,32,128]{2,1,0:T(8,128)(2,1)}, bf16[16,32,128]{2,1,0:T(8,128)(2,1)S(1)}, u32[]{:S(2)}, u32[]{:S(2)}) collective-permute-start(bf16[16,32,128]{2,1,0:T(8,128)(2,1)} %copy-done.12), channel_id=1, source_target_pairs={{0,12},{2,14},{4,0},{6,2},{8,4},{10,6},{12,8},{14,10},{1,13},{3,15... | collective-permute-start | bytes 393224 | tf_op jit(solution)/shard_map/ppermute | solution.py:293
  189.2 7.7 %collective-permute-start.19 = (bf16[16,32,128]{2,1,0:T(8,128)(2,1)}, bf16[16,32,128]{2,1,0:T(8,128)(2,1)S(1)}, u32[]{:S(2)}, u32[]{:S(2)}) collective-permute-start(bf16[16,32,128]{2,1,0:T(8,128)(2,1)} %copy-done.11), channel_id=1, source_target_pairs={{0,14},{2,12},{4,2},{6,0},{8,6},{10,4},{12,10},{14,8},{1,15},{3,13... | collective-permute-start | bytes 393224 | tf_op jit(solution)/shard_map/ppermute | solution.py:293
  196.9 0.9 copy-start.4
  197.8 0.9 copy-start.8
